TPU v7x, 128 devices: a whole 4x4x4 slice. The times are simulated.
128 devices in a mesh: ctx: 16 (over z, y_lo, core), ch: 8 (over y_hi, x).
Axes of the slice: x: 4, y: 4 (y_hi: 2, y_lo: 2; y = y_hi * 2 + y_lo), z: 4, core: 2. Of those that a mesh axis runs over, the one named last changes fastest.
Arguments:
- tokens: bfloat16 [2048, 8192], P('ctx', 'ch'), may hold values from -6 to 6
- w_in: bfloat16 [8192, 3, 4096], P('ctx', None, 'ch'), may hold values from -0.0625 to 0.0625
- short_filter: float32 [3, 3, 4096], P(None, None, 'ch'), may hold values from -3 to 3
- decay_rate: float32 [256, 16], P('ch'), may hold values from 0.00024414062 to 0.1
- residue: float32 [256, 16], P('ch'), may hold values from -1.5 to 1.5
- skip: float32 [4096], P('ch'), may hold values from -6 to 6
Outputs:
- block_out: bfloat16 [2048, 4096], P('ctx', 'ch')
All inputs are finite; a program needn't handle non-finite values.
Results may differ from a plain program's by a relative error of at most 0.011.
Values may be sent and summed in bfloat16 or wider, within the bound.
A program may use at most 128 MiB of HBM per device.

v0:
```python
import math

import jax
import jax.numpy as jnp
from jax import lax
from jax.sharding import PartitionSpec as P

GROUP = 16


def shifted(block, axis, distance):
    devices = range(lax.axis_size(axis))
    route = [(i - distance, i) for i in devices if i - distance in devices]
    return lax.ppermute(block, axis, route)


def short_mix(projected, short_filter_taps, block_len, local_width):
    rounded = lax.optimization_barrier(projected.astype(jnp.bfloat16))
    proj_rows = rounded.astype(jnp.float32).reshape(
        block_len + 2, short_filter_taps.shape[1], local_width
    )
    return (
        short_filter_taps[0] * proj_rows[2:]
        + short_filter_taps[1] * proj_rows[1:-1]
        + short_filter_taps[2] * proj_rows[:-2]
    )


def split_parts(weight_full):
    upper_triangle_part = weight_full.astype(jnp.bfloat16)
    lower_triangle_part = (weight_full - upper_triangle_part.astype(jnp.float32)).astype(
        jnp.bfloat16
    )
    return (upper_triangle_part, lower_triangle_part)


def decay_sum(weight_full, input_half_rows):
    upper_triangle_part, lower_triangle_part = split_parts(weight_full)
    first_sum = jnp.einsum(
        "lbu,lvu->lbv", upper_triangle_part, input_half_rows, preferred_element_type=jnp.float32
    )
    second_partial_sum = jnp.einsum(
        "lbu,lvu->lbv", lower_triangle_part, input_half_rows, preferred_element_type=jnp.float32
    )
    return first_sum + second_partial_sum


def local(tokens, w_in, short_filter, decay_rate, residue, skip):
    block_len = tokens.shape[0]
    local_width = w_in.shape[2]
    group_count = local_width // GROUP
    gathered = lax.all_gather(tokens, "ch", axis=1, tiled=True)
    previous = shifted(gathered[block_len - 2 :], "ctx", 1)
    extended = jnp.concatenate([previous, gathered], axis=0)
    shard_piece = lax.all_gather(w_in, "ctx", axis=0, tiled=True)
    flat_piece = shard_piece.reshape(shard_piece.shape[0], -1)
    proj_all = jnp.dot(extended, flat_piece, preferred_element_type=jnp.float32)
    short_mixed = short_mix(proj_all, short_filter, block_len, local_width)
    query_part = short_mixed[:, 0]
    key_part = short_mixed[:, 1]
    value_part = short_mixed[:, 2]
    gated_input = (key_part * value_part).astype(jnp.bfloat16)
    input_t = gated_input.T
    columns_t = input_t.reshape(group_count, GROUP, block_len)
    pole_weight = residue * jnp.sqrt(2.0 * decay_rate)
    positions = jnp.arange(block_len).astype(jnp.float32)
    near_filter = jnp.einsum(
        "gr,grl->gl",
        pole_weight,
        jnp.exp(-decay_rate[:, :, None] * positions[None, None, :]),
        precision=lax.Precision.HIGHEST,
    )
    padded_filter = jnp.concatenate(
        [
            jnp.zeros((group_count, block_len - 1), jnp.float32),
            near_filter,
            jnp.zeros((group_count, 1), jnp.float32),
        ],
        axis=1,
    )

    def near_one(item_pair):
        filter_row, tok_block = item_pair
        span_len = 2 * block_len - 1
        tiled_rows = jnp.tile(filter_row, block_len)[: block_len * span_len].reshape(
            block_len, span_len
        )
        toeplitz = tiled_rows[:, block_len - 1 :]
        upper_triangle_part, lower_triangle_part = split_parts(toeplitz)
        return jnp.dot(
            tok_block, upper_triangle_part, preferred_element_type=jnp.float32
        ) + jnp.dot(tok_block, lower_triangle_part, preferred_element_type=jnp.float32)

    near_field = lax.map(near_one, (padded_filter, columns_t), batch_size=2)
    my_start = lax.axis_index("ctx") * block_len
    empty_state = jnp.zeros((group_count, decay_rate.shape[1], GROUP), jnp.float32)
    shard_piece = lax.all_gather(input_t, "ctx", axis=1, tiled=True)
    piece_len = shard_piece.shape[1]
    sub_len = math.gcd(piece_len, block_len)

    def sub_step(turn_index, carried):
        part_cols = lax.dynamic_slice_in_dim(shard_piece, turn_index * sub_len, sub_len, 1)
        distance = (my_start - 1 - turn_index * sub_len - jnp.arange(sub_len)).astype(jnp.float32)
        decay_factor_weight = jnp.where(
            distance[None, None, :] >= 0.0,
            jnp.exp(-decay_rate[:, :, None] * jnp.maximum(distance, 0.0)[None, None, :]),
            0.0,
        )
        part_input = part_cols.reshape(group_count, GROUP, sub_len)
        return carried + decay_sum(decay_factor_weight, part_input)

    past_state = lax.fori_loop(0, piece_len // sub_len, sub_step, empty_state)
    far_weight = pole_weight[:, :, None] * jnp.exp(
        -decay_rate[:, :, None] * (positions + 1.0)[None, None, :]
    )
    distant_field_output = jnp.einsum(
        "grc,gri->gci", past_state, far_weight, precision=lax.Precision.HIGHEST
    )
    long_out = (near_field + distant_field_output).reshape(local_width, block_len).T
    return (query_part * (long_out + skip * gated_input.astype(jnp.float32))).astype(jnp.bfloat16)


def solution(mesh):
    return jax.shard_map(
        local,
        mesh=mesh,
        in_specs=(
            P("ctx", "ch"),
            P("ctx", None, "ch"),
            P(None, None, "ch"),
            P("ch", None),
            P("ch", None),
            P("ch"),
        ),
        out_specs=P("ctx", "ch"),
        check_vma=False,
    )
```

profile of v0, /device:TPU:1, one launch (start us, length us, event | category | flops | bytes accessed | tf_op | source)
XLA Modules:
  0.0 289.3 jit_solution(2068078018637368503)
XLA Ops:
  6.5 0.7 all-gather.4.cloned.1.call-update
  7.3 2.6 copy.16
  10.3 0.4 fusion.32
  10.8 55.6 %all-gather.4.cloned.1.call-done = bf16[128,8192]{1,0:T(8,128)(2,1)} async-done(((bf16[128,1024]{1,0:T(8,128)(2,1)}), bf16[128,8192]{1,0:T(8,128)(2,1)}) %all-gather.4.cloned.1.call-update) | async-done | bytes 2097168 | tf_op jit(solution)/shard_map/all_gather | solution.py:52
  66.5 0.9 slice.60
  67.4 4.0 %collective-permute-start = (bf16[2,8192]{1,0:T(2,128)(2,1)S(1)}, bf16[2,8192]{1,0:T(2,128)(2,1)S(1)}, u32[]{:S(2)}, u32[]{:S(2)}) collective-permute-start(bf16[2,8192]{1,0:T(2,128)(2,1)S(1)} %slice.60), channel_id=1, source_target_pairs={{0,8},{8,16},{16,24},{24,32},{32,40},{40,48},{48,56},{56,64},{64,7... | collective-permute-start | bytes 98312 | tf_op jit(solution)/shard_map/ppermute | solution.py:14
  71.6 0.9 collective-permute-done
  72.5 127.4 %all-gather.6.cloned.1.call-done = bf16[8192,3,512]{0,2,1:T(8,128)(2,1)} async-done(((bf16[512,3,512]{0,2,1:T(8,128)(2,1)}), bf16[8192,3,512]{0,2,1:T(8,128)(2,1)}) %all-gather.6.cloned.1.call-update) | async-done | bytes 25165840 | tf_op jit(solution)/shard_map/all_gather | solution.py:55
  199.9 13.7 %convolution_convert_fusion = bf16[130,1536]{1,0:T(8,128)(2,1)S(1)} fusion(bf16[8192,1536]{0,1:T(8,128)(2,1)} %bitcast.89, bf16[128,8192]{1,0:T(8,128)(2,1)} %all-gather.4.cloned.1.call-done, bf16[2,8192]{1,0:T(2,128)(2,1)S(1)} %collective-permute-done), kind=kOutput, calls=%fused_computation.34 | convolution fusion | flops 3276016640 | bytes 27695104 | tf_op jit(solution)/shard_map/dot_general | solution.py:57
  213.8 1.2 copy.19
  215.5 0.6 copy-done
  216.1 0.8 multiply_add_fusion
  216.9 0.7 fusion.47
  217.6 27.3 %while.26 = (s32[]{:T(128)}, f32[16,2,16,128]{3,2,1,0:T(8,128)}, bf16[16,2,16,128]{3,2,1,0:T(8,128)(2,1)S(1)}, f32[16,2,256]{2,1,0:T(2,128)S(1)}, s32[]{:T(128)}) while((s32[]{:T(128)}, f32[16,2,16,128]{3,2,1,0:T(8,128)}, bf16[16,2,16,128]{3,2,1,0:T(8,128)(2,1)S(1)}, f32[16,2,256]{2,1,0:T(2,128)S(1)}, s32[]{:T(128)}) %tuple.71), condition=%wide.region_1.2_spmd, body=%wide.region_0.1_spmd.sunk | while | flops 2232322 | bytes 2100301 | solution.py:94
  217.9 0.4 reshape.72
  218.6 0.8 fusion.60
  219.6 0.4 reshape.72
  220.3 0.8 fusion.60
  221.4 0.4 reshape.72
  222.0 0.8 fusion.60
  223.1 0.4 reshape.72
  223.7 0.8 fusion.60
  224.8 0.4 reshape.72
  225.4 0.8 fusion.60
  226.5 0.4 reshape.72
  227.1 0.8 fusion.60
  228.2 0.4 reshape.72
  228.8 0.8 fusion.60
  229.9 0.4 reshape.72
  230.5 0.8 fusion.60
  231.6 0.4 reshape.72
  232.2 0.8 fusion.60
  233.3 0.4 reshape.72
  233.9 0.8 fusion.60
  235.0 0.4 reshape.72
  235.6 0.8 fusion.60
  236.7 0.4 reshape.72
  237.3 0.8 fusion.60
  238.4 0.4 reshape.72
  239.0 0.8 fusion.60
  240.1 0.4 reshape.72
  240.8 0.8 fusion.60
  242.5 0.8 fusion.60
  244.2 0.8 fusion.60
  245.0 11.1 %all-gather.8.cloned.1.call-done = bf16[512,2048]{1,0:T(8,128)(2,1)} async-done(((bf16[512,128]{1,0:T(8,128)(2,1)}), bf16[512,2048]{1,0:T(8,128)(2,1)}) %all-gather.8.cloned.1.call-update) | async-done | bytes 2097168 | tf_op jit(solution)/shard_map/all_gather | solution.py:97
  256.1 25.0 %while.27 = (s32[]{:T(128)}, f32[32,16,16]{2,1,0:T(8,128)S(1)}, s32[]{:T(128)}, f32[32,16,1]{1,0,2:T(8,128)S(1)}, bf16[512,2048]{1,0:T(8,128)(2,1)}, /*index=5*/s32[]{:T(128)}, s32[]{:T(128)}, s32[]{:T(128)}, s32[]{:T(128)}) while((s32[]{:T(128)}, f32[32,16,16]{2,1,0:T(8,128)S(1)}, s32[]{:T(128)}, f32[32,16,1]{1,0,2:T(8,128)S(1)}, ...), condition=%wide.region_3.4_spmd.clone, body=%wide.region_2.3_spmd.clone.sunk | while | flops 4809480 | bytes 661557 | solution.py:112
  256.1 1.0 constant_dynamic-slice_fusion.2
  257.7 0.9 constant_dynamic-slice_fusion.2
  259.2 0.9 constant_dynamic-slice_fusion.2
  260.8 0.9 constant_dynamic-slice_fusion.2
  262.3 0.9 constant_dynamic-slice_fusion.2
  263.9 0.9 constant_dynamic-slice_fusion.2
  265.5 0.9 constant_dynamic-slice_fusion.2
  267.0 0.9 constant_dynamic-slice_fusion.2
  268.6 0.9 constant_dynamic-slice_fusion.2
  270.1 0.9 constant_dynamic-slice_fusion.2
  271.7 0.9 constant_dynamic-slice_fusion.2
  273.3 0.9 constant_dynamic-slice_fusion.2
  274.8 0.9 constant_dynamic-slice_fusion.2
  276.4 0.9 constant_dynamic-slice_fusion.2
  277.9 0.9 constant_dynamic-slice_fusion.2
  279.5 0.9 constant_dynamic-slice_fusion.2
  281.1 0.7 convolution_add_fusion.2
  282.0 0.8 copy.23
  (182 shorter events, 18.8 us)
Async XLA Ops:
  6.5 59.9 %all-gather.4.cloned.1.call-start = ((), (), s32[]{:S(2)}) async-start(), calls=%async_computation | async-start | bytes 2359296 | tf_op jit(solution)/shard_map/all_gather | solution.py:52
  7.3 2.8 copy-start.2
  7.3 2.8 copy-start.4
  7.3 3.0 %copy-start.3 = (f32[3,3,512]{2,1,0:T(4,128)S(1)}, f32[3,3,512]{2,1,0:T(4,128)}, u32[]{:S(2)}) copy-start(f32[3,3,512]{2,1,0:T(4,128)} %param.12) | copy-start | bytes 55300
  7.3 192.6 %all-gather.6.cloned.1.call-start = ((), (), s32[]{:S(2)}) async-start(), calls=%async_computation.1 | async-start | bytes 26738688 | tf_op jit(solution)/shard_map/all_gather | solution.py:55
  10.0 246.1 %all-gather.8.cloned.1.call-start = ((), (), s32[]{:S(2)}) async-start(), calls=%async_computation.2 | async-start | bytes 2228224 | tf_op jit(solution)/shard_map/all_gather | solution.py:97
  67.4 5.1 %collective-permute-start = (bf16[2,8192]{1,0:T(2,128)(2,1)S(1)}, bf16[2,8192]{1,0:T(2,128)(2,1)S(1)}, u32[]{:S(2)}, u32[]{:S(2)}) collective-permute-start(bf16[2,8192]{1,0:T(2,128)(2,1)S(1)} %slice.60), channel_id=1, source_target_pairs={{0,8},{8,16},{16,24},{24,32},{32,40},{40,48},{48,56},{56,64},{64,7... | collective-permute-start | bytes 98312 | tf_op jit(solution)/shard_map/ppermute | solution.py:14
  215.0 1.1 copy-start
  256.1 25.0 %copy-start.1 = (f32[16,2,16,128]{3,2,1,0:T(8,128)S(1)}, f32[16,2,16,128]{3,2,1,0:T(8,128)}, u32[]{:S(2)}) copy-start(f32[16,2,16,128]{3,2,1,0:T(8,128)} %get-tuple-element.158) | copy-start | bytes 786436
  256.1 25.8 %copy-start.5 = (f32[512]{0:T(512)S(1)}, f32[512]{0:T(512)}, u32[]{:S(2)}) copy-start(f32[512]{0:T(512)} %param.15) | copy-start | bytes 6148
Sparse Core Ops, SparseCore 0:
  9.7 56.7 all-gather.3
  68.1 131.7 all-gather.5
  217.8 38.2 all-gather.7
where the time goes:
time: 290 us; the launch traced here: 289 us
  waiting for transfers between devices  196 us (68%)
  matrix products  40.5 us (14%)
  local copies, waits for them, and re-layouts  32.3 us (11%)
  between operations  13.3 us (5%)
  starting transfers between devices  4.13 us (1%)
    all_gather x1, waiting for transfers between devices, local(): shard_piece = lax.all_gather(w_in, 'ctx', axis=0, tiled=True)  127 us
    all_gather x1, waiting for transfers between devices, local(): gathered = lax.all_gather(tokens, 'ch', axis=1, tiled=True)  55.6 us
    dynamic_slice x16, local copies, waits for them, and re-layouts, sub_step(): lax.dynamic_slice_in_dim(shard_piece, turn_index * sub_len, sub_len, 1)  14.7 us
    dot_general x1, matrix products, local(): proj_all = jnp.dot(extended, flat_piece, preferred_element_type=jnp.float32)  13.7 us
    dot_general x16, matrix products, near_one(): jnp.dot(tok_block, lower_triangle_part, preferred_element_type=jnp.float32)  13.2 us
    all_gather x1, waiting for transfers between devices, local(): shard_piece = lax.all_gather(input_t, 'ctx', axis=1, tiled=True)  11.1 us
    reshape x16, local copies, waits for them, and re-layouts, near_one(): jnp.tile(filter_row, block_len)[:block_len * span_len]  6.48 us
  transfers between devices with their start and end apart: 4, of which 4 were waited for; matrix products, arithmetic and copies ran while one was open for 11% of the time, Pallas kernels for 0%

commit v1 on v0

v1 whole, which is shorter than its diff:
```python
import jax
import jax.numpy as jnp
from jax import lax
from jax.sharding import Mesh
from jax.sharding import PartitionSpec as P

GROUP = 16
HIGH = lax.Precision.HIGHEST


def split_bf16(x):
    hi = x.astype(jnp.bfloat16)
    lo = (x - hi.astype(jnp.float32)).astype(jnp.bfloat16)
    return hi, lo


def dot_split(spec, weight, data):
    hi, lo = split_bf16(weight)
    return jnp.einsum(spec, hi, data, preferred_element_type=jnp.float32) + jnp.einsum(
        spec, lo, data, preferred_element_type=jnp.float32
    )


def local(tokens, w_in, short_filter, decay_rate, residue, skip):
    n_chip = lax.axis_size("p")
    block_len = tokens.shape[0]
    local_width = w_in.shape[2]
    group_count = local_width // GROUP
    chip = lax.axis_index("p")
    core = lax.axis_index("c")
    col = lax.axis_index("ch")

    pairs = [(p * n_chip + m, m * n_chip + p) for p in range(n_chip) for m in range(n_chip)]
    moved = lax.ppermute(tokens, ("p", "ch"), pairs)
    tok_t = lax.all_gather(moved, "ch", axis=0, tiled=False)
    w_chip = lax.all_gather(w_in, "c", axis=0, tiled=True)
    flat_w = w_chip.reshape(w_chip.shape[0], -1)

    tail = tok_t[:, block_len - 2 :]
    partner_tail = lax.ppermute(tail, "c", [(0, 1), (1, 0)])
    shifted_tail = jnp.concatenate([jnp.zeros_like(partner_tail[:1]), partner_tail[:-1]], axis=0)
    prior = jnp.where(core == 1, partner_tail, shifted_tail)
    tok_ext = jnp.concatenate([prior, tok_t], axis=1)
    n_blk, ext_len = tok_ext.shape[0], tok_ext.shape[1]
    partial = jnp.dot(
        tok_ext.reshape(n_blk * ext_len, -1), flat_w, preferred_element_type=jnp.float32
    ).reshape(n_blk, ext_len, -1)
    proj = lax.psum_scatter(partial, "p", scatter_dimension=0, tiled=False)
    first = jnp.logical_and(chip == 0, core == 0)
    row_id = lax.broadcasted_iota(jnp.int32, proj.shape, 0)
    proj = jnp.where(jnp.logical_and(first, row_id < 2), 0.0, proj)
    proj = proj.astype(jnp.bfloat16).astype(jnp.float32).reshape(ext_len, 3, local_width)
    mixed = (
        short_filter[0] * proj[2:]
        + short_filter[1] * proj[1:-1]
        + short_filter[2] * proj[:-2]
    )
    query = mixed[:, 0]
    gated = (mixed[:, 1] * mixed[:, 2]).astype(jnp.bfloat16)
    x = gated.reshape(block_len, group_count, GROUP)

    pole_weight = residue * jnp.sqrt(2.0 * decay_rate)
    pos = jnp.arange(block_len, dtype=jnp.float32)
    lam = decay_rate[:, None, :]
    a_mat = pole_weight[:, None, :] * jnp.exp(-lam * pos[None, :, None])
    b_mat = jnp.exp(lam * pos[None, :, None])
    toep = jnp.einsum("gtr,gsr->gts", a_mat, b_mat, precision=HIGH)
    causal = pos[:, None] >= pos[None, :]
    toep = jnp.where(causal[None], toep, 0.0)
    near = dot_split("gts,sgc->tgc", toep, x)

    e_mat = jnp.exp(-lam * (block_len - 1 - pos)[None, :, None])
    s_loc = dot_split("gsr,sgc->grc", e_mat, x)
    s_all = lax.all_gather(s_loc, ("p", "c"), axis=0, tiled=False)
    me = chip * lax.axis_size("c") + core
    k_idx = jnp.arange(s_all.shape[0])
    gap = (me - 1 - k_idx).astype(jnp.float32)
    decay = jnp.where(
        gap[:, None, None] >= 0.0,
        jnp.exp(-decay_rate[None] * (block_len * jnp.maximum(gap, 0.0))[:, None, None]),
        0.0,
    )
    s_in = jnp.einsum("kgr,kgrc->grc", decay, s_all, precision=HIGH)
    f_mat = pole_weight[:, None, :] * jnp.exp(-lam * (pos + 1.0)[None, :, None])
    far = jnp.einsum("gtr,grc->tgc", f_mat, s_in, precision=HIGH)
    long_out = (near + far).reshape(block_len, local_width)
    out = query * (long_out + skip * gated.astype(jnp.float32))
    return out.astype(jnp.bfloat16)


def solution(mesh):
    n_ctx, n_ch = mesh.devices.shape
    sub = Mesh(mesh.devices.reshape(n_ctx // 2, 2, n_ch), ("p", "c", "ch"))
    ctx = ("p", "c")
    return jax.shard_map(
        local,
        mesh=sub,
        in_specs=(
            P(ctx, "ch"),
            P(ctx, None, "ch"),
            P(None, None, "ch"),
            P("ch", None),
            P("ch", None),
            P("ch"),
        ),
        out_specs=P(ctx, "ch"),
        check_vma=False,
    )
```

time: 290 us -> 318 us (1.097)
  blocking collectives: 0 us -> 48.4 us
  matrix products: 40.5 us -> 15.2 us
  waiting for transfers between devices: 196 us -> 219 us
  local copies, waits for them, and re-layouts: 32.3 us -> 13 us
  other arithmetic: 1.94 us -> 5.14 us
    reduce_scatter x0 -> x1, waiting for transfers between devices: none -> 134 us  [local(): proj = lax.psum_scatter(partial, 'p', scatter_dimension=0, tiled=False)]
    all_gather x3 -> x2, waiting for transfers between devices: 194 us -> 84.1 us  [the longest x1 71 us: local(): tok_t = lax.all_gather(moved, 'ch', axis=0, tiled=False)]
    all_gather x0 -> x1, blocking collectives: none -> 48.4 us  [local(): s_all = lax.all_gather(s_loc, ('p', 'c'), axis=0, tiled=False)]
    dot_general x67 -> x7, matrix products: 40.5 us -> 15.2 us  [the longest x1 8.96 us: local(): jnp.dot(tok_ext.reshape(n_blk * ext_len, -1), flat_w, preferred_element_t...]
    dynamic_slice x16 -> x0, local copies, waits for them, and re-layouts: 14.7 us -> none  [sub_step(): lax.dynamic_slice_in_dim(shard_piece, turn_index * sub_len, sub_len, 1)]
    reshape x17 -> x0, local copies, waits for them, and re-layouts: 6.51 us -> none  [the longest x16 6.48 us: near_one(): jnp.tile(filter_row, block_len)[:block_len * span_len]]
    slice x21 -> x6, local copies, waits for them, and re-layouts: 3.11 us -> 8.04 us  [the longest x2 3.6 us: local(): proj[2:]]
    while x32 -> x0, local copies, waits for them, and re-layouts: 3.62 us -> none
  transfers between devices with their start and end apart: 4 -> 5, of which waited for: 4 -> 4; matrix products, arithmetic and copies ran while one was open for 11% -> 2% of each run, Pallas kernels for 0% -> 0%
where the time goes in v1:
time: 318 us; the launch traced here: 317 us
  waiting for transfers between devices  219 us (69%)
  blocking collectives  48.4 us (15%)
  matrix products  15.2 us (5%)
  between operations  13.3 us (4%)
  local copies, waits for them, and re-layouts  13 us (4%)
  other arithmetic  5.14 us (2%)
  starting transfers between devices  3.74 us (1%)
    reduce_scatter x1, waiting for transfers between devices, local(): proj = lax.psum_scatter(partial, 'p', scatter_dimension=0, tiled=False)  134 us
    all_gather x1, waiting for transfers between devices, local(): tok_t = lax.all_gather(moved, 'ch', axis=0, tiled=False)  71 us
    all_gather x1, blocking collectives, local(): s_all = lax.all_gather(s_loc, ('p', 'c'), axis=0, tiled=False)  48.4 us
    all_gather x1, waiting for transfers between devices, local(): w_chip = lax.all_gather(w_in, 'c', axis=0, tiled=True)  13.2 us
    dot_general x1, matrix products, local(): jnp.dot(tok_ext.reshape(n_blk * ext_len, -1), flat_w, preferred_element_t...  8.96 us
  transfers between devices with their start and end apart: 5, of which 4 were waited for; matrix products, arithmetic and copies ran while one was open for 2% of the time, Pallas kernels for 0%

profile of v1, /device:TPU:1, one launch (start us, length us, event | category | flops | bytes accessed | tf_op | source)
XLA Modules:
  0.0 317.4 jit_solution(15747033902599304451)
XLA Ops:
  6.5 0.0 all-gather.7.cloned.1.call-start
  6.5 1.6 collective-permute-start
  8.1 0.0 collective-permute-done
  8.1 0.0 copy-start
  8.1 0.7 copy-done
  8.8 0.0 all-gather.7.cloned.1.call-update
  8.9 0.0 all-gather.5.cloned.1.call-start
  8.9 2.6 copy.30
  11.5 0.0 all-gather.5.cloned.1.call-update
  11.5 0.0 reduce-scatter.2.cloned.1.call-start
  11.6 71.0 %all-gather.7.cloned.1.call-done = bf16[1024,1024]{1,0:T(8,128)(2,1)} async-done(((bf16[128,1024]{1,0:T(8,128)(2,1)}), bf16[1024,1024]{1,0:T(8,128)(2,1)}) %all-gather.7.cloned.1.call-update) | async-done | bytes 2097168 | tf_op jit(solution)/shard_map/all_gather | solution.py:35
  82.6 0.9 slice.56
  83.5 2.1 collective-permute-start.1
  85.6 0.9 collective-permute-done.1
  86.4 0.1 broadcast_select_fusion
  86.5 13.2 %all-gather.5.cloned.1.call-done = bf16[1024,3,512]{0,2,1:T(8,128)(2,1)} async-done(((bf16[512,3,512]{0,2,1:T(8,128)(2,1)}), bf16[1024,3,512]{0,2,1:T(8,128)(2,1)}) %all-gather.5.cloned.1.call-update) | async-done | bytes 3145744 | tf_op jit(solution)/shard_map/all_gather | solution.py:36
  99.7 9.0 %fusion = f32[8,130,1536]{2,1,0:T(8,128)} fusion(bf16[1024,1536,1]{0,1,2:T(8,128)(2,1)} %bitcast.54, bf16[8,128,1024]{2,1,0:T(8,128)(2,1)} %bitcast.53, bf16[8,2,1024]{2,1,0:T(2,128)(2,1)S(1)} %broadcast_select_fusion), kind=kOutput, calls=%fused_computation.1 | convolution fusion | flops 3275816960 | bytes 11665408 | tf_op jit(solution)/shard_map/dot_general | solution.py:45
  108.6 0.0 copy-start.1
  108.6 0.0 copy-start.3
  108.6 0.0 copy-start.2
  108.6 0.0 reduce-scatter.2.cloned.1.call-update
  108.7 0.7 copy-done.1
  109.3 0.1 copy.37
  109.4 0.0 copy-done.3
  109.4 0.1 copy.36
  109.5 0.1 copy.35
  109.7 0.0 copy-done.2
  109.7 0.1 select_bitcast_fusion
  109.8 3.7 %fusion.21 = f32[32,128,128]{2,1,0:T(8,128)S(1)} fusion(f32[32,16]{1,0:T(8,128)S(1)} %copy.37, f32[32,16]{1,0:T(8,128)S(1)} %copy.36, f32[32,16]{1,0:T(8,128)S(1)} %copy.35), kind=kOutput, calls=%fused_computation.34 | convolution fusion | flops 100859904 | bytes 2103296 | tf_op jit(solution)/shard_map/gtr,gsr->gts/dot_general | solution.py:67
  113.5 133.6 %reduce-scatter.2.cloned.1.call-done = f32[1,130,1536]{2,1,0:T(8,128)} async-done(((f32[8,130,1536]{2,1,0:T(8,128)}), f32[1,130,1536]{2,1,0:T(8,128)}) %reduce-scatter.2.cloned.1.call-update) | async-done | bytes 798736 | tf_op jit(solution)/shard_map/reduce_scatter | solution.py:48
  247.1 1.3 fusion.12
  248.4 1.3 fusion.44
  249.7 2.3 copy.34
  252.0 2.3 copy.32
  254.3 1.2 copy.33
  255.4 2.0 multiply_add_fusion
  257.5 0.3 fusion.29
  257.8 0.3 convolution_add_fusion.1
  258.1 48.4 %all-gather.1 = f32[512,16,16]{2,1,0:T(8,128)S(1)} all-gather(f32[32,16,16]{2,1,0:T(8,128)S(1)} %convolution_add_fusion.1), channel_id=3, replica_groups=mesh['p'=8,'c'=2,'ch'=8] {'p','c'}, dimensions={0}, use_global_device_ids=true | all-gather | bytes 557056 | tf_op jit(solution)/shard_map/all_gather | solution.py:74
  306.5 0.6 fusion.6
  307.1 0.7 fusion.5
  307.8 0.0 copy-start.4
  307.8 1.4 multiply_reduce_fusion
  309.2 0.7 convolution_add_fusion
  310.0 0.0 copy-done.4
  310.0 0.1 fusion.15
  310.1 0.8 copy.39
  (10 shorter events, 0.1 us)
Async XLA Ops:
  6.5 76.0 %all-gather.7.cloned.1.call-start = ((), (), s32[]{:S(2)}) async-start(), calls=%async_computation.3 | async-start | bytes 2359296 | tf_op jit(solution)/shard_map/all_gather | solution.py:35
  6.5 1.6 collective-permute-start
  8.1 0.7 copy-start
  8.9 90.8 %all-gather.5.cloned.1.call-start = ((), (), s32[]{:S(2)}) async-start(), calls=%async_computation.1 | async-start | bytes 4718592 | tf_op jit(solution)/shard_map/all_gather | solution.py:36
  11.5 235.6 %reduce-scatter.2.cloned.1.call-start = ((), (), s32[]{:S(2)}) async-start(), calls=%async_computation.2 | async-start | bytes 7520256 | tf_op jit(solution)/shard_map/reduce_scatter | solution.py:48
  83.5 2.9 collective-permute-start.1
  108.6 0.7 copy-start.1
  108.6 0.8 copy-start.3
  108.6 1.0 copy-start.2
  307.8 2.2 copy-start.4
Sparse Core Ops, SparseCore 0:
  9.7 72.8 all-gather.6
  84.2 15.4 all-gather.4
  108.8 138.2 reduce-scatter.1

commit v2 on v1

--- a/solution.py
+++ b/solution.py
@@ -30,11 +30,22 @@
     core = lax.axis_index("c")
     col = lax.axis_index("ch")
 
-    pairs = [(p * n_chip + m, m * n_chip + p) for p in range(n_chip) for m in range(n_chip)]
-    moved = lax.ppermute(tokens, ("p", "ch"), pairs)
-    tok_t = lax.all_gather(moved, "ch", axis=0, tiled=False)
-    w_chip = lax.all_gather(w_in, "c", axis=0, tiled=True)
-    flat_w = w_chip.reshape(w_chip.shape[0], -1)
+    n_col = lax.axis_size("ch")
+    pieces = []
+    for k in range(n_col):
+        pairs = [(p * n_col + m, m * n_col + (p + k) % n_col) for p in range(n_chip) for m in range(n_col)]
+        pieces.append(lax.ppermute(tokens, ("p", "ch"), pairs))
+    stacked = jnp.stack(pieces)
+    src = (col - jnp.arange(n_col)) % n_col
+    order = jnp.argsort(src)
+    tok_t = jnp.take(stacked, order, axis=0)
+    w_flat = w_in.reshape(w_in.shape[0], -1)
+    w_other = lax.ppermute(w_flat, "c", [(0, 1), (1, 0)])
+    flat_w = jnp.where(
+        core == 0,
+        jnp.concatenate([w_flat, w_other], axis=0),
+        jnp.concatenate([w_other, w_flat], axis=0),
+    )
 
     tail = tok_t[:, block_len - 2 :]
     partner_tail = lax.ppermute(tail, "c", [(0, 1), (1, 0)])
@@ -45,7 +56,9 @@
     partial = jnp.dot(
         tok_ext.reshape(n_blk * ext_len, -1), flat_w, preferred_element_type=jnp.float32
     ).reshape(n_blk, ext_len, -1)
-    proj = lax.psum_scatter(partial, "p", scatter_dimension=0, tiled=False)
+    proj = lax.psum_scatter(
+        partial.astype(jnp.bfloat16), "p", scatter_dimension=0, tiled=False
+    ).astype(jnp.float32)
     first = jnp.logical_and(chip == 0, core == 0)
     row_id = lax.broadcasted_iota(jnp.int32, proj.shape, 0)
     proj = jnp.where(jnp.logical_and(first, row_id < 2), 0.0, proj)
@@ -71,16 +84,17 @@
 
     e_mat = jnp.exp(-lam * (block_len - 1 - pos)[None, :, None])
     s_loc = dot_split("gsr,sgc->grc", e_mat, x)
-    s_all = lax.all_gather(s_loc, ("p", "c"), axis=0, tiled=False)
+    n_ctx = n_chip * lax.axis_size("c")
     me = chip * lax.axis_size("c") + core
-    k_idx = jnp.arange(s_all.shape[0])
-    gap = (me - 1 - k_idx).astype(jnp.float32)
-    decay = jnp.where(
-        gap[:, None, None] >= 0.0,
-        jnp.exp(-decay_rate[None] * (block_len * jnp.maximum(gap, 0.0))[:, None, None]),
-        0.0,
-    )
-    s_in = jnp.einsum("kgr,kgrc->grc", decay, s_all, precision=HIGH)
+    s_flat = s_loc.reshape(group_count, -1)
+    s_in = jnp.zeros_like(s_flat)
+    for k in range(1, n_ctx):
+        pairs = [(i, i + k) for i in range(n_ctx - k)]
+        got = lax.ppermute(s_flat, ("p", "c"), pairs)
+        fac = jnp.exp(-decay_rate * (block_len * (k - 1.0)))
+        fac = jnp.where(me >= k, fac, 0.0)
+        s_in = s_in + (fac[:, :, None] * got.reshape(s_loc.shape)).reshape(s_flat.shape)
+    s_in = s_in.reshape(s_loc.shape)
     f_mat = pole_weight[:, None, :] * jnp.exp(-lam * (pos + 1.0)[None, :, None])
     far = jnp.einsum("gtr,grc->tgc", f_mat, s_in, precision=HIGH)
     long_out = (near + far).reshape(block_len, local_width)

time: 318 us -> 227 us (0.71)
  waiting for transfers between devices: 219 us -> 88.8 us
  starting transfers between devices: 3.74 us -> 81.1 us
  blocking collectives: 48.4 us -> 0 us
  local copies, waits for them, and re-layouts: 13 us -> 21.2 us
    all_gather x2 -> x0, waiting for transfers between devices: 84.1 us -> none  [the longest x1 71 us: local(): tok_t = lax.all_gather(moved, 'ch', axis=0, tiled=False)]
    ppermute x1 -> x24, starting transfers between devices: 1.6 us -> 75 us  [the longest x8 35.4 us: local(): pieces.append(lax.ppermute(tokens, ('p', 'ch'), pairs))]
    reduce_scatter x1, waiting for transfers between devices: 134 us -> 76.1 us  [local(): lax.psum_scatter(partial.astype(jnp.bfloat16), 'p', scatter_dimension=0,...]
    all_gather x1 -> x0, blocking collectives: 48.4 us -> none  [local(): s_all = lax.all_gather(s_loc, ('p', 'c'), axis=0, tiled=False)]
    ppermute x1 -> x24, waiting for transfers between devices: 0.01 us -> 11.8 us  [the longest x15 9.85 us: local(): got = lax.ppermute(s_flat, ('p', 'c'), pairs)]
    unnamed x12 -> x27, local copies, waits for them, and re-layouts: 4.03 us -> 9.77 us
    ppermute x1, starting transfers between devices: 2.06 us -> 6.16 us  [local(): partner_tail = lax.ppermute(tail, 'c', [(0, 1), (1, 0)])]
  transfers between devices with their start and end apart: 5 -> 26, of which waited for: 4 -> 6; matrix products, arithmetic and copies ran while one was open for 2% -> 8% of each run, Pallas kernels for 0% -> 0%
where the time goes in v2:
time: 227 us
  waiting for transfers between devices  88.8 us (39%)
  starting transfers between devices  81.1 us (36%)
  local copies, waits for them, and re-layouts  21.2 us (9%)
  matrix products  15.6 us (7%)
  between operations  13.8 us (6%)
  other arithmetic  6.05 us (3%)
    reduce_scatter x1, waiting for transfers between devices, local(): lax.psum_scatter(partial.astype(jnp.bfloat16), 'p', scatter_dimension=0,...  76.1 us
    ppermute x8, starting transfers between devices, local(): pieces.append(lax.ppermute(tokens, ('p', 'ch'), pairs))  35.4 us
    ppermute x15, starting transfers between devices, local(): got = lax.ppermute(s_flat, ('p', 'c'), pairs)  35.2 us
    ppermute x15, waiting for transfers between devices, local(): got = lax.ppermute(s_flat, ('p', 'c'), pairs)  9.85 us
    unnamed x27, local copies, waits for them, and re-layouts  9.77 us
    dot_general x1, matrix products, local(): jnp.dot(tok_ext.reshape(n_blk * ext_len, -1), flat_w, preferred_element_t...  8.95 us
    ppermute x1, starting transfers between devices, local(): partner_tail = lax.ppermute(tail, 'c', [(0, 1), (1, 0)])  6.16 us
  transfers between devices with their start and end apart: 26, of which 6 were waited for; matrix products, arithmetic and copies ran while one was open for 8% of the time, Pallas kernels for 0%

profile of v2, /device:TPU:1, one launch (start us, length us, event | category | flops | bytes accessed | tf_op | source)
XLA Modules:
  0.0 226.5 jit_solution(2030672418971019783)
XLA Ops:
  6.5 1.7 collective-permute-start
  8.3 3.7 %collective-permute-start.1 = (bf16[128,1024]{1,0:T(8,128)(2,1)}, bf16[128,1024]{1,0:T(8,128)(2,1)S(1)}, u32[]{:S(2)}, u32[]{:S(2)}) collective-permute-start(bf16[128,1024]{1,0:T(8,128)(2,1)} %param.6), channel_id=1, source_target_pairs={{0,1},{1,17},{2,33},{3,49},{4,65},{5,81},{6,97},{7,113},{16,2},{17... | collective-permute-start | bytes 786440 | tf_op jit(solution)/shard_map/ppermute | solution.py:37
  12.0 3.6 %collective-permute-start.2 = (bf16[128,1024]{1,0:T(8,128)(2,1)}, bf16[128,1024]{1,0:T(8,128)(2,1)S(1)}, u32[]{:S(2)}, u32[]{:S(2)}) collective-permute-start(bf16[128,1024]{1,0:T(8,128)(2,1)} %param.6), channel_id=1, source_target_pairs={{0,2},{1,18},{2,34},{3,50},{4,66},{5,82},{6,98},{7,114},{16,3},{17... | collective-permute-start | bytes 786440 | tf_op jit(solution)/shard_map/ppermute | solution.py:37
  15.6 4.4 %collective-permute-start.3 = (bf16[128,1024]{1,0:T(8,128)(2,1)}, bf16[128,1024]{1,0:T(8,128)(2,1)S(1)}, u32[]{:S(2)}, u32[]{:S(2)}) collective-permute-start(bf16[128,1024]{1,0:T(8,128)(2,1)} %param.6), channel_id=1, source_target_pairs={{0,3},{1,19},{2,35},{3,51},{4,67},{5,83},{6,99},{7,115},{16,4},{17... | collective-permute-start | bytes 786440 | tf_op jit(solution)/shard_map/ppermute | solution.py:37
  20.0 5.9 %collective-permute-start.4 = (bf16[128,1024]{1,0:T(8,128)(2,1)}, bf16[128,1024]{1,0:T(8,128)(2,1)S(1)}, u32[]{:S(2)}, u32[]{:S(2)}) collective-permute-start(bf16[128,1024]{1,0:T(8,128)(2,1)} %param.6), channel_id=1, source_target_pairs={{0,4},{1,20},{2,36},{3,52},{4,68},{5,84},{6,100},{7,116},{16,5},{1... | collective-permute-start | bytes 786440 | tf_op jit(solution)/shard_map/ppermute | solution.py:37
  25.9 1.0 sort.17
  26.9 2.6 %copy.33 = bf16[512,3,512]{0,2,1:T(8,128)(2,1)} copy(bf16[512,3,512]{2,0,1:T(8,128)(2,1)} %param.7) | data formatting | bytes 3145728 | tf_op args[1]
  29.5 1.9 collective-permute-start.5
  31.4 0.7 bitcast_dynamic-update-slice_fusion.7
  32.1 6.7 %collective-permute-start.6 = (bf16[128,1024]{1,0:T(8,128)(2,1)S(1)}, bf16[128,1024]{1,0:T(8,128)(2,1)S(1)}, u32[]{:S(2)}, u32[]{:S(2)}) collective-permute-start(bf16[128,1024]{1,0:T(8,128)(2,1)S(1)} %copy-done.8), channel_id=1, source_target_pairs={{0,6},{1,22},{2,38},{3,54},{4,70},{5,86},{6,102},{7,118},{16,7},{1... | collective-permute-start | bytes 786440 | tf_op jit(solution)/shard_map/ppermute | solution.py:37
  38.9 0.7 bitcast_dynamic-update-slice_fusion.6
  39.6 7.4 %collective-permute-start.7 = (bf16[128,1024]{1,0:T(8,128)(2,1)S(1)}, bf16[128,1024]{1,0:T(8,128)(2,1)S(1)}, u32[]{:S(2)}, u32[]{:S(2)}) collective-permute-start(bf16[128,1024]{1,0:T(8,128)(2,1)S(1)} %copy-done.8), channel_id=1, source_target_pairs={{0,7},{1,23},{2,39},{3,55},{4,71},{5,87},{6,103},{7,119},{16,0},{1... | collective-permute-start | bytes 786440 | tf_op jit(solution)/shard_map/ppermute | solution.py:37
  47.0 0.7 bitcast_dynamic-update-slice_fusion.5
  47.8 4.3 %collective-permute-start.9 = (bf16[512,1536]{0,1:T(8,128)(2,1)}, bf16[512,1536]{0,1:T(8,128)(2,1)}, u32[]{:S(2)}, u32[]{:S(2)}) collective-permute-start(bf16[512,1536]{0,1:T(8,128)(2,1)} %bitcast.9), channel_id=1, source_target_pairs={{0,8},{8,0},{1,9},{9,1},{2,10},{10,2},{3,11},{11,3},{4,12},{12,4},... | collective-permute-start | bytes 4718600 | tf_op jit(solution)/shard_map/ppermute | solution.py:43
  52.1 0.7 bitcast_dynamic-update-slice_fusion.4
  52.8 0.7 bitcast_dynamic-update-slice_fusion.3
  53.5 0.7 bitcast_dynamic-update-slice_fusion.2
  54.3 0.7 bitcast_dynamic-update-slice_fusion.1
  55.0 2.0 collective-permute-done.7
  57.0 0.7 bitcast_dynamic-update-slice_fusion
  57.7 2.3 %gather_fusion = bf16[8,128,1024]{2,1,0:T(8,128)(2,1)S(1)} fusion(bf16[8,128,1024]{2,1,0:T(8,128)(2,1)} %bitcast_dynamic-update-slice_fusion, s32[1024]{0:T(1024)S(1)} %pad_clamp_fusion), kind=kCustom, calls=%fused_computation | custom fusion | bytes 4194336 | tf_op jit(solution)/shard_map/jit(_take)/gather | solution.py:41
  59.9 0.3 broadcast_select_fusion
  60.2 1.3 copy-done
  61.6 6.2 %collective-permute-start.8 = (bf16[8,2,1024]{2,1,0:T(2,128)(2,1)S(1)}, bf16[8,2,1024]{2,1,0:T(2,128)(2,1)S(1)}, u32[]{:S(2)}, u32[]{:S(2)}) collective-permute-start(bf16[8,2,1024]{2,1,0:T(2,128)(2,1)S(1)} %slice.58), channel_id=1, source_target_pairs={{0,8},{8,0},{1,9},{9,1},{2,10},{10,2},{3,11},{11,3},{4,12},{12,4},... | collective-permute-start | bytes 98312 | tf_op jit(solution)/shard_map/ppermute | solution.py:51
  67.8 0.9 collective-permute-done.8
  68.7 8.9 %convolution_convert_fusion = bf16[8,130,1536]{2,1,0:T(8,128)(2,1)} fusion(bf16[512,1536]{0,1:T(8,128)(2,1)} %collective-permute-done.9, bf16[512,1536]{0,1:T(8,128)(2,1)} %bitcast.9, pred[]{:T(512)S(6)} %eq.13, bf16[8,128,1024]{2,1,0:T(8,128)(2,1)} %copy-done, bf16[8,2,1024]{2,1,0:T(2,128)(2,1)S(1)} %broadcast_select_fusion.1), kind=kOutput, calls=%fused_computation.1 | convolution fusion | flops 3291570176 | bytes 8470529 | tf_op jit(solution)/shard_map/dot_general | solution.py:56
  77.7 0.6 copy-done.4
  78.4 0.6 exponential_select_fusion.14
  79.3 3.7 %fusion.28 = f32[32,128,128]{2,1,0:T(8,128)S(1)} fusion(f32[32,16]{1,0:T(8,128)S(1)} %copy.40, f32[32,16]{1,0:T(8,128)S(1)} %copy.39, f32[32,16]{1,0:T(8,128)S(1)} %copy.38), kind=kOutput, calls=%fused_computation.50 | convolution fusion | flops 100859904 | bytes 2103296 | tf_op jit(solution)/shard_map/gtr,gsr->gts/dot_general | solution.py:80
  83.0 76.1 %reduce-scatter.2.cloned.1.call-done = bf16[1,130,1536]{2,1,0:T(8,128)(2,1)} async-done(((bf16[8,130,1536]{2,1,0:T(8,128)(2,1)}), bf16[1,130,1536]{2,1,0:T(8,128)(2,1)}) %reduce-scatter.2.cloned.1.call-update) | async-done | bytes 399376 | tf_op jit(solution)/shard_map/reduce_scatter | solution.py:59
  159.0 1.1 fusion.19
  160.2 1.3 fusion.66
  161.5 2.3 %copy.37 = f32[128,1536]{0,1:T(8,128)} copy(f32[128,1536]{1,0:T(8,128)} %get-tuple-element.8) | data formatting | bytes 1572864 | tf_op jit(solution)/shard_map/slice | solution.py:69
  163.8 2.3 %copy.36 = f32[128,1536]{0,1:T(8,128)} copy(f32[128,1536]{1,0:T(8,128)} %get-tuple-element.9) | data formatting | bytes 1572864 | tf_op jit(solution)/shard_map/slice | solution.py:68
  166.1 1.2 copy.35
  167.3 2.0 multiply_add_fusion
  169.4 0.3 fusion.36
  169.7 0.3 convolution_add_fusion.1
  170.0 0.2 copy.41
  170.1 0.7 collective-permute-start.24
  170.8 3.2 %collective-permute-start.23 = (f32[32,256]{0,1:T(8,128)S(1)}, f32[32,256]{0,1:T(8,128)S(1)}, u32[]{:S(2)}, u32[]{:S(2)}) collective-permute-start(f32[32,256]{0,1:T(8,128)S(1)} %bitcast.148), channel_id=1, source_target_pairs={{0,112},{8,120},{1,113},{9,121},{2,114},{10,122},{3,115},{11,123},... | collective-permute-start | bytes 98312 | tf_op jit(solution)/shard_map/ppermute | solution.py:93
  174.0 1.3 collective-permute-start.22
  175.4 1.3 collective-permute-start.21
  176.7 1.3 collective-permute-start.20
  178.0 0.5 iota_add_fusion
  178.5 1.4 collective-permute-start.19
  180.0 1.3 collective-permute-start.18
  181.3 1.3 collective-permute-start.17
  182.6 7.0 %collective-permute-done.21 = f32[32,256]{0,1:T(8,128)S(1)} collective-permute-done((f32[32,256]{0,1:T(8,128)S(1)}, f32[32,256]{0,1:T(8,128)S(1)}, u32[]{:S(2)}, u32[]{:S(2)}) %collective-permute-start.21) | collective-permute-done | bytes 32800 | tf_op jit(solution)/shard_map/ppermute | solution.py:93
  189.6 1.3 collective-permute-start.16
  190.9 1.0 collective-permute-done.20
  191.9 10.5 %collective-permute-start.15 = (f32[32,256]{0,1:T(8,128)S(1)}, f32[32,256]{0,1:T(8,128)S(1)}, u32[]{:S(2)}, u32[]{:S(2)}) collective-permute-start(f32[32,256]{0,1:T(8,128)S(1)} %bitcast.156), channel_id=1, source_target_pairs={{0,48},{8,56},{16,64},{24,72},{32,80},{40,88},{48,96},{56,104},{64... | collective-permute-start | bytes 98312 | tf_op jit(solution)/shard_map/ppermute | solution.py:93
  202.4 0.6 fusion.13
  203.0 1.3 collective-permute-start.14
  204.4 1.3 collective-permute-start.13
  205.7 3.4 %collective-permute-start.12 = (f32[32,256]{0,1:T(8,128)S(1)}, f32[32,256]{0,1:T(8,128)S(1)}, u32[]{:S(2)}, u32[]{:S(2)}) collective-permute-start(f32[32,256]{0,1:T(8,128)S(1)} %bitcast.159), channel_id=1, source_target_pairs={{0,24},{8,32},{16,40},{24,48},{32,56},{40,64},{48,72},{56,80},{64,... | collective-permute-start | bytes 98312 | tf_op jit(solution)/shard_map/ppermute | solution.py:93
  209.1 2.5 %collective-permute-start.11 = (f32[32,256]{0,1:T(8,128)S(1)}, f32[32,256]{0,1:T(8,128)S(1)}, u32[]{:S(2)}, u32[]{:S(2)}) collective-permute-start(f32[32,256]{0,1:T(8,128)S(1)} %bitcast.160), channel_id=1, source_target_pairs={{0,16},{8,24},{16,32},{24,40},{32,48},{40,56},{48,64},{56,72},{64,... | collective-permute-start | bytes 98312 | tf_op jit(solution)/shard_map/ppermute | solution.py:93
  211.6 3.1 %collective-permute-start.10 = (f32[32,256]{0,1:T(8,128)S(1)}, f32[32,256]{0,1:T(8,128)S(1)}, u32[]{:S(2)}, u32[]{:S(2)}) collective-permute-start(f32[32,256]{0,1:T(8,128)S(1)} %bitcast.161), channel_id=1, source_target_pairs={{0,8},{8,16},{16,24},{24,32},{32,40},{40,48},{48,56},{56,64},{64,7... | collective-permute-start | bytes 98312 | tf_op jit(solution)/shard_map/ppermute | solution.py:93
  214.7 0.6 fusion.12
  215.4 1.8 collective-permute-done.12
  217.2 0.2 fusion.38
  217.4 0.2 copy.42
  217.6 1.1 convolution_add_fusion
  218.9 0.8 copy.43
  (55 shorter events, 0.7 us)
Async XLA Ops:
  6.5 23.0 %copy-start.8 = (bf16[128,1024]{1,0:T(8,128)(2,1)S(1)}, bf16[128,1024]{1,0:T(8,128)(2,1)}, u32[]{:S(2)}) copy-start(bf16[128,1024]{1,0:T(8,128)(2,1)} %param.6) | copy-start | bytes 786436
  6.5 152.5 %reduce-scatter.2.cloned.1.call-start = ((), (), s32[]{:S(2)}) async-start(), calls=%async_computation.1 | async-start | bytes 3760128 | tf_op jit(solution)/shard_map/reduce_scatter | solution.py:59
  6.5 23.0 %collective-permute-start = (bf16[128,1024]{1,0:T(8,128)(2,1)}, bf16[128,1024]{1,0:T(8,128)(2,1)S(1)}, u32[]{:S(2)}, u32[]{:S(2)}) collective-permute-start(bf16[128,1024]{1,0:T(8,128)(2,1)} %param.6), channel_id=1, source_target_pairs={{0,0},{1,16},{2,32},{3,48},{4,64},{5,80},{6,96},{7,112},{16,1},{17... | collective-permute-start | bytes 786440 | tf_op jit(solution)/shard_map/ppermute | solution.py:37
  8.3 23.9 %collective-permute-start.1 = (bf16[128,1024]{1,0:T(8,128)(2,1)}, bf16[128,1024]{1,0:T(8,128)(2,1)S(1)}, u32[]{:S(2)}, u32[]{:S(2)}) collective-permute-start(bf16[128,1024]{1,0:T(8,128)(2,1)} %param.6), channel_id=1, source_target_pairs={{0,1},{1,17},{2,33},{3,49},{4,65},{5,81},{6,97},{7,113},{16,2},{17... | collective-permute-start | bytes 786440 | tf_op jit(solution)/shard_map/ppermute | solution.py:37
  12.0 27.7 %collective-permute-start.2 = (bf16[128,1024]{1,0:T(8,128)(2,1)}, bf16[128,1024]{1,0:T(8,128)(2,1)S(1)}, u32[]{:S(2)}, u32[]{:S(2)}) collective-permute-start(bf16[128,1024]{1,0:T(8,128)(2,1)} %param.6), channel_id=1, source_target_pairs={{0,2},{1,18},{2,34},{3,50},{4,66},{5,82},{6,98},{7,114},{16,3},{17... | collective-permute-start | bytes 786440 | tf_op jit(solution)/shard_map/ppermute | solution.py:37
  15.6 32.2 %collective-permute-start.3 = (bf16[128,1024]{1,0:T(8,128)(2,1)}, bf16[128,1024]{1,0:T(8,128)(2,1)S(1)}, u32[]{:S(2)}, u32[]{:S(2)}) collective-permute-start(bf16[128,1024]{1,0:T(8,128)(2,1)} %param.6), channel_id=1, source_target_pairs={{0,3},{1,19},{2,35},{3,51},{4,67},{5,83},{6,99},{7,115},{16,4},{17... | collective-permute-start | bytes 786440 | tf_op jit(solution)/shard_map/ppermute | solution.py:37
  20.0 32.8 %collective-permute-start.4 = (bf16[128,1024]{1,0:T(8,128)(2,1)}, bf16[128,1024]{1,0:T(8,128)(2,1)S(1)}, u32[]{:S(2)}, u32[]{:S(2)}) collective-permute-start(bf16[128,1024]{1,0:T(8,128)(2,1)} %param.6), channel_id=1, source_target_pairs={{0,4},{1,20},{2,36},{3,52},{4,68},{5,84},{6,100},{7,116},{16,5},{1... | collective-permute-start | bytes 786440 | tf_op jit(solution)/shard_map/ppermute | solution.py:37
  29.5 24.0 %collective-permute-start.5 = (bf16[128,1024]{1,0:T(8,128)(2,1)S(1)}, bf16[128,1024]{1,0:T(8,128)(2,1)S(1)}, u32[]{:S(2)}, u32[]{:S(2)}) collective-permute-start(bf16[128,1024]{1,0:T(8,128)(2,1)S(1)} %copy-done.8), channel_id=1, source_target_pairs={{0,5},{1,21},{2,37},{3,53},{4,69},{5,85},{6,101},{7,117},{16,6},{1... | collective-permute-start | bytes 786440 | tf_op jit(solution)/shard_map/ppermute | solution.py:37
  32.1 22.1 %collective-permute-start.6 = (bf16[128,1024]{1,0:T(8,128)(2,1)S(1)}, bf16[128,1024]{1,0:T(8,128)(2,1)S(1)}, u32[]{:S(2)}, u32[]{:S(2)}) collective-permute-start(bf16[128,1024]{1,0:T(8,128)(2,1)S(1)} %copy-done.8), channel_id=1, source_target_pairs={{0,6},{1,22},{2,38},{3,54},{4,70},{5,86},{6,102},{7,118},{16,7},{1... | collective-permute-start | bytes 786440 | tf_op jit(solution)/shard_map/ppermute | solution.py:37
  39.6 17.3 %collective-permute-start.7 = (bf16[128,1024]{1,0:T(8,128)(2,1)S(1)}, bf16[128,1024]{1,0:T(8,128)(2,1)S(1)}, u32[]{:S(2)}, u32[]{:S(2)}) collective-permute-start(bf16[128,1024]{1,0:T(8,128)(2,1)S(1)} %copy-done.8), channel_id=1, source_target_pairs={{0,7},{1,23},{2,39},{3,55},{4,71},{5,87},{6,103},{7,119},{16,0},{1... | collective-permute-start | bytes 786440 | tf_op jit(solution)/shard_map/ppermute | solution.py:37
  47.8 20.9 %collective-permute-start.9 = (bf16[512,1536]{0,1:T(8,128)(2,1)}, bf16[512,1536]{0,1:T(8,128)(2,1)}, u32[]{:S(2)}, u32[]{:S(2)}) collective-permute-start(bf16[512,1536]{0,1:T(8,128)(2,1)} %bitcast.9), channel_id=1, source_target_pairs={{0,8},{8,0},{1,9},{9,1},{2,10},{10,2},{3,11},{11,3},{4,12},{12,4},... | collective-permute-start | bytes 4718600 | tf_op jit(solution)/shard_map/ppermute | solution.py:43
  60.2 1.3 copy-start
  61.6 7.0 %collective-permute-start.8 = (bf16[8,2,1024]{2,1,0:T(2,128)(2,1)S(1)}, bf16[8,2,1024]{2,1,0:T(2,128)(2,1)S(1)}, u32[]{:S(2)}, u32[]{:S(2)}) collective-permute-start(bf16[8,2,1024]{2,1,0:T(2,128)(2,1)S(1)} %slice.58), channel_id=1, source_target_pairs={{0,8},{8,0},{1,9},{9,1},{2,10},{10,2},{3,11},{11,3},{4,12},{12,4},... | collective-permute-start | bytes 98312 | tf_op jit(solution)/shard_map/ppermute | solution.py:51
  77.7 0.7 copy-start.4
  77.7 0.8 copy-start.6
  77.7 1.6 copy-start.5
  170.1 8.4 %collective-permute-start.24 = (f32[32,256]{0,1:T(8,128)S(1)}, f32[32,256]{0,1:T(8,128)S(1)}, u32[]{:S(2)}, u32[]{:S(2)}) collective-permute-start(f32[32,256]{0,1:T(8,128)S(1)} %bitcast.147), channel_id=1, source_target_pairs={{0,120},{1,121},{2,122},{3,123},{4,124},{5,125},{6,126},{7,127}} | collective-permute-start | bytes 98312 | tf_op jit(solution)/shard_map/ppermute | solution.py:93
  170.8 9.2 %collective-permute-start.23 = (f32[32,256]{0,1:T(8,128)S(1)}, f32[32,256]{0,1:T(8,128)S(1)}, u32[]{:S(2)}, u32[]{:S(2)}) collective-permute-start(f32[32,256]{0,1:T(8,128)S(1)} %bitcast.148), channel_id=1, source_target_pairs={{0,112},{8,120},{1,113},{9,121},{2,114},{10,122},{3,115},{11,123},... | collective-permute-start | bytes 98312 | tf_op jit(solution)/shard_map/ppermute | solution.py:93
  174.0 7.2 %collective-permute-start.22 = (f32[32,256]{0,1:T(8,128)S(1)}, f32[32,256]{0,1:T(8,128)S(1)}, u32[]{:S(2)}, u32[]{:S(2)}) collective-permute-start(f32[32,256]{0,1:T(8,128)S(1)} %bitcast.149), channel_id=1, source_target_pairs={{0,104},{8,112},{16,120},{1,105},{9,113},{17,121},{2,106},{10,114}... | collective-permute-start | bytes 98312 | tf_op jit(solution)/shard_map/ppermute | solution.py:93
  175.4 14.2 %collective-permute-start.21 = (f32[32,256]{0,1:T(8,128)S(1)}, f32[32,256]{0,1:T(8,128)S(1)}, u32[]{:S(2)}, u32[]{:S(2)}) collective-permute-start(f32[32,256]{0,1:T(8,128)S(1)} %bitcast.150), channel_id=1, source_target_pairs={{0,96},{8,104},{16,112},{24,120},{1,97},{9,105},{17,113},{25,121},... | collective-permute-start | bytes 98312 | tf_op jit(solution)/shard_map/ppermute | solution.py:93
  176.7 15.2 %collective-permute-start.20 = (f32[32,256]{0,1:T(8,128)S(1)}, f32[32,256]{0,1:T(8,128)S(1)}, u32[]{:S(2)}, u32[]{:S(2)}) collective-permute-start(f32[32,256]{0,1:T(8,128)S(1)} %bitcast.151), channel_id=1, source_target_pairs={{0,88},{8,96},{16,104},{24,112},{32,120},{1,89},{9,97},{17,105},{2... | collective-permute-start | bytes 98312 | tf_op jit(solution)/shard_map/ppermute | solution.py:93
  178.5 38.7 %copy-start.1 = (f32[32,16]{0,1:T(8,128)S(1)}, f32[32,16]{0,1:T(8,128)}, u32[]{:S(2)}) copy-start(f32[32,16]{0,1:T(8,128)} %get-tuple-element.25) | copy-start | bytes 6148
  178.5 38.7 %copy-start.2 = (f32[32,16]{0,1:T(8,128)S(1)}, f32[32,16]{0,1:T(8,128)}, u32[]{:S(2)}) copy-start(f32[32,16]{0,1:T(8,128)} %get-tuple-element.26) | copy-start | bytes 6148
  178.5 38.7 %copy-start.3 = (f32[32,16]{0,1:T(8,128)S(1)}, f32[32,16]{0,1:T(8,128)}, u32[]{:S(2)}) copy-start(f32[32,16]{0,1:T(8,128)} %get-tuple-element.27) | copy-start | bytes 6148
  178.5 24.5 %collective-permute-start.19 = (f32[32,256]{0,1:T(8,128)S(1)}, f32[32,256]{0,1:T(8,128)S(1)}, u32[]{:S(2)}, u32[]{:S(2)}) collective-permute-start(f32[32,256]{0,1:T(8,128)S(1)} %bitcast.152), channel_id=1, source_target_pairs={{0,80},{8,88},{16,96},{24,104},{32,112},{40,120},{1,81},{9,89},{17... | collective-permute-start | bytes 98312 | tf_op jit(solution)/shard_map/ppermute | solution.py:93
  180.0 24.4 %collective-permute-start.18 = (f32[32,256]{0,1:T(8,128)S(1)}, f32[32,256]{0,1:T(8,128)S(1)}, u32[]{:S(2)}, u32[]{:S(2)}) collective-permute-start(f32[32,256]{0,1:T(8,128)S(1)} %bitcast.153), channel_id=1, source_target_pairs={{0,72},{8,80},{16,88},{24,96},{32,104},{40,112},{48,120},{1,73},{9... | collective-permute-start | bytes 98312 | tf_op jit(solution)/shard_map/ppermute | solution.py:93
  181.3 24.4 %collective-permute-start.17 = (f32[32,256]{0,1:T(8,128)S(1)}, f32[32,256]{0,1:T(8,128)S(1)}, u32[]{:S(2)}, u32[]{:S(2)}) collective-permute-start(f32[32,256]{0,1:T(8,128)S(1)} %bitcast.154), channel_id=1, source_target_pairs={{0,64},{8,72},{16,80},{24,88},{32,96},{40,104},{48,112},{56,120},{... | collective-permute-start | bytes 98312 | tf_op jit(solution)/shard_map/ppermute | solution.py:93
  189.6 19.5 %collective-permute-start.16 = (f32[32,256]{0,1:T(8,128)S(1)}, f32[32,256]{0,1:T(8,128)S(1)}, u32[]{:S(2)}, u32[]{:S(2)}) collective-permute-start(f32[32,256]{0,1:T(8,128)S(1)} %bitcast.155), channel_id=1, source_target_pairs={{0,56},{8,64},{16,72},{24,80},{32,88},{40,96},{48,104},{56,112},{6... | collective-permute-start | bytes 98312 | tf_op jit(solution)/shard_map/ppermute | solution.py:93
  191.9 19.7 %collective-permute-start.15 = (f32[32,256]{0,1:T(8,128)S(1)}, f32[32,256]{0,1:T(8,128)S(1)}, u32[]{:S(2)}, u32[]{:S(2)}) collective-permute-start(f32[32,256]{0,1:T(8,128)S(1)} %bitcast.156), channel_id=1, source_target_pairs={{0,48},{8,56},{16,64},{24,72},{32,80},{40,88},{48,96},{56,104},{64... | collective-permute-start | bytes 98312 | tf_op jit(solution)/shard_map/ppermute | solution.py:93
  203.0 12.3 %collective-permute-start.14 = (f32[32,256]{0,1:T(8,128)S(1)}, f32[32,256]{0,1:T(8,128)S(1)}, u32[]{:S(2)}, u32[]{:S(2)}) collective-permute-start(f32[32,256]{0,1:T(8,128)S(1)} %bitcast.157), channel_id=1, source_target_pairs={{0,40},{8,48},{16,56},{24,64},{32,72},{40,80},{48,88},{56,96},{64,... | collective-permute-start | bytes 98312 | tf_op jit(solution)/shard_map/ppermute | solution.py:93
  204.4 11.0 %collective-permute-start.13 = (f32[32,256]{0,1:T(8,128)S(1)}, f32[32,256]{0,1:T(8,128)S(1)}, u32[]{:S(2)}, u32[]{:S(2)}) collective-permute-start(f32[32,256]{0,1:T(8,128)S(1)} %bitcast.158), channel_id=1, source_target_pairs={{0,32},{8,40},{16,48},{24,56},{32,64},{40,72},{48,80},{56,88},{64,... | collective-permute-start | bytes 98312 | tf_op jit(solution)/shard_map/ppermute | solution.py:93
  205.7 11.5 %collective-permute-start.12 = (f32[32,256]{0,1:T(8,128)S(1)}, f32[32,256]{0,1:T(8,128)S(1)}, u32[]{:S(2)}, u32[]{:S(2)}) collective-permute-start(f32[32,256]{0,1:T(8,128)S(1)} %bitcast.159), channel_id=1, source_target_pairs={{0,24},{8,32},{16,40},{24,48},{32,56},{40,64},{48,72},{56,80},{64,... | collective-permute-start | bytes 98312 | tf_op jit(solution)/shard_map/ppermute | solution.py:93
  209.1 8.1 %collective-permute-start.11 = (f32[32,256]{0,1:T(8,128)S(1)}, f32[32,256]{0,1:T(8,128)S(1)}, u32[]{:S(2)}, u32[]{:S(2)}) collective-permute-start(f32[32,256]{0,1:T(8,128)S(1)} %bitcast.160), channel_id=1, source_target_pairs={{0,16},{8,24},{16,32},{24,40},{32,48},{40,56},{48,64},{56,72},{64,... | collective-permute-start | bytes 98312 | tf_op jit(solution)/shard_map/ppermute | solution.py:93
  211.6 5.6 %collective-permute-start.10 = (f32[32,256]{0,1:T(8,128)S(1)}, f32[32,256]{0,1:T(8,128)S(1)}, u32[]{:S(2)}, u32[]{:S(2)}) collective-permute-start(f32[32,256]{0,1:T(8,128)S(1)} %bitcast.161), channel_id=1, source_target_pairs={{0,8},{8,16},{16,24},{24,32},{32,40},{40,48},{48,56},{56,64},{64,7... | collective-permute-start | bytes 98312 | tf_op jit(solution)/shard_map/ppermute | solution.py:93
  215.4 3.4 %copy-start.7 = (f32[512]{0:T(512)S(1)}, f32[512]{0:T(512)}, u32[]{:S(2)}) copy-start(f32[512]{0:T(512)} %param.11) | copy-start | bytes 6148
Sparse Core Ops, SparseCore 0:
  77.8 81.1 reduce-scatter.1

commit v3 on v2

--- a/solution.py
+++ b/solution.py
@@ -1,6 +1,8 @@
 import jax
 import jax.numpy as jnp
 from jax import lax
+from jax.experimental import pallas as pl
+from jax.experimental.pallas import tpu as pltpu
 from jax.sharding import Mesh
 from jax.sharding import PartitionSpec as P
 
@@ -19,6 +21,73 @@
     return jnp.einsum(spec, hi, data, preferred_element_type=jnp.float32) + jnp.einsum(
         spec, lo, data, preferred_element_type=jnp.float32
     )
+
+
+def ring_chip(r, n):
+    hi = r // (n // 2)
+    return 2 * (r + hi * (n - 1 - 2 * r)) + hi
+
+
+def ring_pos(p, n):
+    z, y = p // 2, p % 2
+    return z + y * (n - 1 - 2 * z)
+
+
+def rs_kernel(part_ref, out_ref, sbuf, rbuf, send_sem, recv_sem):
+    n = part_ref.shape[0]
+    chip = lax.axis_index("p")
+    core = lax.axis_index("c")
+    col = lax.axis_index("ch")
+    r = ring_pos(chip, n)
+    d = 1 - 2 * core
+    nxt = ring_chip((r + d + n) % n, n)
+    prv = ring_chip((r - d + n) % n, n)
+    mesh_id = pl.DeviceIdType.MESH
+    barrier = pltpu.get_barrier_semaphore()
+    for nb in (nxt, prv):
+        pl.semaphore_signal(barrier, 1, device_id=(nb, core, col), device_id_type=mesh_id)
+    pl.semaphore_wait(barrier, 2)
+    copies = []
+    for s in range(n - 1):
+        q = ring_chip((r - d * (1 + s) + 2 * n) % n, n)
+        if s == 0:
+            sbuf[0] = part_ref[q].astype(sbuf.dtype)
+        else:
+            copies[s - 1].wait_recv()
+            sbuf[s] = (rbuf[s - 1].astype(jnp.float32) + part_ref[q]).astype(sbuf.dtype)
+        copy = pltpu.make_async_remote_copy(
+            src_ref=sbuf.at[s],
+            dst_ref=rbuf.at[s],
+            send_sem=send_sem.at[s],
+            recv_sem=recv_sem.at[s],
+            device_id=(nxt, core, col),
+            device_id_type=mesh_id,
+        )
+        copy.start()
+        copies.append(copy)
+    copies[-1].wait_recv()
+    out_ref[...] = (rbuf[n - 2].astype(jnp.float32) + part_ref[chip]).astype(out_ref.dtype)
+    for copy in copies:
+        copy.wait_send()
+
+
+def ring_reduce_scatter(partial):
+    n, rows, width = partial.shape
+    return pl.pallas_call(
+        rs_kernel,
+        out_shape=jax.ShapeDtypeStruct((rows, width), jnp.bfloat16),
+        in_specs=[pl.BlockSpec(memory_space=pltpu.VMEM)],
+        out_specs=pl.BlockSpec(memory_space=pltpu.VMEM),
+        scratch_shapes=[
+            pltpu.VMEM((n - 1, rows, width), jnp.bfloat16),
+            pltpu.VMEM((n - 1, rows, width), jnp.bfloat16),
+            pltpu.SemaphoreType.DMA((n - 1,)),
+            pltpu.SemaphoreType.DMA((n - 1,)),
+        ],
+        compiler_params=pltpu.CompilerParams(
+            collective_id=0, has_side_effects=True, vmem_limit_bytes=48 * 1024 * 1024
+        ),
+    )(partial)
 
 
 def local(tokens, w_in, short_filter, decay_rate, residue, skip):
@@ -56,9 +125,7 @@
     partial = jnp.dot(
         tok_ext.reshape(n_blk * ext_len, -1), flat_w, preferred_element_type=jnp.float32
     ).reshape(n_blk, ext_len, -1)
-    proj = lax.psum_scatter(
-        partial.astype(jnp.bfloat16), "p", scatter_dimension=0, tiled=False
-    ).astype(jnp.float32)
+    proj = ring_reduce_scatter(partial).astype(jnp.float32)
     first = jnp.logical_and(chip == 0, core == 0)
     row_id = lax.broadcasted_iota(jnp.int32, proj.shape, 0)
     proj = jnp.where(jnp.logical_and(first, row_id < 2), 0.0, proj)

time: 227 us -> 195 us (0.86)
  waiting for transfers between devices: 88.8 us -> 12.9 us
  Pallas kernels: 0 us -> 51.1 us
  between operations: 13.8 us -> 0.6 us
    reduce_scatter x1 -> x0, waiting for transfers between devices: 76.1 us -> none  [local(): lax.psum_scatter(partial.astype(jnp.bfloat16), 'p', scatter_dimension=0,...]
    pallas_call x0 -> x1, Pallas kernels: none -> 51.1 us  [ring_reduce_scatter(): pl.pallas_call(rs_kernel, out_shape=jax.ShapeDtypeStruct((rows, width), j...]
    ppermute x8, starting transfers between devices: 35.4 us -> 27.9 us  [local(): pieces.append(lax.ppermute(tokens, ('p', 'ch'), pairs))]
    ppermute x15, starting transfers between devices: 35.2 us -> 42.4 us  [local(): got = lax.ppermute(s_flat, ('p', 'c'), pairs)]
    unnamed x27 -> x51, local copies, waits for them, and re-layouts: 9.77 us -> 9.87 us
  transfers between devices with their start and end apart: 26 -> 25, of which waited for: 6 -> 5; matrix products, arithmetic and copies ran while one was open for 8% -> 12% of each run, Pallas kernels for 0% -> 0%
where the time goes in v3:
time: 195 us; the launch traced here: 192 us
  starting transfers between devices  80.5 us (41%)
  Pallas kernels  51.1 us (26%)
  local copies, waits for them, and re-layouts  23.3 us (12%)
  matrix products  16.6 us (9%)
  waiting for transfers between devices  12.9 us (7%)
  other arithmetic  7.49 us (4%)
    pallas_call x1, Pallas kernels, ring_reduce_scatter(): pl.pallas_call(rs_kernel, out_shape=jax.ShapeDtypeStruct((rows, width), j...  51.1 us
    ppermute x15, starting transfers between devices, local(): got = lax.ppermute(s_flat, ('p', 'c'), pairs)  42.4 us
    ppermute x8, starting transfers between devices, local(): pieces.append(lax.ppermute(tokens, ('p', 'ch'), pairs))  27.9 us
    dot_general x1, matrix products, local(): jnp.dot(tok_ext.reshape(n_blk * ext_len, -1), flat_w, preferred_element_t...  9.96 us
    unnamed x51, local copies, waits for them, and re-layouts  9.87 us
    ppermute x15, waiting for transfers between devices, local(): got = lax.ppermute(s_flat, ('p', 'c'), pairs)  9.12 us
    ppermute x1, starting transfers between devices, local(): partner_tail = lax.ppermute(tail, 'c', [(0, 1), (1, 0)])  5.88 us
    ppermute x1, starting transfers between devices, local(): w_other = lax.ppermute(w_flat, 'c', [(0, 1), (1, 0)])  4.25 us
  transfers between devices with their start and end apart: 25, of which 5 were waited for; matrix products, arithmetic and copies ran while one was open for 12% of the time, Pallas kernels for 0%

profile of v3, /device:TPU:1, one launch (start us, length us, event | category | flops | bytes accessed | tf_op | source)
XLA Modules:
  0.0 192.4 jit_solution(11869941138506086300)
XLA Ops:
  0.0 1.6 collective-permute-start
  1.6 3.7 %collective-permute-start.1 = (bf16[128,1024]{1,0:T(8,128)(2,1)}, bf16[128,1024]{1,0:T(8,128)(2,1)S(1)}, u32[]{:S(2)}, u32[]{:S(2)}) collective-permute-start(bf16[128,1024]{1,0:T(8,128)(2,1)} %param.6), channel_id=1, source_target_pairs={{0,1},{1,17},{2,33},{3,49},{4,65},{5,81},{6,97},{7,113},{16,2},{17... | collective-permute-start | bytes 786440 | tf_op jit(solution)/shard_map/ppermute | solution.py:106
  5.3 3.6 %collective-permute-start.2 = (bf16[128,1024]{1,0:T(8,128)(2,1)}, bf16[128,1024]{1,0:T(8,128)(2,1)S(1)}, u32[]{:S(2)}, u32[]{:S(2)}) collective-permute-start(bf16[128,1024]{1,0:T(8,128)(2,1)} %param.6), channel_id=1, source_target_pairs={{0,2},{1,18},{2,34},{3,50},{4,66},{5,82},{6,98},{7,114},{16,3},{17... | collective-permute-start | bytes 786440 | tf_op jit(solution)/shard_map/ppermute | solution.py:106
  8.9 4.4 %collective-permute-start.3 = (bf16[128,1024]{1,0:T(8,128)(2,1)}, bf16[128,1024]{1,0:T(8,128)(2,1)S(1)}, u32[]{:S(2)}, u32[]{:S(2)}) collective-permute-start(bf16[128,1024]{1,0:T(8,128)(2,1)} %param.6), channel_id=1, source_target_pairs={{0,3},{1,19},{2,35},{3,51},{4,67},{5,83},{6,99},{7,115},{16,4},{17... | collective-permute-start | bytes 786440 | tf_op jit(solution)/shard_map/ppermute | solution.py:106
  13.3 5.9 %collective-permute-start.4 = (bf16[128,1024]{1,0:T(8,128)(2,1)}, bf16[128,1024]{1,0:T(8,128)(2,1)S(1)}, u32[]{:S(2)}, u32[]{:S(2)}) collective-permute-start(bf16[128,1024]{1,0:T(8,128)(2,1)} %param.6), channel_id=1, source_target_pairs={{0,4},{1,20},{2,36},{3,52},{4,68},{5,84},{6,100},{7,116},{16,5},{1... | collective-permute-start | bytes 786440 | tf_op jit(solution)/shard_map/ppermute | solution.py:106
  19.2 1.0 sort.17
  20.2 0.7 slice_bitcast_fusion.3
  21.0 0.8 copy.40
  21.7 1.4 exponential_select_fusion.14
  23.3 3.7 %fusion.28 = f32[32,128,128]{2,1,0:T(8,128)S(1)} fusion(f32[32,16]{1,0:T(8,128)S(1)} %copy.40, f32[32,16]{1,0:T(8,128)S(1)} %copy.39, f32[32,16]{1,0:T(8,128)S(1)} %copy.38), kind=kOutput, calls=%fused_computation.49 | convolution fusion | flops 100859904 | bytes 2103296 | tf_op jit(solution)/shard_map/gtr,gsr->gts/dot_general | solution.py:147
  27.0 0.6 iota_compare_fusion
  27.6 2.6 %copy.33 = bf16[512,3,512]{0,2,1:T(8,128)(2,1)} copy(bf16[512,3,512]{2,0,1:T(8,128)(2,1)} %param.7) | data formatting | bytes 3145728 | tf_op args[1]
  30.2 1.9 collective-permute-start.5
  32.2 0.7 bitcast_dynamic-update-slice_fusion.7
  32.9 0.6 collective-permute-start.6
  33.5 0.7 bitcast_dynamic-update-slice_fusion.6
  34.2 6.1 %collective-permute-start.7 = (bf16[128,1024]{1,0:T(8,128)(2,1)}, bf16[128,1024]{1,0:T(8,128)(2,1)S(1)}, u32[]{:S(2)}, u32[]{:S(2)}) collective-permute-start(bf16[128,1024]{1,0:T(8,128)(2,1)} %param.6), channel_id=1, source_target_pairs={{0,7},{1,23},{2,39},{3,55},{4,71},{5,87},{6,103},{7,119},{16,0},{1... | collective-permute-start | bytes 786440 | tf_op jit(solution)/shard_map/ppermute | solution.py:106
  40.4 0.7 bitcast_dynamic-update-slice_fusion.5
  41.1 4.2 %collective-permute-start.9 = (bf16[512,1536]{0,1:T(8,128)(2,1)}, bf16[512,1536]{0,1:T(8,128)(2,1)}, u32[]{:S(2)}, u32[]{:S(2)}) collective-permute-start(bf16[512,1536]{0,1:T(8,128)(2,1)} %bitcast.143), channel_id=1, source_target_pairs={{0,8},{8,0},{1,9},{9,1},{2,10},{10,2},{3,11},{11,3},{4,12},{12,4},... | collective-permute-start | bytes 4718600 | tf_op jit(solution)/shard_map/ppermute | solution.py:112
  45.3 0.7 bitcast_dynamic-update-slice_fusion.4
  46.0 0.7 bitcast_dynamic-update-slice_fusion.3
  46.8 0.4 collective-permute-done.5
  47.2 0.7 bitcast_dynamic-update-slice_fusion.2
  47.9 0.7 bitcast_dynamic-update-slice_fusion.1
  48.6 2.4 %collective-permute-done.7 = bf16[128,1024]{1,0:T(8,128)(2,1)S(1)} collective-permute-done((bf16[128,1024]{1,0:T(8,128)(2,1)}, bf16[128,1024]{1,0:T(8,128)(2,1)S(1)}, u32[]{:S(2)}, u32[]{:S(2)}) %collective-permute-start.7) | collective-permute-done | bytes 262176 | tf_op jit(solution)/shard_map/ppermute | solution.py:106
  51.1 0.7 bitcast_dynamic-update-slice_fusion
  51.8 3.6 %gather_fusion = bf16[8,128,1024]{2,1,0:T(8,128)(2,1)} fusion(bf16[8,128,1024]{2,1,0:T(8,128)(2,1)} %bitcast_dynamic-update-slice_fusion, s32[1024]{0:T(1024)S(1)} %pad_clamp_fusion), kind=kCustom, calls=%fused_computation | custom fusion | bytes 4194336 | tf_op jit(solution)/shard_map/jit(_take)/gather | solution.py:110
  55.4 1.9 broadcast_select_fusion
  57.3 1.4 copy-done
  58.7 5.9 %collective-permute-start.8 = (bf16[8,2,1024]{2,1,0:T(2,128)(2,1)S(1)}, bf16[8,2,1024]{2,1,0:T(2,128)(2,1)S(1)}, u32[]{:S(2)}, u32[]{:S(2)}) collective-permute-start(bf16[8,2,1024]{2,1,0:T(2,128)(2,1)S(1)} %slice.58), channel_id=1, source_target_pairs={{0,8},{8,0},{1,9},{9,1},{2,10},{10,2},{3,11},{11,3},{4,12},{12,4},... | collective-permute-start | bytes 98312 | tf_op jit(solution)/shard_map/ppermute | solution.py:120
  64.6 0.9 collective-permute-done.8
  65.5 10.0 %fusion.1.part_ref = f32[8,130,1536]{2,1,0:T(8,128)} fusion(bf16[512,1536]{0,1:T(8,128)(2,1)} %collective-permute-done.9, bf16[512,1536]{0,1:T(8,128)(2,1)} %bitcast.144, pred[]{:T(512)S(6)} %eq.13, bf16[8,128,1024]{2,1,0:T(8,128)(2,1)} %copy-done, bf16[8,2,1024]{2,1,0:T(2,128)(2,1)S(1)} %broadcast_select_fusion.1), kind=kOutput, calls=%fused_computation.3 | convolution fusion | flops 3289972736 | bytes 11665409 | tf_op jit(solution)/shard_map/dot_general | solution.py:125
  75.5 51.1 %shard_map.64 = bf16[130,1536]{1,0:T(8,128)(2,1)S(1)} custom-call(f32[8,130,1536]{2,1,0:T(8,128)} %fusion.1.part_ref), custom_call_target="tpu_custom_call" | custom-call | tf_op jit(solution)/shard_map/pallas_call | solution.py:76
  126.7 1.3 fusion.66
  128.0 2.3 %copy.37 = f32[128,1536]{0,1:T(8,128)} copy(f32[128,1536]{1,0:T(8,128)} %get-tuple-element.8) | data formatting | bytes 1572864 | tf_op jit(solution)/shard_map/slice | solution.py:136
  130.3 2.3 %copy.36 = f32[128,1536]{0,1:T(8,128)} copy(f32[128,1536]{1,0:T(8,128)} %get-tuple-element.9) | data formatting | bytes 1572864 | tf_op jit(solution)/shard_map/slice | solution.py:135
  132.6 1.2 copy.35
  133.7 2.0 %multiply_add_fusion = f32[128,3,512]{0,2,1:T(8,128)S(1)} fusion(f32[128,3,512]{0,2,1:T(8,128)} %bitcast.140, f32[128,3,512]{0,2,1:T(8,128)} %bitcast.141, f32[128,3,512]{0,2,1:T(8,128)} %bitcast.142, f32[3,512]{1,0:T(4,128)S(1)} %get-tuple-element.11, f32[3,512]{1,0:T(4,128)S(1)} %get-tuple-element.12, f32[3,512]{1,0:T(4,128)S(1)} %get-tuple-element.10), kind=kLoop, calls=%fused_computation.26 | loop fusion | flops 983040 | bytes 3164160 | tf_op jit(solution)/shard_map/add | solution.py:134
  135.8 0.3 fusion.36
  136.1 1.0 convolution_add_fusion.1
  137.1 0.2 copy.41
  137.3 0.7 collective-permute-start.24
  137.9 8.6 %collective-permute-start.23 = (f32[32,256]{0,1:T(8,128)S(1)}, f32[32,256]{0,1:T(8,128)S(1)}, u32[]{:S(2)}, u32[]{:S(2)}) collective-permute-start(f32[32,256]{0,1:T(8,128)S(1)} %bitcast.147), channel_id=1, source_target_pairs={{0,112},{8,120},{1,113},{9,121},{2,114},{10,122},{3,115},{11,123},... | collective-permute-start | bytes 98312 | tf_op jit(solution)/shard_map/ppermute | solution.py:160
  146.5 3.8 %collective-permute-start.22 = (f32[32,256]{0,1:T(8,128)S(1)}, f32[32,256]{0,1:T(8,128)S(1)}, u32[]{:S(2)}, u32[]{:S(2)}) collective-permute-start(f32[32,256]{0,1:T(8,128)S(1)} %bitcast.148), channel_id=1, source_target_pairs={{0,104},{8,112},{16,120},{1,105},{9,113},{17,121},{2,106},{10,114}... | collective-permute-start | bytes 98312 | tf_op jit(solution)/shard_map/ppermute | solution.py:160
  150.4 1.3 collective-permute-start.21
  151.7 2.3 %collective-permute-start.20 = (f32[32,256]{0,1:T(8,128)S(1)}, f32[32,256]{0,1:T(8,128)S(1)}, u32[]{:S(2)}, u32[]{:S(2)}) collective-permute-start(f32[32,256]{0,1:T(8,128)S(1)} %bitcast.150), channel_id=1, source_target_pairs={{0,88},{8,96},{16,104},{24,112},{32,120},{1,89},{9,97},{17,105},{2... | collective-permute-start | bytes 98312 | tf_op jit(solution)/shard_map/ppermute | solution.py:160
  154.1 1.4 collective-permute-start.19
  155.6 1.3 collective-permute-start.18
  156.9 1.3 collective-permute-start.17
  158.2 1.3 collective-permute-start.16
  159.5 7.4 %collective-permute-done.20 = f32[32,256]{0,1:T(8,128)S(1)} collective-permute-done((f32[32,256]{0,1:T(8,128)S(1)}, f32[32,256]{0,1:T(8,128)S(1)}, u32[]{:S(2)}, u32[]{:S(2)}) %collective-permute-start.20) | collective-permute-done | bytes 32800 | tf_op jit(solution)/shard_map/ppermute | solution.py:160
  166.9 8.7 %collective-permute-start.15 = (f32[32,256]{0,1:T(8,128)S(1)}, f32[32,256]{0,1:T(8,128)S(1)}, u32[]{:S(2)}, u32[]{:S(2)}) collective-permute-start(f32[32,256]{0,1:T(8,128)S(1)} %bitcast.155), channel_id=1, source_target_pairs={{0,48},{8,56},{16,64},{24,72},{32,80},{40,88},{48,96},{56,104},{64... | collective-permute-start | bytes 98312 | tf_op jit(solution)/shard_map/ppermute | solution.py:160
  175.6 0.6 fusion.14
  176.3 1.5 collective-permute-start.14
  177.8 1.3 collective-permute-start.13
  179.1 3.3 %collective-permute-start.12 = (f32[32,256]{0,1:T(8,128)S(1)}, f32[32,256]{0,1:T(8,128)S(1)}, u32[]{:S(2)}, u32[]{:S(2)}) collective-permute-start(f32[32,256]{0,1:T(8,128)S(1)} %bitcast.158), channel_id=1, source_target_pairs={{0,24},{8,32},{16,40},{24,48},{32,56},{40,64},{48,72},{56,80},{64,... | collective-permute-start | bytes 98312 | tf_op jit(solution)/shard_map/ppermute | solution.py:160
  182.4 2.5 %collective-permute-start.11 = (f32[32,256]{0,1:T(8,128)S(1)}, f32[32,256]{0,1:T(8,128)S(1)}, u32[]{:S(2)}, u32[]{:S(2)}) collective-permute-start(f32[32,256]{0,1:T(8,128)S(1)} %bitcast.159), channel_id=1, source_target_pairs={{0,16},{8,24},{16,32},{24,40},{32,48},{40,56},{48,64},{56,72},{64,... | collective-permute-start | bytes 98312 | tf_op jit(solution)/shard_map/ppermute | solution.py:160
  185.0 3.1 %collective-permute-start.10 = (f32[32,256]{0,1:T(8,128)S(1)}, f32[32,256]{0,1:T(8,128)S(1)}, u32[]{:S(2)}, u32[]{:S(2)}) collective-permute-start(f32[32,256]{0,1:T(8,128)S(1)} %bitcast.160), channel_id=1, source_target_pairs={{0,8},{8,16},{16,24},{24,32},{32,40},{40,48},{48,56},{56,64},{64,7... | collective-permute-start | bytes 98312 | tf_op jit(solution)/shard_map/ppermute | solution.py:160
  188.1 0.6 fusion.13
  188.8 1.7 collective-permute-done.12
  190.6 0.2 fusion.38
  190.8 0.2 copy.42
  191.0 0.5 convolution_add_fusion
  191.7 0.8 copy.43
  (77 shorter events, 0.8 us)
Async XLA Ops:
  0.0 30.2 %collective-permute-start = (bf16[128,1024]{1,0:T(8,128)(2,1)}, bf16[128,1024]{1,0:T(8,128)(2,1)S(1)}, u32[]{:S(2)}, u32[]{:S(2)}) collective-permute-start(bf16[128,1024]{1,0:T(8,128)(2,1)} %param.6), channel_id=1, source_target_pairs={{0,0},{1,16},{2,32},{3,48},{4,64},{5,80},{6,96},{7,112},{16,1},{17... | collective-permute-start | bytes 786440 | tf_op jit(solution)/shard_map/ppermute | solution.py:106
  1.6 31.3 %collective-permute-start.1 = (bf16[128,1024]{1,0:T(8,128)(2,1)}, bf16[128,1024]{1,0:T(8,128)(2,1)S(1)}, u32[]{:S(2)}, u32[]{:S(2)}) collective-permute-start(bf16[128,1024]{1,0:T(8,128)(2,1)} %param.6), channel_id=1, source_target_pairs={{0,1},{1,17},{2,33},{3,49},{4,65},{5,81},{6,97},{7,113},{16,2},{17... | collective-permute-start | bytes 786440 | tf_op jit(solution)/shard_map/ppermute | solution.py:106
  5.3 29.0 %collective-permute-start.2 = (bf16[128,1024]{1,0:T(8,128)(2,1)}, bf16[128,1024]{1,0:T(8,128)(2,1)S(1)}, u32[]{:S(2)}, u32[]{:S(2)}) collective-permute-start(bf16[128,1024]{1,0:T(8,128)(2,1)} %param.6), channel_id=1, source_target_pairs={{0,2},{1,18},{2,34},{3,50},{4,66},{5,82},{6,98},{7,114},{16,3},{17... | collective-permute-start | bytes 786440 | tf_op jit(solution)/shard_map/ppermute | solution.py:106
  8.9 32.2 %collective-permute-start.3 = (bf16[128,1024]{1,0:T(8,128)(2,1)}, bf16[128,1024]{1,0:T(8,128)(2,1)S(1)}, u32[]{:S(2)}, u32[]{:S(2)}) collective-permute-start(bf16[128,1024]{1,0:T(8,128)(2,1)} %param.6), channel_id=1, source_target_pairs={{0,3},{1,19},{2,35},{3,51},{4,67},{5,83},{6,99},{7,115},{16,4},{17... | collective-permute-start | bytes 786440 | tf_op jit(solution)/shard_map/ppermute | solution.py:106
  13.3 32.7 %collective-permute-start.4 = (bf16[128,1024]{1,0:T(8,128)(2,1)}, bf16[128,1024]{1,0:T(8,128)(2,1)S(1)}, u32[]{:S(2)}, u32[]{:S(2)}) collective-permute-start(bf16[128,1024]{1,0:T(8,128)(2,1)} %param.6), channel_id=1, source_target_pairs={{0,4},{1,20},{2,36},{3,52},{4,68},{5,84},{6,100},{7,116},{16,5},{1... | collective-permute-start | bytes 786440 | tf_op jit(solution)/shard_map/ppermute | solution.py:106
  23.3 6.9 %copy-start.2 = (f32[32,16]{1,0:T(8,128)}, f32[32,16]{1,0:T(8,128)S(1)}, u32[]{:S(2)}) copy-start(f32[32,16]{1,0:T(8,128)S(1)} %copy.38) | copy-start | bytes 6148
  27.6 108.2 %copy-start.20 = (f32[128]{0:T(128)}, f32[128]{0:T(128)S(1)}, u32[]{:S(2)}) copy-start(f32[128]{0:T(128)S(1)} %iota_subtract_fusion) | copy-start | bytes 1540
  30.2 16.9 %collective-permute-start.5 = (bf16[128,1024]{1,0:T(8,128)(2,1)}, bf16[128,1024]{1,0:T(8,128)(2,1)S(1)}, u32[]{:S(2)}, u32[]{:S(2)}) collective-permute-start(bf16[128,1024]{1,0:T(8,128)(2,1)} %param.6), channel_id=1, source_target_pairs={{0,5},{1,21},{2,37},{3,53},{4,69},{5,85},{6,101},{7,117},{16,6},{1... | collective-permute-start | bytes 786440 | tf_op jit(solution)/shard_map/ppermute | solution.py:106
  32.9 15.0 %collective-permute-start.6 = (bf16[128,1024]{1,0:T(8,128)(2,1)}, bf16[128,1024]{1,0:T(8,128)(2,1)S(1)}, u32[]{:S(2)}, u32[]{:S(2)}) collective-permute-start(bf16[128,1024]{1,0:T(8,128)(2,1)} %param.6), channel_id=1, source_target_pairs={{0,6},{1,22},{2,38},{3,54},{4,70},{5,86},{6,102},{7,118},{16,7},{1... | collective-permute-start | bytes 786440 | tf_op jit(solution)/shard_map/ppermute | solution.py:106
  34.2 16.8 %collective-permute-start.7 = (bf16[128,1024]{1,0:T(8,128)(2,1)}, bf16[128,1024]{1,0:T(8,128)(2,1)S(1)}, u32[]{:S(2)}, u32[]{:S(2)}) collective-permute-start(bf16[128,1024]{1,0:T(8,128)(2,1)} %param.6), channel_id=1, source_target_pairs={{0,7},{1,23},{2,39},{3,55},{4,71},{5,87},{6,103},{7,119},{16,0},{1... | collective-permute-start | bytes 786440 | tf_op jit(solution)/shard_map/ppermute | solution.py:106
  41.1 24.4 %collective-permute-start.9 = (bf16[512,1536]{0,1:T(8,128)(2,1)}, bf16[512,1536]{0,1:T(8,128)(2,1)}, u32[]{:S(2)}, u32[]{:S(2)}) collective-permute-start(bf16[512,1536]{0,1:T(8,128)(2,1)} %bitcast.143), channel_id=1, source_target_pairs={{0,8},{8,0},{1,9},{9,1},{2,10},{10,2},{3,11},{11,3},{4,12},{12,4},... | collective-permute-start | bytes 4718600 | tf_op jit(solution)/shard_map/ppermute | solution.py:112
  57.3 1.4 copy-start
  58.7 6.7 %collective-permute-start.8 = (bf16[8,2,1024]{2,1,0:T(2,128)(2,1)S(1)}, bf16[8,2,1024]{2,1,0:T(2,128)(2,1)S(1)}, u32[]{:S(2)}, u32[]{:S(2)}) collective-permute-start(bf16[8,2,1024]{2,1,0:T(2,128)(2,1)S(1)} %slice.58), channel_id=1, source_target_pairs={{0,8},{8,0},{1,9},{9,1},{2,10},{10,2},{3,11},{11,3},{4,12},{12,4},... | collective-permute-start | bytes 98312 | tf_op jit(solution)/shard_map/ppermute | solution.py:120
  133.7 41.9 %copy-start.1 = (pred[128,128]{1,0:T(8,128)(4,1)S(1)}, pred[128,128]{1,0:T(8,128)(4,1)}, u32[]{:S(2)}) copy-start(pred[128,128]{1,0:T(8,128)(4,1)} %iota_compare_fusion) | copy-start | bytes 49156
  137.3 16.9 %collective-permute-start.24 = (f32[32,256]{0,1:T(8,128)S(1)}, f32[32,256]{0,1:T(8,128)S(1)}, u32[]{:S(2)}, u32[]{:S(2)}) collective-permute-start(f32[32,256]{0,1:T(8,128)S(1)} %bitcast.146), channel_id=1, source_target_pairs={{0,120},{1,121},{2,122},{3,123},{4,124},{5,125},{6,126},{7,127}} | collective-permute-start | bytes 98312 | tf_op jit(solution)/shard_map/ppermute | solution.py:160
  137.9 17.7 %collective-permute-start.23 = (f32[32,256]{0,1:T(8,128)S(1)}, f32[32,256]{0,1:T(8,128)S(1)}, u32[]{:S(2)}, u32[]{:S(2)}) collective-permute-start(f32[32,256]{0,1:T(8,128)S(1)} %bitcast.147), channel_id=1, source_target_pairs={{0,112},{8,120},{1,113},{9,121},{2,114},{10,122},{3,115},{11,123},... | collective-permute-start | bytes 98312 | tf_op jit(solution)/shard_map/ppermute | solution.py:160
  146.5 10.4 %collective-permute-start.22 = (f32[32,256]{0,1:T(8,128)S(1)}, f32[32,256]{0,1:T(8,128)S(1)}, u32[]{:S(2)}, u32[]{:S(2)}) collective-permute-start(f32[32,256]{0,1:T(8,128)S(1)} %bitcast.148), channel_id=1, source_target_pairs={{0,104},{8,112},{16,120},{1,105},{9,113},{17,121},{2,106},{10,114}... | collective-permute-start | bytes 98312 | tf_op jit(solution)/shard_map/ppermute | solution.py:160
  150.4 7.8 %collective-permute-start.21 = (f32[32,256]{0,1:T(8,128)S(1)}, f32[32,256]{0,1:T(8,128)S(1)}, u32[]{:S(2)}, u32[]{:S(2)}) collective-permute-start(f32[32,256]{0,1:T(8,128)S(1)} %bitcast.149), channel_id=1, source_target_pairs={{0,96},{8,104},{16,112},{24,120},{1,97},{9,105},{17,113},{25,121},... | collective-permute-start | bytes 98312 | tf_op jit(solution)/shard_map/ppermute | solution.py:160
  151.7 15.2 %collective-permute-start.20 = (f32[32,256]{0,1:T(8,128)S(1)}, f32[32,256]{0,1:T(8,128)S(1)}, u32[]{:S(2)}, u32[]{:S(2)}) collective-permute-start(f32[32,256]{0,1:T(8,128)S(1)} %bitcast.150), channel_id=1, source_target_pairs={{0,88},{8,96},{16,104},{24,112},{32,120},{1,89},{9,97},{17,105},{2... | collective-permute-start | bytes 98312 | tf_op jit(solution)/shard_map/ppermute | solution.py:160
  154.0 36.5 %copy-start.4 = (f32[32,16]{0,1:T(8,128)S(1)}, f32[32,16]{0,1:T(8,128)}, u32[]{:S(2)}) copy-start(f32[32,16]{0,1:T(8,128)} %get-tuple-element.13) | copy-start | bytes 6148
  154.0 36.5 %copy-start.5 = (f32[32,16]{0,1:T(8,128)S(1)}, f32[32,16]{0,1:T(8,128)}, u32[]{:S(2)}) copy-start(f32[32,16]{0,1:T(8,128)} %get-tuple-element.14) | copy-start | bytes 6148
  154.0 36.5 %copy-start.6 = (f32[32,16]{0,1:T(8,128)S(1)}, f32[32,16]{0,1:T(8,128)}, u32[]{:S(2)}) copy-start(f32[32,16]{0,1:T(8,128)} %get-tuple-element.15) | copy-start | bytes 6148
  154.0 36.5 %copy-start.7 = (f32[32,16]{0,1:T(8,128)S(1)}, f32[32,16]{0,1:T(8,128)}, u32[]{:S(2)}) copy-start(f32[32,16]{0,1:T(8,128)} %get-tuple-element.16) | copy-start | bytes 6148
  154.0 36.5 %copy-start.8 = (f32[32,16]{0,1:T(8,128)S(1)}, f32[32,16]{0,1:T(8,128)}, u32[]{:S(2)}) copy-start(f32[32,16]{0,1:T(8,128)} %get-tuple-element.17) | copy-start | bytes 6148
  154.0 36.5 %copy-start.9 = (f32[32,16]{0,1:T(8,128)S(1)}, f32[32,16]{0,1:T(8,128)}, u32[]{:S(2)}) copy-start(f32[32,16]{0,1:T(8,128)} %get-tuple-element.18) | copy-start | bytes 6148
  154.0 36.5 %copy-start.10 = (f32[32,16]{0,1:T(8,128)S(1)}, f32[32,16]{0,1:T(8,128)}, u32[]{:S(2)}) copy-start(f32[32,16]{0,1:T(8,128)} %get-tuple-element.19) | copy-start | bytes 6148
  154.1 36.5 %copy-start.11 = (f32[32,16]{0,1:T(8,128)S(1)}, f32[32,16]{0,1:T(8,128)}, u32[]{:S(2)}) copy-start(f32[32,16]{0,1:T(8,128)} %get-tuple-element.20) | copy-start | bytes 6148
  154.1 36.5 %copy-start.12 = (f32[32,16]{0,1:T(8,128)S(1)}, f32[32,16]{0,1:T(8,128)}, u32[]{:S(2)}) copy-start(f32[32,16]{0,1:T(8,128)} %get-tuple-element.21) | copy-start | bytes 6148
  154.1 36.5 %copy-start.13 = (f32[32,16]{0,1:T(8,128)S(1)}, f32[32,16]{0,1:T(8,128)}, u32[]{:S(2)}) copy-start(f32[32,16]{0,1:T(8,128)} %get-tuple-element.22) | copy-start | bytes 6148
  154.1 36.5 %copy-start.14 = (f32[32,16]{0,1:T(8,128)S(1)}, f32[32,16]{0,1:T(8,128)}, u32[]{:S(2)}) copy-start(f32[32,16]{0,1:T(8,128)} %get-tuple-element.23) | copy-start | bytes 6148
  154.1 36.5 %copy-start.15 = (f32[32,16]{0,1:T(8,128)S(1)}, f32[32,16]{0,1:T(8,128)}, u32[]{:S(2)}) copy-start(f32[32,16]{0,1:T(8,128)} %get-tuple-element.24) | copy-start | bytes 6148
  154.1 36.5 %copy-start.16 = (f32[32,16]{0,1:T(8,128)S(1)}, f32[32,16]{0,1:T(8,128)}, u32[]{:S(2)}) copy-start(f32[32,16]{0,1:T(8,128)} %get-tuple-element.25) | copy-start | bytes 6148
  154.1 36.5 %copy-start.17 = (f32[32,16]{0,1:T(8,128)S(1)}, f32[32,16]{0,1:T(8,128)}, u32[]{:S(2)}) copy-start(f32[32,16]{0,1:T(8,128)} %get-tuple-element.26) | copy-start | bytes 6148
  154.1 36.5 %copy-start.18 = (f32[32,16]{0,1:T(8,128)S(1)}, f32[32,16]{0,1:T(8,128)}, u32[]{:S(2)}) copy-start(f32[32,16]{0,1:T(8,128)} %get-tuple-element.27) | copy-start | bytes 6148
  154.1 22.1 %collective-permute-start.19 = (f32[32,256]{0,1:T(8,128)S(1)}, f32[32,256]{0,1:T(8,128)S(1)}, u32[]{:S(2)}, u32[]{:S(2)}) collective-permute-start(f32[32,256]{0,1:T(8,128)S(1)} %bitcast.151), channel_id=1, source_target_pairs={{0,80},{8,88},{16,96},{24,104},{32,112},{40,120},{1,81},{9,89},{17... | collective-permute-start | bytes 98312 | tf_op jit(solution)/shard_map/ppermute | solution.py:160
  155.6 22.2 %collective-permute-start.18 = (f32[32,256]{0,1:T(8,128)S(1)}, f32[32,256]{0,1:T(8,128)S(1)}, u32[]{:S(2)}, u32[]{:S(2)}) collective-permute-start(f32[32,256]{0,1:T(8,128)S(1)} %bitcast.152), channel_id=1, source_target_pairs={{0,72},{8,80},{16,88},{24,96},{32,104},{40,112},{48,120},{1,73},{9... | collective-permute-start | bytes 98312 | tf_op jit(solution)/shard_map/ppermute | solution.py:160
  156.9 22.2 %collective-permute-start.17 = (f32[32,256]{0,1:T(8,128)S(1)}, f32[32,256]{0,1:T(8,128)S(1)}, u32[]{:S(2)}, u32[]{:S(2)}) collective-permute-start(f32[32,256]{0,1:T(8,128)S(1)} %bitcast.153), channel_id=1, source_target_pairs={{0,64},{8,72},{16,80},{24,88},{32,96},{40,104},{48,112},{56,120},{... | collective-permute-start | bytes 98312 | tf_op jit(solution)/shard_map/ppermute | solution.py:160
  158.2 24.2 %collective-permute-start.16 = (f32[32,256]{0,1:T(8,128)S(1)}, f32[32,256]{0,1:T(8,128)S(1)}, u32[]{:S(2)}, u32[]{:S(2)}) collective-permute-start(f32[32,256]{0,1:T(8,128)S(1)} %bitcast.154), channel_id=1, source_target_pairs={{0,56},{8,64},{16,72},{24,80},{32,88},{40,96},{48,104},{56,112},{6... | collective-permute-start | bytes 98312 | tf_op jit(solution)/shard_map/ppermute | solution.py:160
  166.9 18.1 %collective-permute-start.15 = (f32[32,256]{0,1:T(8,128)S(1)}, f32[32,256]{0,1:T(8,128)S(1)}, u32[]{:S(2)}, u32[]{:S(2)}) collective-permute-start(f32[32,256]{0,1:T(8,128)S(1)} %bitcast.155), channel_id=1, source_target_pairs={{0,48},{8,56},{16,64},{24,72},{32,80},{40,88},{48,96},{56,104},{64... | collective-permute-start | bytes 98312 | tf_op jit(solution)/shard_map/ppermute | solution.py:160
  176.3 14.7 %copy-start.3 = (f32[32,16]{1,0:T(8,128)S(1)}, f32[32,16]{1,0:T(8,128)}, u32[]{:S(2)}) copy-start(f32[32,16]{1,0:T(8,128)} %copy-done.2) | copy-start | bytes 6148
  176.3 12.5 %collective-permute-start.14 = (f32[32,256]{0,1:T(8,128)S(1)}, f32[32,256]{0,1:T(8,128)S(1)}, u32[]{:S(2)}, u32[]{:S(2)}) collective-permute-start(f32[32,256]{0,1:T(8,128)S(1)} %bitcast.156), channel_id=1, source_target_pairs={{0,40},{8,48},{16,56},{24,64},{32,72},{40,80},{48,88},{56,96},{64,... | collective-permute-start | bytes 98312 | tf_op jit(solution)/shard_map/ppermute | solution.py:160
  177.8 10.9 %collective-permute-start.13 = (f32[32,256]{0,1:T(8,128)S(1)}, f32[32,256]{0,1:T(8,128)S(1)}, u32[]{:S(2)}, u32[]{:S(2)}) collective-permute-start(f32[32,256]{0,1:T(8,128)S(1)} %bitcast.157), channel_id=1, source_target_pairs={{0,32},{8,40},{16,48},{24,56},{32,64},{40,72},{48,80},{56,88},{64,... | collective-permute-start | bytes 98312 | tf_op jit(solution)/shard_map/ppermute | solution.py:160
  179.1 11.3 %collective-permute-start.12 = (f32[32,256]{0,1:T(8,128)S(1)}, f32[32,256]{0,1:T(8,128)S(1)}, u32[]{:S(2)}, u32[]{:S(2)}) collective-permute-start(f32[32,256]{0,1:T(8,128)S(1)} %bitcast.158), channel_id=1, source_target_pairs={{0,24},{8,32},{16,40},{24,48},{32,56},{40,64},{48,72},{56,80},{64,... | collective-permute-start | bytes 98312 | tf_op jit(solution)/shard_map/ppermute | solution.py:160
  182.4 8.0 %collective-permute-start.11 = (f32[32,256]{0,1:T(8,128)S(1)}, f32[32,256]{0,1:T(8,128)S(1)}, u32[]{:S(2)}, u32[]{:S(2)}) collective-permute-start(f32[32,256]{0,1:T(8,128)S(1)} %bitcast.159), channel_id=1, source_target_pairs={{0,16},{8,24},{16,32},{24,40},{32,48},{40,56},{48,64},{56,72},{64,... | collective-permute-start | bytes 98312 | tf_op jit(solution)/shard_map/ppermute | solution.py:160
  185.0 5.5 %collective-permute-start.10 = (f32[32,256]{0,1:T(8,128)S(1)}, f32[32,256]{0,1:T(8,128)S(1)}, u32[]{:S(2)}, u32[]{:S(2)}) collective-permute-start(f32[32,256]{0,1:T(8,128)S(1)} %bitcast.160), channel_id=1, source_target_pairs={{0,8},{8,16},{16,24},{24,32},{32,40},{40,48},{48,56},{56,64},{64,7... | collective-permute-start | bytes 98312 | tf_op jit(solution)/shard_map/ppermute | solution.py:160
  188.7 2.8 %copy-start.19 = (f32[512]{0:T(512)S(1)}, f32[512]{0:T(512)}, u32[]{:S(2)}) copy-start(f32[512]{0:T(512)} %param.11) | copy-start | bytes 6148

commit v4 on v3

--- a/solution.py
+++ b/solution.py
@@ -90,6 +90,127 @@
     )(partial)
 
 
+def tok_kernel(src_ref, out_ref, send_sem, recv_sem):
+    n = out_ref.shape[0]
+    chip = lax.axis_index("p")
+    core = lax.axis_index("c")
+    col = lax.axis_index("ch")
+    mesh_id = pl.DeviceIdType.MESH
+    diag = chip == col
+    barrier = pltpu.get_barrier_semaphore()
+    for k in range(n):
+        dest = (col, core, (chip + k) % n)
+        srce = ((chip + k) % n, core, chip)
+        if k == 0:
+            @pl.when(jnp.logical_not(diag))
+            def _():
+                pl.semaphore_signal(barrier, 1, device_id=dest, device_id_type=mesh_id)
+                pl.semaphore_signal(barrier, 1, device_id=srce, device_id_type=mesh_id)
+        else:
+            pl.semaphore_signal(barrier, 1, device_id=dest, device_id_type=mesh_id)
+            pl.semaphore_signal(barrier, 1, device_id=srce, device_id_type=mesh_id)
+    pl.semaphore_wait(barrier, 2 * n - 2 * diag.astype(jnp.int32))
+    copies = []
+    for k in range(n):
+        copy = pltpu.make_async_remote_copy(
+            src_ref=src_ref,
+            dst_ref=out_ref.at[chip],
+            send_sem=send_sem.at[k],
+            recv_sem=recv_sem.at[chip],
+            device_id=(col, core, (chip + k) % n),
+            device_id_type=mesh_id,
+        )
+        if k == 0:
+            own = pltpu.make_async_copy(src_ref, out_ref.at[chip], recv_sem.at[chip])
+
+            @pl.when(diag)
+            def _():
+                own.start()
+
+            @pl.when(jnp.logical_not(diag))
+            def _():
+                copy.start()
+        else:
+            copy.start()
+        copies.append(copy)
+    for j in range(n):
+        pltpu.make_async_copy(src_ref, out_ref.at[j], recv_sem.at[j]).wait()
+    for k in range(n):
+        if k == 0:
+            @pl.when(jnp.logical_not(diag))
+            def _():
+                copies[0].wait_send()
+        else:
+            copies[k].wait_send()
+
+
+def spread_tokens(tokens, n):
+    rows, width = tokens.shape
+    return pl.pallas_call(
+        tok_kernel,
+        out_shape=jax.ShapeDtypeStruct((n, rows, width), tokens.dtype),
+        in_specs=[pl.BlockSpec(memory_space=pltpu.VMEM)],
+        out_specs=pl.BlockSpec(memory_space=pltpu.VMEM),
+        scratch_shapes=[pltpu.SemaphoreType.DMA((n,)), pltpu.SemaphoreType.DMA((n,))],
+        compiler_params=pltpu.CompilerParams(collective_id=1, has_side_effects=True),
+    )(tokens)
+
+
+def state_kernel(src_ref, out_ref, send_sem, recv_sem):
+    n = out_ref.shape[0]
+    n_core = lax.axis_size("c")
+    me = lax.axis_index("p") * n_core + lax.axis_index("c")
+    col = lax.axis_index("ch")
+    mesh_id = pl.DeviceIdType.MESH
+    barrier = pltpu.get_barrier_semaphore()
+    for k in range(1, n):
+        other = (me + k) % n
+        pl.semaphore_signal(
+            barrier, 1, device_id=(other // n_core, other % n_core, col), device_id_type=mesh_id
+        )
+    for j in range(n):
+        @pl.when(j >= me)
+        def _():
+            out_ref[j] = jnp.zeros(out_ref.shape[1:], out_ref.dtype)
+    pl.semaphore_wait(barrier, n - 1)
+    copies = []
+    for k in range(1, n):
+        other = me + k
+        copy = pltpu.make_async_remote_copy(
+            src_ref=src_ref,
+            dst_ref=out_ref.at[me],
+            send_sem=send_sem.at[k],
+            recv_sem=recv_sem.at[me],
+            device_id=(other // n_core, other % n_core, col),
+            device_id_type=mesh_id,
+        )
+
+        @pl.when(other < n)
+        def _():
+            copy.start()
+
+        copies.append((other, copy))
+    for j in range(n):
+        @pl.when(j < me)
+        def _():
+            pltpu.make_async_copy(src_ref, out_ref.at[j], recv_sem.at[j]).wait()
+    for other, copy in copies:
+        @pl.when(other < n)
+        def _():
+            copy.wait_send()
+
+
+def gather_earlier(state, n):
+    return pl.pallas_call(
+        state_kernel,
+        out_shape=jax.ShapeDtypeStruct((n,) + state.shape, state.dtype),
+        in_specs=[pl.BlockSpec(memory_space=pltpu.VMEM)],
+        out_specs=pl.BlockSpec(memory_space=pltpu.VMEM),
+        scratch_shapes=[pltpu.SemaphoreType.DMA((n,)), pltpu.SemaphoreType.DMA((n,))],
+        compiler_params=pltpu.CompilerParams(collective_id=2, has_side_effects=True),
+    )(state)
+
+
 def local(tokens, w_in, short_filter, decay_rate, residue, skip):
     n_chip = lax.axis_size("p")
     block_len = tokens.shape[0]
@@ -100,14 +221,7 @@
     col = lax.axis_index("ch")
 
     n_col = lax.axis_size("ch")
-    pieces = []
-    for k in range(n_col):
-        pairs = [(p * n_col + m, m * n_col + (p + k) % n_col) for p in range(n_chip) for m in range(n_col)]
-        pieces.append(lax.ppermute(tokens, ("p", "ch"), pairs))
-    stacked = jnp.stack(pieces)
-    src = (col - jnp.arange(n_col)) % n_col
-    order = jnp.argsort(src)
-    tok_t = jnp.take(stacked, order, axis=0)
+    tok_t = spread_tokens(tokens, n_col)
     w_flat = w_in.reshape(w_in.shape[0], -1)
     w_other = lax.ppermute(w_flat, "c", [(0, 1), (1, 0)])
     flat_w = jnp.where(
@@ -154,14 +268,11 @@
     n_ctx = n_chip * lax.axis_size("c")
     me = chip * lax.axis_size("c") + core
     s_flat = s_loc.reshape(group_count, -1)
-    s_in = jnp.zeros_like(s_flat)
-    for k in range(1, n_ctx):
-        pairs = [(i, i + k) for i in range(n_ctx - k)]
-        got = lax.ppermute(s_flat, ("p", "c"), pairs)
-        fac = jnp.exp(-decay_rate * (block_len * (k - 1.0)))
-        fac = jnp.where(me >= k, fac, 0.0)
-        s_in = s_in + (fac[:, :, None] * got.reshape(s_loc.shape)).reshape(s_flat.shape)
-    s_in = s_in.reshape(s_loc.shape)
+    s_all = gather_earlier(s_flat, n_ctx).reshape((n_ctx,) + s_loc.shape)
+    gap = (me - 1 - jnp.arange(n_ctx)).astype(jnp.float32)
+    fac = jnp.exp(-decay_rate[None] * (block_len * jnp.maximum(gap, 0.0))[:, None, None])
+    fac = jnp.where(gap[:, None, None] >= 0.0, fac, 0.0)
+    s_in = jnp.sum(fac[..., None] * s_all, axis=0)
     f_mat = pole_weight[:, None, :] * jnp.exp(-lam * (pos + 1.0)[None, :, None])
     far = jnp.einsum("gtr,grc->tgc", f_mat, s_in, precision=HIGH)
     long_out = (near + far).reshape(block_len, local_width)

time: 195 us -> 168 us (0.86)
  starting transfers between devices: 80.5 us -> 1 us
  Pallas kernels: 51.1 us -> 124 us
  waiting for transfers between devices: 12.9 us -> 0.01 us
  local copies, waits for them, and re-layouts: 23.3 us -> 18.8 us
    ppermute x23 -> x0, starting transfers between devices: 70.3 us -> none  [the longest x15 42.4 us: local(): got = lax.ppermute(s_flat, ('p', 'c'), pairs)]
    pallas_call x0 -> x2, Pallas kernels: none -> 54.7 us  [the longest x1 35.2 us: spread_tokens(): pl.pallas_call(tok_kernel, out_shape=jax.ShapeDtypeStruct((n, rows, width...]
    pallas_call x1, Pallas kernels: 51.1 us -> 69.2 us  [ring_reduce_scatter(): pl.pallas_call(rs_kernel, out_shape=jax.ShapeDtypeStruct((rows, width), j...]
    ppermute x23 -> x0, waiting for transfers between devices: 12 us -> none  [the longest x15 9.12 us: local(): got = lax.ppermute(s_flat, ('p', 'c'), pairs)]
    unnamed x51 -> x22, local copies, waits for them, and re-layouts: 9.87 us -> 1.67 us
    ppermute x1, starting transfers between devices: 5.88 us -> 0.97 us  [local(): partner_tail = lax.ppermute(tail, 'c', [(0, 1), (1, 0)])]
    ppermute x1, starting transfers between devices: 4.25 us -> 0.03 us  [local(): w_other = lax.ppermute(w_flat, 'c', [(0, 1), (1, 0)])]
    mul x0 -> x2, local copies, waits for them, and re-layouts: none -> 3.65 us  [local(): s_in = jnp.sum(fac[..., None] * s_all, axis=0)]
  transfers between devices with their start and end apart: 25 -> 2, of which waited for: 5 -> 0; matrix products, arithmetic and copies ran while one was open for 12% -> 7% of each run, Pallas kernels for 0% -> 0%
where the time goes in v4:
time: 168 us; the launch traced here: 167 us
  Pallas kernels  124 us (74%)
  local copies, waits for them, and re-layouts  18.8 us (11%)
  matrix products  17.5 us (10%)
  other arithmetic  5.98 us (4%)
    pallas_call x1, Pallas kernels, ring_reduce_scatter(): pl.pallas_call(rs_kernel, out_shape=jax.ShapeDtypeStruct((rows, width), j...  69.2 us
    pallas_call x1, Pallas kernels, spread_tokens(): pl.pallas_call(tok_kernel, out_shape=jax.ShapeDtypeStruct((n, rows, width...  35.2 us
    pallas_call x1, Pallas kernels, gather_earlier(): pl.pallas_call(state_kernel, out_shape=jax.ShapeDtypeStruct((n,) + state....  19.5 us
    dot_general x1, matrix products, local(): jnp.dot(tok_ext.reshape(n_blk * ext_len, -1), flat_w, preferred_element_t...  10 us
    slice x2, local copies, waits for them, and re-layouts, local(): proj[2:]  3.7 us
    dot_general x1, matrix products, local(): toep = jnp.einsum('gtr,gsr->gts', a_mat, b_mat, precision=HIGH)  3.65 us
    mul x2, local copies, waits for them, and re-layouts, local(): s_in = jnp.sum(fac[..., None] * s_all, axis=0)  3.65 us
  transfers between devices with their start and end apart: 2, of which 0 were waited for; matrix products, arithmetic and copies ran while one was open for 7% of the time, Pallas kernels for 0%

profile of v4, /device:TPU:1, one launch (start us, length us, event | category | flops | bytes accessed | tf_op | source)
XLA Modules:
  0.0 167.3 jit_solution(14942157711704408505)
XLA Ops:
  0.0 0.0 copy-start
  0.0 0.0 copy-start.6
  0.0 0.0 copy-start.4
  0.0 35.2 %shard_map.64 = bf16[8,128,1024]{2,1,0:T(8,128)(2,1)} custom-call(bf16[128,1024]{1,0:T(8,128)(2,1)} %src_ref.1), custom_call_target="tpu_custom_call" | custom-call | tf_op jit(solution)/shard_map/pallas_call | solution.py:149
  35.2 0.0 copy-start.5
  35.2 0.9 slice.43
  36.2 1.0 collective-permute-start
  37.1 0.0 copy-done
  37.1 1.6 copy.32
  38.7 0.0 collective-permute-start.1
  38.7 0.0 copy-done.6
  38.7 0.0 copy-done.4
  38.8 0.5 iota_subtract_fusion
  39.3 0.1 copy.39
  39.3 0.1 copy.38
  39.4 0.1 copy.37
  39.5 0.0 copy-start.2
  39.5 0.6 iota_add_fusion
  40.1 0.6 iota_compare_fusion
  40.7 0.0 copy-done.5
  40.8 0.1 exponential_select_fusion
  40.9 3.7 %fusion.28 = f32[32,128,128]{2,1,0:T(8,128)S(1)} fusion(f32[32,16]{1,0:T(8,128)S(1)} %copy.39, f32[32,16]{1,0:T(8,128)S(1)} %copy.38, f32[32,16]{1,0:T(8,128)S(1)} %copy.37), kind=kOutput, calls=%fused_computation.40 | convolution fusion | flops 100859904 | bytes 2103296 | tf_op jit(solution)/shard_map/gtr,gsr->gts/dot_general | solution.py:261
  44.5 1.5 mul.182
  46.0 0.0 copy-done.2
  46.0 2.2 %copy.42 = f32[16,32,256]{2,1,0:T(8,128)S(1)} copy(f32[16,32,256]{1,2,0:T(8,128)} %bitcast.35) | data formatting | bytes 1048576 | tf_op jit(solution)/shard_map/mul | solution.py:275
  48.2 0.0 collective-permute-done
  48.2 0.1 broadcast_select_fusion
  48.3 0.0 collective-permute-done.1
  48.3 10.0 %fusion.1.part_ref = f32[8,130,1536]{2,1,0:T(8,128)} fusion(bf16[512,1536]{0,1:T(8,128)(2,1)} %collective-permute-done.1, bf16[512,1536]{0,1:T(8,128)(2,1)} %bitcast.1, pred[]{:T(512)S(6)} %eq.11, bf16[8,128,1024]{2,1,0:T(8,128)(2,1)} %shard_map.64, bf16[8,2,1024]{2,1,0:T(2,128)(2,1)S(1)} %broadcast_select_fusion), kind=kOutput, calls=%fused_computation.2 | convolution fusion | flops 3289972736 | bytes 11665409 | tf_op jit(solution)/shard_map/dot_general | solution.py:239
  58.3 69.2 %shard_map.65 = bf16[130,1536]{1,0:T(8,128)(2,1)S(1)} custom-call(f32[8,130,1536]{2,1,0:T(8,128)} %fusion.1.part_ref), custom_call_target="tpu_custom_call" | custom-call | tf_op jit(solution)/shard_map/pallas_call | solution.py:76
  127.5 0.1 fusion.19
  127.6 1.4 fusion.51
  129.0 2.3 %copy.34 = f32[128,1536]{0,1:T(8,128)} copy(f32[128,1536]{1,0:T(8,128)} %get-tuple-element.5) | data formatting | bytes 1572864 | tf_op jit(solution)/shard_map/slice | solution.py:248
  131.3 2.3 %copy.35 = f32[128,1536]{0,1:T(8,128)} copy(f32[128,1536]{1,0:T(8,128)} %get-tuple-element.7) | data formatting | bytes 1572864 | tf_op jit(solution)/shard_map/slice | solution.py:249
  133.6 1.2 copy.36
  134.8 0.0 copy-start.8
  134.8 2.0 %multiply_add_fusion = f32[128,3,512]{0,2,1:T(8,128)S(1)} fusion(f32[128,3,512]{0,2,1:T(8,128)} %bitcast.42, f32[128,3,512]{0,2,1:T(8,128)} %bitcast.41, f32[128,3,512]{0,2,1:T(8,128)} %bitcast.40, f32[3,512]{1,0:T(4,128)S(1)} %get-tuple-element.9, f32[3,512]{1,0:T(4,128)S(1)} %get-tuple-element.10, f32[3,512]{1,0:T(4,128)S(1)} %get-tuple-element.8), kind=kLoop, calls=%fused_computation.24 | loop fusion | flops 983040 | bytes 3164160 | tf_op jit(solution)/shard_map/add | solution.py:248
  136.9 0.0 copy-done.8
  136.9 0.3 fusion.36
  137.2 1.0 convolution_add_fusion.1
  138.2 1.8 %copy.40 = f32[32,16,16]{0,2,1:T(8,128)} copy(f32[32,16,16]{2,1,0:T(8,128)} %convolution_add_fusion.1) | data formatting | bytes 65536 | tf_op jit(solution)/shard_map/add | solution.py:21
  139.9 1.6 copy.41.src_ref
  141.5 19.5 %shard_map.66 = f32[16,32,256]{2,1,0:T(8,128)} custom-call(f32[32,256]{1,0:T(8,128)} %copy.41.src_ref), custom_call_target="tpu_custom_call" | custom-call | tf_op jit(solution)/shard_map/pallas_call | solution.py:204
  161.0 1.7 %multiply_reduce_fusion = f32[32,256]{1,0:T(8,128)} fusion(f32[16,32,256]{2,1,0:T(8,128)S(1)} %copy.42, f32[16,32,256]{2,1,0:T(8,128)} %shard_map.66), kind=kLoop, calls=%fused_computation.25 | loop fusion | flops 253952 | bytes 1081344 | tf_op jit(solution)/shard_map/reduce_sum | solution.py:275
  162.7 0.0 copy-start.1
  162.7 0.9 copy.43
  163.6 0.2 copy.44
  163.8 0.0 copy-start.3
  163.8 0.0 copy-start.9
  163.8 1.4 fusion.14
  165.2 0.0 copy-done.1
  165.2 0.0 copy-start.7
  165.2 0.7 fusion.13
  165.8 0.0 copy-done.3
  165.8 0.0 copy-done.9
  165.9 0.5 convolution_add_fusion
  166.4 0.0 copy-done.7
  166.4 0.1 fusion.22
  166.5 0.8 copy.45
  (7 shorter events, 0.1 us)
Async XLA Ops:
  0.0 37.1 %copy-start = (bf16[512,3,512]{2,0,1:T(8,128)(2,1)S(1)}, bf16[512,3,512]{2,0,1:T(8,128)(2,1)}, u32[]{:S(2)}) copy-start(bf16[512,3,512]{2,0,1:T(8,128)(2,1)} %param.7) | copy-start | bytes 4718596
  0.0 38.7 %copy-start.6 = (f32[32,16]{0,1:T(8,128)S(1)}, f32[32,16]{0,1:T(8,128)}, u32[]{:S(2)}) copy-start(f32[32,16]{0,1:T(8,128)} %param.10) | copy-start | bytes 6148
  0.0 38.7 %copy-start.4 = (f32[32,16]{0,1:T(8,128)S(1)}, f32[32,16]{0,1:T(8,128)}, u32[]{:S(2)}) copy-start(f32[32,16]{0,1:T(8,128)} %param.9) | copy-start | bytes 6148
  35.2 5.5 %copy-start.5 = (f32[3,3,512]{2,1,0:T(4,128)S(1)}, f32[3,3,512]{2,1,0:T(4,128)}, u32[]{:S(2)}) copy-start(f32[3,3,512]{2,1,0:T(4,128)} %param.8) | copy-start | bytes 55300
  36.2 12.0 %collective-permute-start = (bf16[8,2,1024]{2,1,0:T(2,128)(2,1)S(1)}, bf16[8,2,1024]{2,1,0:T(2,128)(2,1)S(1)}, u32[]{:S(2)}, u32[]{:S(2)}) collective-permute-start(bf16[8,2,1024]{2,1,0:T(2,128)(2,1)S(1)} %slice.43), channel_id=1, source_target_pairs={{0,8},{8,0},{1,9},{9,1},{2,10},{10,2},{3,11},{11,3},{4,12},{12,4},... | collective-permute-start | bytes 98312 | tf_op jit(solution)/shard_map/ppermute | solution.py:234
  38.7 9.6 %collective-permute-start.1 = (bf16[512,1536]{0,1:T(8,128)(2,1)}, bf16[512,1536]{0,1:T(8,128)(2,1)}, u32[]{:S(2)}, u32[]{:S(2)}) collective-permute-start(bf16[512,1536]{0,1:T(8,128)(2,1)} %bitcast.1), channel_id=1, source_target_pairs={{0,8},{8,0},{1,9},{9,1},{2,10},{10,2},{3,11},{11,3},{4,12},{12,4},... | collective-permute-start | bytes 4718600 | tf_op jit(solution)/shard_map/ppermute | solution.py:226
  39.5 6.5 %copy-start.2 = (f32[32,16]{1,0:T(8,128)}, f32[32,16]{1,0:T(8,128)S(1)}, u32[]{:S(2)}) copy-start(f32[32,16]{1,0:T(8,128)S(1)} %copy.37) | copy-start | bytes 6148
  134.8 2.1 %copy-start.8 = (f32[128]{0:T(128)S(1)}, f32[128]{0:T(128)}, u32[]{:S(2)}) copy-start(f32[128]{0:T(128)} %iota_subtract_fusion) | copy-start | bytes 1540
  162.7 2.4 %copy-start.1 = (pred[128,128]{1,0:T(8,128)(4,1)S(1)}, pred[128,128]{1,0:T(8,128)(4,1)}, u32[]{:S(2)}) copy-start(pred[128,128]{1,0:T(8,128)(4,1)} %iota_compare_fusion) | copy-start | bytes 49156
  163.8 2.0 %copy-start.3 = (f32[32,16]{1,0:T(8,128)S(1)}, f32[32,16]{1,0:T(8,128)}, u32[]{:S(2)}) copy-start(f32[32,16]{1,0:T(8,128)} %copy-done.2) | copy-start | bytes 6148
  163.8 2.0 %copy-start.9 = (f32[128]{0:T(128)S(1)}, f32[128]{0:T(128)}, u32[]{:S(2)}) copy-start(f32[128]{0:T(128)} %iota_add_fusion) | copy-start | bytes 1540
  165.2 1.2 copy-start.7

commit v5 on v4

--- a/solution.py
+++ b/solution.py
@@ -34,41 +34,50 @@
 
 
 def rs_kernel(part_ref, out_ref, sbuf, rbuf, send_sem, recv_sem):
-    n = part_ref.shape[0]
+    n, _, width = part_ref.shape
+    half = width // 2
     chip = lax.axis_index("p")
     core = lax.axis_index("c")
     col = lax.axis_index("ch")
     r = ring_pos(chip, n)
-    d = 1 - 2 * core
-    nxt = ring_chip((r + d + n) % n, n)
-    prv = ring_chip((r - d + n) % n, n)
+    nxt = ring_chip((r + 1) % n, n)
+    prv = ring_chip((r - 1 + n) % n, n)
     mesh_id = pl.DeviceIdType.MESH
     barrier = pltpu.get_barrier_semaphore()
     for nb in (nxt, prv):
         pl.semaphore_signal(barrier, 1, device_id=(nb, core, col), device_id_type=mesh_id)
     pl.semaphore_wait(barrier, 2)
-    copies = []
+    copies = [[], []]
     for s in range(n - 1):
-        q = ring_chip((r - d * (1 + s) + 2 * n) % n, n)
-        if s == 0:
-            sbuf[0] = part_ref[q].astype(sbuf.dtype)
-        else:
-            copies[s - 1].wait_recv()
-            sbuf[s] = (rbuf[s - 1].astype(jnp.float32) + part_ref[q]).astype(sbuf.dtype)
-        copy = pltpu.make_async_remote_copy(
-            src_ref=sbuf.at[s],
-            dst_ref=rbuf.at[s],
-            send_sem=send_sem.at[s],
-            recv_sem=recv_sem.at[s],
-            device_id=(nxt, core, col),
-            device_id_type=mesh_id,
+        for h, (d, dest) in enumerate(((1, nxt), (-1, prv))):
+            cols = pl.ds(h * half, half)
+            q = ring_chip((r - d * (1 + s) + 2 * n) % n, n)
+            if s == 0:
+                sbuf[h, 0] = part_ref[q, :, cols].astype(sbuf.dtype)
+            else:
+                copies[h][s - 1].wait_recv()
+                sbuf[h, s] = (rbuf[h, s - 1].astype(jnp.float32) + part_ref[q, :, cols]).astype(
+                    sbuf.dtype
+                )
+            copy = pltpu.make_async_remote_copy(
+                src_ref=sbuf.at[h, s],
+                dst_ref=rbuf.at[h, s],
+                send_sem=send_sem.at[h, s],
+                recv_sem=recv_sem.at[h, s],
+                device_id=(dest, core, col),
+                device_id_type=mesh_id,
+            )
+            copy.start()
+            copies[h].append(copy)
+    for h in range(2):
+        cols = pl.ds(h * half, half)
+        copies[h][-1].wait_recv()
+        out_ref[:, cols] = (rbuf[h, n - 2].astype(jnp.float32) + part_ref[chip, :, cols]).astype(
+            out_ref.dtype
         )
-        copy.start()
-        copies.append(copy)
-    copies[-1].wait_recv()
-    out_ref[...] = (rbuf[n - 2].astype(jnp.float32) + part_ref[chip]).astype(out_ref.dtype)
-    for copy in copies:
-        copy.wait_send()
+    for h in range(2):
+        for copy in copies[h]:
+            copy.wait_send()
 
 
 def ring_reduce_scatter(partial):
@@ -79,10 +88,10 @@
         in_specs=[pl.BlockSpec(memory_space=pltpu.VMEM)],
         out_specs=pl.BlockSpec(memory_space=pltpu.VMEM),
         scratch_shapes=[
-            pltpu.VMEM((n - 1, rows, width), jnp.bfloat16),
-            pltpu.VMEM((n - 1, rows, width), jnp.bfloat16),
-            pltpu.SemaphoreType.DMA((n - 1,)),
-            pltpu.SemaphoreType.DMA((n - 1,)),
+            pltpu.VMEM((2, n - 1, rows, width // 2), jnp.bfloat16),
+            pltpu.VMEM((2, n - 1, rows, width // 2), jnp.bfloat16),
+            pltpu.SemaphoreType.DMA((2, n - 1)),
+            pltpu.SemaphoreType.DMA((2, n - 1)),
         ],
         compiler_params=pltpu.CompilerParams(
             collective_id=0, has_side_effects=True, vmem_limit_bytes=48 * 1024 * 1024

time: 168 us -> 161 us (0.958)
  Pallas kernels: 124 us -> 117 us
    pallas_call x1, Pallas kernels: 19.5 us -> 15.6 us  [gather_earlier(): pl.pallas_call(state_kernel, out_shape=jax.ShapeDtypeStruct((n,) + state....]
    pallas_call x1, Pallas kernels: 69.2 us -> 66.3 us  [ring_reduce_scatter(): pl.pallas_call(rs_kernel, out_shape=jax.ShapeDtypeStruct((rows, width), j...]
where the time goes in v5:
time: 161 us
  Pallas kernels  117 us (73%)
  local copies, waits for them, and re-layouts  18.8 us (12%)
  matrix products  17.5 us (11%)
  other arithmetic  5.98 us (4%)
    pallas_call x1, Pallas kernels, ring_reduce_scatter(): pl.pallas_call(rs_kernel, out_shape=jax.ShapeDtypeStruct((rows, width), j...  66.3 us
    pallas_call x1, Pallas kernels, spread_tokens(): pl.pallas_call(tok_kernel, out_shape=jax.ShapeDtypeStruct((n, rows, width...  35.2 us
    pallas_call x1, Pallas kernels, gather_earlier(): pl.pallas_call(state_kernel, out_shape=jax.ShapeDtypeStruct((n,) + state....  15.6 us
    dot_general x1, matrix products, local(): jnp.dot(tok_ext.reshape(n_blk * ext_len, -1), flat_w, preferred_element_t...  10 us
    slice x2, local copies, waits for them, and re-layouts, local(): proj[2:]  3.7 us
    dot_general x1, matrix products, local(): toep = jnp.einsum('gtr,gsr->gts', a_mat, b_mat, precision=HIGH)  3.65 us
    mul x2, local copies, waits for them, and re-layouts, local(): s_in = jnp.sum(fac[..., None] * s_all, axis=0)  3.65 us
  transfers between devices with their start and end apart: 2, of which 0 were waited for; matrix products, arithmetic and copies ran while one was open for 7% of the time, Pallas kernels for 0%

profile of v5, /device:TPU:1, one launch (start us, length us, event | category | flops | bytes accessed | tf_op | source)
XLA Modules:
  0.0 160.6 jit_solution(12104728617310000931)
XLA Ops:
  0.0 0.0 copy-start
  0.0 0.0 copy-start.6
  0.0 0.0 copy-start.4
  0.0 35.2 %shard_map.64 = bf16[8,128,1024]{2,1,0:T(8,128)(2,1)} custom-call(bf16[128,1024]{1,0:T(8,128)(2,1)} %src_ref.1), custom_call_target="tpu_custom_call" | custom-call | tf_op jit(solution)/shard_map/pallas_call | solution.py:158
  35.2 0.0 copy-start.5
  35.2 0.9 slice.43
  36.2 1.0 collective-permute-start
  37.1 0.0 copy-done
  37.1 1.6 copy.32
  38.7 0.0 collective-permute-start.1
  38.7 0.0 copy-done.6
  38.7 0.0 copy-done.4
  38.8 0.5 iota_subtract_fusion
  39.3 0.1 copy.39
  39.3 0.1 copy.38
  39.4 0.1 copy.37
  39.5 0.0 copy-start.2
  39.5 0.6 iota_add_fusion
  40.1 0.6 iota_compare_fusion
  40.7 0.0 copy-done.5
  40.8 0.1 exponential_select_fusion
  40.9 3.7 %fusion.28 = f32[32,128,128]{2,1,0:T(8,128)S(1)} fusion(f32[32,16]{1,0:T(8,128)S(1)} %copy.39, f32[32,16]{1,0:T(8,128)S(1)} %copy.38, f32[32,16]{1,0:T(8,128)S(1)} %copy.37), kind=kOutput, calls=%fused_computation.40 | convolution fusion | flops 100859904 | bytes 2103296 | tf_op jit(solution)/shard_map/gtr,gsr->gts/dot_general | solution.py:270
  44.5 1.5 mul.182
  46.0 0.0 copy-done.2
  46.0 2.2 %copy.42 = f32[16,32,256]{2,1,0:T(8,128)S(1)} copy(f32[16,32,256]{1,2,0:T(8,128)} %bitcast.35) | data formatting | bytes 1048576 | tf_op jit(solution)/shard_map/mul | solution.py:284
  48.2 0.0 collective-permute-done
  48.2 0.1 broadcast_select_fusion
  48.3 0.0 collective-permute-done.1
  48.3 10.0 %fusion.1.part_ref = f32[8,130,1536]{2,1,0:T(8,128)} fusion(bf16[512,1536]{0,1:T(8,128)(2,1)} %collective-permute-done.1, bf16[512,1536]{0,1:T(8,128)(2,1)} %bitcast.1, pred[]{:T(512)S(6)} %eq.11, bf16[8,128,1024]{2,1,0:T(8,128)(2,1)} %shard_map.64, bf16[8,2,1024]{2,1,0:T(2,128)(2,1)S(1)} %broadcast_select_fusion), kind=kOutput, calls=%fused_computation.2 | convolution fusion | flops 3289972736 | bytes 11665409 | tf_op jit(solution)/shard_map/dot_general | solution.py:248
  58.3 66.3 %shard_map.65 = bf16[130,1536]{1,0:T(8,128)(2,1)S(1)} custom-call(f32[8,130,1536]{2,1,0:T(8,128)} %fusion.1.part_ref), custom_call_target="tpu_custom_call" | custom-call | tf_op jit(solution)/shard_map/pallas_call | solution.py:85
  124.6 0.1 fusion.19
  124.7 1.4 fusion.51
  126.2 2.3 %copy.34 = f32[128,1536]{0,1:T(8,128)} copy(f32[128,1536]{1,0:T(8,128)} %get-tuple-element.5) | data formatting | bytes 1572864 | tf_op jit(solution)/shard_map/slice | solution.py:257
  128.4 2.3 %copy.35 = f32[128,1536]{0,1:T(8,128)} copy(f32[128,1536]{1,0:T(8,128)} %get-tuple-element.7) | data formatting | bytes 1572864 | tf_op jit(solution)/shard_map/slice | solution.py:258
  130.7 1.2 copy.36
  131.9 0.0 copy-start.8
  131.9 2.0 %multiply_add_fusion = f32[128,3,512]{0,2,1:T(8,128)S(1)} fusion(f32[128,3,512]{0,2,1:T(8,128)} %bitcast.42, f32[128,3,512]{0,2,1:T(8,128)} %bitcast.41, f32[128,3,512]{0,2,1:T(8,128)} %bitcast.40, f32[3,512]{1,0:T(4,128)S(1)} %get-tuple-element.9, f32[3,512]{1,0:T(4,128)S(1)} %get-tuple-element.10, f32[3,512]{1,0:T(4,128)S(1)} %get-tuple-element.8), kind=kLoop, calls=%fused_computation.24 | loop fusion | flops 983040 | bytes 3164160 | tf_op jit(solution)/shard_map/add | solution.py:257
  134.0 0.0 copy-done.8
  134.0 0.3 fusion.36
  134.3 1.0 convolution_add_fusion.1
  135.3 1.8 %copy.40 = f32[32,16,16]{0,2,1:T(8,128)} copy(f32[32,16,16]{2,1,0:T(8,128)} %convolution_add_fusion.1) | data formatting | bytes 65536 | tf_op jit(solution)/shard_map/add | solution.py:21
  137.0 1.6 copy.41.src_ref
  138.6 15.6 %shard_map.66 = f32[16,32,256]{2,1,0:T(8,128)} custom-call(f32[32,256]{1,0:T(8,128)} %copy.41.src_ref), custom_call_target="tpu_custom_call" | custom-call | tf_op jit(solution)/shard_map/pallas_call | solution.py:213
  154.3 1.7 %multiply_reduce_fusion = f32[32,256]{1,0:T(8,128)} fusion(f32[16,32,256]{2,1,0:T(8,128)S(1)} %copy.42, f32[16,32,256]{2,1,0:T(8,128)} %shard_map.66), kind=kLoop, calls=%fused_computation.25 | loop fusion | flops 253952 | bytes 1081344 | tf_op jit(solution)/shard_map/reduce_sum | solution.py:284
  156.0 0.0 copy-start.1
  156.0 0.9 copy.43
  156.9 0.2 copy.44
  157.0 0.0 copy-start.3
  157.0 0.0 copy-start.9
  157.1 1.4 fusion.14
  158.4 0.0 copy-done.1
  158.4 0.0 copy-start.7
  158.4 0.7 fusion.13
  159.1 0.0 copy-done.3
  159.1 0.0 copy-done.9
  159.1 0.5 convolution_add_fusion
  159.6 0.0 copy-done.7
  159.6 0.1 fusion.22
  159.8 0.8 copy.45
  (7 shorter events, 0.1 us)
Async XLA Ops:
  0.0 37.1 %copy-start = (bf16[512,3,512]{2,0,1:T(8,128)(2,1)S(1)}, bf16[512,3,512]{2,0,1:T(8,128)(2,1)}, u32[]{:S(2)}) copy-start(bf16[512,3,512]{2,0,1:T(8,128)(2,1)} %param.7) | copy-start | bytes 4718596
  0.0 38.7 %copy-start.6 = (f32[32,16]{0,1:T(8,128)S(1)}, f32[32,16]{0,1:T(8,128)}, u32[]{:S(2)}) copy-start(f32[32,16]{0,1:T(8,128)} %param.10) | copy-start | bytes 6148
  0.0 38.7 %copy-start.4 = (f32[32,16]{0,1:T(8,128)S(1)}, f32[32,16]{0,1:T(8,128)}, u32[]{:S(2)}) copy-start(f32[32,16]{0,1:T(8,128)} %param.9) | copy-start | bytes 6148
  35.2 5.5 %copy-start.5 = (f32[3,3,512]{2,1,0:T(4,128)S(1)}, f32[3,3,512]{2,1,0:T(4,128)}, u32[]{:S(2)}) copy-start(f32[3,3,512]{2,1,0:T(4,128)} %param.8) | copy-start | bytes 55300
  36.2 12.0 %collective-permute-start = (bf16[8,2,1024]{2,1,0:T(2,128)(2,1)S(1)}, bf16[8,2,1024]{2,1,0:T(2,128)(2,1)S(1)}, u32[]{:S(2)}, u32[]{:S(2)}) collective-permute-start(bf16[8,2,1024]{2,1,0:T(2,128)(2,1)S(1)} %slice.43), channel_id=1, source_target_pairs={{0,8},{8,0},{1,9},{9,1},{2,10},{10,2},{3,11},{11,3},{4,12},{12,4},... | collective-permute-start | bytes 98312 | tf_op jit(solution)/shard_map/ppermute | solution.py:243
  38.7 9.6 %collective-permute-start.1 = (bf16[512,1536]{0,1:T(8,128)(2,1)}, bf16[512,1536]{0,1:T(8,128)(2,1)}, u32[]{:S(2)}, u32[]{:S(2)}) collective-permute-start(bf16[512,1536]{0,1:T(8,128)(2,1)} %bitcast.1), channel_id=1, source_target_pairs={{0,8},{8,0},{1,9},{9,1},{2,10},{10,2},{3,11},{11,3},{4,12},{12,4},... | collective-permute-start | bytes 4718600 | tf_op jit(solution)/shard_map/ppermute | solution.py:235
  39.5 6.5 %copy-start.2 = (f32[32,16]{1,0:T(8,128)}, f32[32,16]{1,0:T(8,128)S(1)}, u32[]{:S(2)}) copy-start(f32[32,16]{1,0:T(8,128)S(1)} %copy.37) | copy-start | bytes 6148
  131.9 2.1 %copy-start.8 = (f32[128]{0:T(128)S(1)}, f32[128]{0:T(128)}, u32[]{:S(2)}) copy-start(f32[128]{0:T(128)} %iota_subtract_fusion) | copy-start | bytes 1540
  156.0 2.4 %copy-start.1 = (pred[128,128]{1,0:T(8,128)(4,1)S(1)}, pred[128,128]{1,0:T(8,128)(4,1)}, u32[]{:S(2)}) copy-start(pred[128,128]{1,0:T(8,128)(4,1)} %iota_compare_fusion) | copy-start | bytes 49156
  157.0 2.0 %copy-start.3 = (f32[32,16]{1,0:T(8,128)S(1)}, f32[32,16]{1,0:T(8,128)}, u32[]{:S(2)}) copy-start(f32[32,16]{1,0:T(8,128)} %copy-done.2) | copy-start | bytes 6148
  157.0 2.0 %copy-start.9 = (f32[128]{0:T(128)S(1)}, f32[128]{0:T(128)}, u32[]{:S(2)}) copy-start(f32[128]{0:T(128)} %iota_add_fusion) | copy-start | bytes 1540
  158.4 1.2 copy-start.7

commit v6 on v5

--- a/solution.py
+++ b/solution.py
@@ -35,7 +35,8 @@
 
 def rs_kernel(part_ref, out_ref, sbuf, rbuf, send_sem, recv_sem):
     n, _, width = part_ref.shape
-    half = width // 2
+    n_ring = sbuf.shape[0]
+    chunk = width // n_ring
     chip = lax.axis_index("p")
     core = lax.axis_index("c")
     col = lax.axis_index("ch")
@@ -47,40 +48,42 @@
     for nb in (nxt, prv):
         pl.semaphore_signal(barrier, 1, device_id=(nb, core, col), device_id_type=mesh_id)
     pl.semaphore_wait(barrier, 2)
-    copies = [[], []]
+    copies = [[] for _ in range(n_ring)]
+    order = [h * (n_ring // 2) + k for k in range(n_ring // 2) for h in range(2)]
     for s in range(n - 1):
-        for h, (d, dest) in enumerate(((1, nxt), (-1, prv))):
-            cols = pl.ds(h * half, half)
+        for ring in order:
+            d, dest = (1, nxt) if ring < n_ring // 2 else (-1, prv)
+            cols = pl.ds(ring * chunk, chunk)
             q = ring_chip((r - d * (1 + s) + 2 * n) % n, n)
             if s == 0:
-                sbuf[h, 0] = part_ref[q, :, cols].astype(sbuf.dtype)
+                sbuf[ring, 0] = part_ref[q, :, cols].astype(sbuf.dtype)
             else:
-                copies[h][s - 1].wait_recv()
-                sbuf[h, s] = (rbuf[h, s - 1].astype(jnp.float32) + part_ref[q, :, cols]).astype(
-                    sbuf.dtype
-                )
+                copies[ring][s - 1].wait_recv()
+                sbuf[ring, s] = (
+                    rbuf[ring, s - 1].astype(jnp.float32) + part_ref[q, :, cols]
+                ).astype(sbuf.dtype)
             copy = pltpu.make_async_remote_copy(
-                src_ref=sbuf.at[h, s],
-                dst_ref=rbuf.at[h, s],
-                send_sem=send_sem.at[h, s],
-                recv_sem=recv_sem.at[h, s],
+                src_ref=sbuf.at[ring, s],
+                dst_ref=rbuf.at[ring, s],
+                send_sem=send_sem.at[ring, s],
+                recv_sem=recv_sem.at[ring, s],
                 device_id=(dest, core, col),
                 device_id_type=mesh_id,
             )
             copy.start()
-            copies[h].append(copy)
-    for h in range(2):
-        cols = pl.ds(h * half, half)
-        copies[h][-1].wait_recv()
-        out_ref[:, cols] = (rbuf[h, n - 2].astype(jnp.float32) + part_ref[chip, :, cols]).astype(
-            out_ref.dtype
-        )
-    for h in range(2):
-        for copy in copies[h]:
+            copies[ring].append(copy)
+    for ring in order:
+        cols = pl.ds(ring * chunk, chunk)
+        copies[ring][-1].wait_recv()
+        out_ref[:, cols] = (
+            rbuf[ring, n - 2].astype(jnp.float32) + part_ref[chip, :, cols]
+        ).astype(out_ref.dtype)
+    for ring in order:
+        for copy in copies[ring]:
             copy.wait_send()
 
 
-def ring_reduce_scatter(partial):
+def ring_reduce_scatter(partial, n_ring=6):
     n, rows, width = partial.shape
     return pl.pallas_call(
         rs_kernel,
@@ -88,10 +91,10 @@
         in_specs=[pl.BlockSpec(memory_space=pltpu.VMEM)],
         out_specs=pl.BlockSpec(memory_space=pltpu.VMEM),
         scratch_shapes=[
-            pltpu.VMEM((2, n - 1, rows, width // 2), jnp.bfloat16),
-            pltpu.VMEM((2, n - 1, rows, width // 2), jnp.bfloat16),
-            pltpu.SemaphoreType.DMA((2, n - 1)),
-            pltpu.SemaphoreType.DMA((2, n - 1)),
+            pltpu.VMEM((n_ring, n - 1, rows, width // n_ring), jnp.bfloat16),
+            pltpu.VMEM((n_ring, n - 1, rows, width // n_ring), jnp.bfloat16),
+            pltpu.SemaphoreType.DMA((n_ring, n - 1)),
+            pltpu.SemaphoreType.DMA((n_ring, n - 1)),
         ],
         compiler_params=pltpu.CompilerParams(
             collective_id=0, has_side_effects=True, vmem_limit_bytes=48 * 1024 * 1024

time: 161 us -> 153 us (0.950)
  Pallas kernels: 117 us -> 109 us
    pallas_call x1, Pallas kernels: 66.3 us -> 60.7 us  [ring_reduce_scatter(): pl.pallas_call(rs_kernel, out_shape=jax.ShapeDtypeStruct((rows, width), j...]
    pallas_call x1, Pallas kernels: 15.6 us -> 13 us  [gather_earlier(): pl.pallas_call(state_kernel, out_shape=jax.ShapeDtypeStruct((n,) + state....]
where the time goes in v6:
time: 153 us; the launch traced here: 152 us
  Pallas kernels  109 us (71%)
  local copies, waits for them, and re-layouts  18.8 us (12%)
  matrix products  17.5 us (11%)
  other arithmetic  5.98 us (4%)
    pallas_call x1, Pallas kernels, ring_reduce_scatter(): pl.pallas_call(rs_kernel, out_shape=jax.ShapeDtypeStruct((rows, width), j...  60.7 us
    pallas_call x1, Pallas kernels, spread_tokens(): pl.pallas_call(tok_kernel, out_shape=jax.ShapeDtypeStruct((n, rows, width...  35.2 us
    pallas_call x1, Pallas kernels, gather_earlier(): pl.pallas_call(state_kernel, out_shape=jax.ShapeDtypeStruct((n,) + state....  13 us
    dot_general x1, matrix products, local(): jnp.dot(tok_ext.reshape(n_blk * ext_len, -1), flat_w, preferred_element_t...  10 us
    slice x2, local copies, waits for them, and re-layouts, local(): proj[2:]  3.7 us
    dot_general x1, matrix products, local(): toep = jnp.einsum('gtr,gsr->gts', a_mat, b_mat, precision=HIGH)  3.65 us
    mul x2, local copies, waits for them, and re-layouts, local(): s_in = jnp.sum(fac[..., None] * s_all, axis=0)  3.65 us
  transfers between devices with their start and end apart: 2, of which 0 were waited for; matrix products, arithmetic and copies ran while one was open for 7% of the time, Pallas kernels for 0%

profile of v6, /device:TPU:1, one launch (start us, length us, event | category | flops | bytes accessed | tf_op | source)
XLA Modules:
  0.0 152.3 jit_solution(7484273305653339748)
XLA Ops:
  0.0 0.0 copy-start
  0.0 0.0 copy-start.6
  0.0 0.0 copy-start.4
  0.0 35.2 %shard_map.64 = bf16[8,128,1024]{2,1,0:T(8,128)(2,1)} custom-call(bf16[128,1024]{1,0:T(8,128)(2,1)} %src_ref.1), custom_call_target="tpu_custom_call" | custom-call | tf_op jit(solution)/shard_map/pallas_call | solution.py:161
  35.2 0.0 copy-start.5
  35.2 0.9 slice.43
  36.2 1.0 collective-permute-start
  37.1 0.0 copy-done
  37.1 1.6 %copy.32 = bf16[512,3,512]{0,2,1:T(8,128)(2,1)} copy(bf16[512,3,512]{2,0,1:T(8,128)(2,1)S(1)} %copy-done) | data formatting | bytes 3145728 | tf_op args[1]
  38.7 0.0 collective-permute-start.1
  38.7 0.0 copy-done.6
  38.7 0.0 copy-done.4
  38.8 0.5 iota_subtract_fusion
  39.3 0.1 copy.39
  39.3 0.1 copy.38
  39.4 0.1 copy.37
  39.5 0.0 copy-start.2
  39.5 0.6 iota_add_fusion
  40.1 0.6 iota_compare_fusion
  40.7 0.0 copy-done.5
  40.8 0.1 exponential_select_fusion
  40.9 3.7 %fusion.28 = f32[32,128,128]{2,1,0:T(8,128)S(1)} fusion(f32[32,16]{1,0:T(8,128)S(1)} %copy.39, f32[32,16]{1,0:T(8,128)S(1)} %copy.38, f32[32,16]{1,0:T(8,128)S(1)} %copy.37), kind=kOutput, calls=%fused_computation.40 | convolution fusion | flops 100859904 | bytes 2103296 | tf_op jit(solution)/shard_map/gtr,gsr->gts/dot_general | solution.py:273
  44.5 1.5 mul.182
  46.0 0.0 copy-done.2
  46.0 2.2 %copy.42 = f32[16,32,256]{2,1,0:T(8,128)S(1)} copy(f32[16,32,256]{1,2,0:T(8,128)} %bitcast.35) | data formatting | bytes 1048576 | tf_op jit(solution)/shard_map/mul | solution.py:287
  48.2 0.0 collective-permute-done
  48.2 0.1 broadcast_select_fusion
  48.3 0.0 collective-permute-done.1
  48.3 10.0 %fusion.1.part_ref = f32[8,130,1536]{2,1,0:T(8,128)} fusion(bf16[512,1536]{0,1:T(8,128)(2,1)} %collective-permute-done.1, bf16[512,1536]{0,1:T(8,128)(2,1)} %bitcast.1, pred[]{:T(512)S(6)} %eq.11, bf16[8,128,1024]{2,1,0:T(8,128)(2,1)} %shard_map.64, bf16[8,2,1024]{2,1,0:T(2,128)(2,1)S(1)} %broadcast_select_fusion), kind=kOutput, calls=%fused_computation.2 | convolution fusion | flops 3289972736 | bytes 11665409 | tf_op jit(solution)/shard_map/dot_general | solution.py:251
  58.3 60.7 %shard_map.65 = bf16[130,1536]{1,0:T(8,128)(2,1)S(1)} custom-call(f32[8,130,1536]{2,1,0:T(8,128)} %fusion.1.part_ref), custom_call_target="tpu_custom_call" | custom-call | tf_op jit(solution)/shard_map/pallas_call | solution.py:88
  119.0 0.1 fusion.19
  119.1 1.4 fusion.51
  120.5 2.3 %copy.34 = f32[128,1536]{0,1:T(8,128)} copy(f32[128,1536]{1,0:T(8,128)} %get-tuple-element.5) | data formatting | bytes 1572864 | tf_op jit(solution)/shard_map/slice | solution.py:260
  122.8 2.3 %copy.35 = f32[128,1536]{0,1:T(8,128)} copy(f32[128,1536]{1,0:T(8,128)} %get-tuple-element.7) | data formatting | bytes 1572864 | tf_op jit(solution)/shard_map/slice | solution.py:261
  125.1 1.2 copy.36
  126.3 0.0 copy-start.8
  126.3 2.0 %multiply_add_fusion = f32[128,3,512]{0,2,1:T(8,128)S(1)} fusion(f32[128,3,512]{0,2,1:T(8,128)} %bitcast.42, f32[128,3,512]{0,2,1:T(8,128)} %bitcast.41, f32[128,3,512]{0,2,1:T(8,128)} %bitcast.40, f32[3,512]{1,0:T(4,128)S(1)} %get-tuple-element.9, f32[3,512]{1,0:T(4,128)S(1)} %get-tuple-element.10, f32[3,512]{1,0:T(4,128)S(1)} %get-tuple-element.8), kind=kLoop, calls=%fused_computation.24 | loop fusion | flops 983040 | bytes 3164160 | tf_op jit(solution)/shard_map/add | solution.py:260
  128.4 0.0 copy-done.8
  128.4 0.3 fusion.36
  128.7 1.0 convolution_add_fusion.1
  129.7 1.8 %copy.40 = f32[32,16,16]{0,2,1:T(8,128)} copy(f32[32,16,16]{2,1,0:T(8,128)} %convolution_add_fusion.1) | data formatting | bytes 65536 | tf_op jit(solution)/shard_map/add | solution.py:21
  131.4 1.6 %copy.41.src_ref = f32[32,256]{1,0:T(8,128)} copy(f32[32,256]{0,1:T(8,128)} %bitcast.43) | data formatting | bytes 65536 | tf_op jit(solution)/shard_map/reshape | solution.py:282
  133.0 13.0 %shard_map.66 = f32[16,32,256]{2,1,0:T(8,128)} custom-call(f32[32,256]{1,0:T(8,128)} %copy.41.src_ref), custom_call_target="tpu_custom_call" | custom-call | tf_op jit(solution)/shard_map/pallas_call | solution.py:216
  146.0 1.7 %multiply_reduce_fusion = f32[32,256]{1,0:T(8,128)} fusion(f32[16,32,256]{2,1,0:T(8,128)S(1)} %copy.42, f32[16,32,256]{2,1,0:T(8,128)} %shard_map.66), kind=kLoop, calls=%fused_computation.25 | loop fusion | flops 253952 | bytes 1081344 | tf_op jit(solution)/shard_map/reduce_sum | solution.py:287
  147.7 0.0 copy-start.1
  147.7 0.9 copy.43
  148.6 0.2 copy.44
  148.8 0.0 copy-start.3
  148.8 0.0 copy-start.9
  148.8 1.4 fusion.14
  150.2 0.0 copy-done.1
  150.2 0.0 copy-start.7
  150.2 0.7 fusion.13
  150.8 0.0 copy-done.3
  150.8 0.0 copy-done.9
  150.8 0.5 convolution_add_fusion
  151.4 0.0 copy-done.7
  151.4 0.1 fusion.22
  151.5 0.8 copy.45
  (7 shorter events, 0.1 us)
Async XLA Ops:
  0.0 37.1 %copy-start = (bf16[512,3,512]{2,0,1:T(8,128)(2,1)S(1)}, bf16[512,3,512]{2,0,1:T(8,128)(2,1)}, u32[]{:S(2)}) copy-start(bf16[512,3,512]{2,0,1:T(8,128)(2,1)} %param.7) | copy-start | bytes 4718596
  0.0 38.7 %copy-start.6 = (f32[32,16]{0,1:T(8,128)S(1)}, f32[32,16]{0,1:T(8,128)}, u32[]{:S(2)}) copy-start(f32[32,16]{0,1:T(8,128)} %param.10) | copy-start | bytes 6148
  0.0 38.7 %copy-start.4 = (f32[32,16]{0,1:T(8,128)S(1)}, f32[32,16]{0,1:T(8,128)}, u32[]{:S(2)}) copy-start(f32[32,16]{0,1:T(8,128)} %param.9) | copy-start | bytes 6148
  35.2 5.5 %copy-start.5 = (f32[3,3,512]{2,1,0:T(4,128)S(1)}, f32[3,3,512]{2,1,0:T(4,128)}, u32[]{:S(2)}) copy-start(f32[3,3,512]{2,1,0:T(4,128)} %param.8) | copy-start | bytes 55300
  36.2 12.0 %collective-permute-start = (bf16[8,2,1024]{2,1,0:T(2,128)(2,1)S(1)}, bf16[8,2,1024]{2,1,0:T(2,128)(2,1)S(1)}, u32[]{:S(2)}, u32[]{:S(2)}) collective-permute-start(bf16[8,2,1024]{2,1,0:T(2,128)(2,1)S(1)} %slice.43), channel_id=1, source_target_pairs={{0,8},{8,0},{1,9},{9,1},{2,10},{10,2},{3,11},{11,3},{4,12},{12,4},... | collective-permute-start | bytes 98312 | tf_op jit(solution)/shard_map/ppermute | solution.py:246
  38.7 9.6 %collective-permute-start.1 = (bf16[512,1536]{0,1:T(8,128)(2,1)}, bf16[512,1536]{0,1:T(8,128)(2,1)}, u32[]{:S(2)}, u32[]{:S(2)}) collective-permute-start(bf16[512,1536]{0,1:T(8,128)(2,1)} %bitcast.1), channel_id=1, source_target_pairs={{0,8},{8,0},{1,9},{9,1},{2,10},{10,2},{3,11},{11,3},{4,12},{12,4},... | collective-permute-start | bytes 4718600 | tf_op jit(solution)/shard_map/ppermute | solution.py:238
  39.5 6.5 %copy-start.2 = (f32[32,16]{1,0:T(8,128)}, f32[32,16]{1,0:T(8,128)S(1)}, u32[]{:S(2)}) copy-start(f32[32,16]{1,0:T(8,128)S(1)} %copy.37) | copy-start | bytes 6148
  126.3 2.1 %copy-start.8 = (f32[128]{0:T(128)S(1)}, f32[128]{0:T(128)}, u32[]{:S(2)}) copy-start(f32[128]{0:T(128)} %iota_subtract_fusion) | copy-start | bytes 1540
  147.7 2.4 %copy-start.1 = (pred[128,128]{1,0:T(8,128)(4,1)S(1)}, pred[128,128]{1,0:T(8,128)(4,1)}, u32[]{:S(2)}) copy-start(pred[128,128]{1,0:T(8,128)(4,1)} %iota_compare_fusion) | copy-start | bytes 49156
  148.8 2.0 %copy-start.3 = (f32[32,16]{1,0:T(8,128)S(1)}, f32[32,16]{1,0:T(8,128)}, u32[]{:S(2)}) copy-start(f32[32,16]{1,0:T(8,128)} %copy-done.2) | copy-start | bytes 6148
  148.8 2.0 %copy-start.9 = (f32[128]{0:T(128)S(1)}, f32[128]{0:T(128)}, u32[]{:S(2)}) copy-start(f32[128]{0:T(128)} %iota_add_fusion) | copy-start | bytes 1540
  150.2 1.2 copy-start.7

commit v7 on v6

--- a/solution.py
+++ b/solution.py
@@ -33,8 +33,9 @@
     return z + y * (n - 1 - 2 * z)
 
 
-def rs_kernel(part_ref, out_ref, sbuf, rbuf, send_sem, recv_sem):
-    n, _, width = part_ref.shape
+def rs_kernel(tok_ref, w_ref, taps_ref, q_ref, g_ref, sbuf, rbuf, proj, send_sem, recv_sem):
+    n, ext_len, _ = tok_ref.shape
+    width = w_ref.shape[1]
     n_ring = sbuf.shape[0]
     chunk = width // n_ring
     chip = lax.axis_index("p")
@@ -48,6 +49,10 @@
     for nb in (nxt, prv):
         pl.semaphore_signal(barrier, 1, device_id=(nb, core, col), device_id_type=mesh_id)
     pl.semaphore_wait(barrier, 2)
+
+    def part(blk, cols):
+        return jnp.dot(tok_ref[blk], w_ref[:, cols], preferred_element_type=jnp.float32)
+
     copies = [[] for _ in range(n_ring)]
     order = [h * (n_ring // 2) + k for k in range(n_ring // 2) for h in range(2)]
     for s in range(n - 1):
@@ -56,12 +61,11 @@
             cols = pl.ds(ring * chunk, chunk)
             q = ring_chip((r - d * (1 + s) + 2 * n) % n, n)
             if s == 0:
-                sbuf[ring, 0] = part_ref[q, :, cols].astype(sbuf.dtype)
+                sbuf[ring, 0] = part(q, cols).astype(sbuf.dtype)
             else:
+                mine = part(q, cols)
                 copies[ring][s - 1].wait_recv()
-                sbuf[ring, s] = (
-                    rbuf[ring, s - 1].astype(jnp.float32) + part_ref[q, :, cols]
-                ).astype(sbuf.dtype)
+                sbuf[ring, s] = (rbuf[ring, s - 1].astype(jnp.float32) + mine).astype(sbuf.dtype)
             copy = pltpu.make_async_remote_copy(
                 src_ref=sbuf.at[ring, s],
                 dst_ref=rbuf.at[ring, s],
@@ -74,32 +78,56 @@
             copies[ring].append(copy)
     for ring in order:
         cols = pl.ds(ring * chunk, chunk)
+        mine = part(chip, cols)
         copies[ring][-1].wait_recv()
-        out_ref[:, cols] = (
-            rbuf[ring, n - 2].astype(jnp.float32) + part_ref[chip, :, cols]
-        ).astype(out_ref.dtype)
+        total = rbuf[ring, n - 2].astype(jnp.float32) + mine
+        proj[:, cols] = total.astype(jnp.bfloat16).astype(jnp.float32)
+
+    @pl.when(jnp.logical_and(chip == 0, core == 0))
+    def _():
+        proj[0:2, :] = jnp.zeros((2, width), jnp.float32)
+
+    rows = ext_len - 2
+    third = width // 3
+    mixed = []
+    for j in range(3):
+        cols = pl.ds(j * third, third)
+        mixed.append(
+            taps_ref[0, j][None, :] * proj[pl.ds(2, rows), cols]
+            + taps_ref[1, j][None, :] * proj[pl.ds(1, rows), cols]
+            + taps_ref[2, j][None, :] * proj[pl.ds(0, rows), cols]
+        )
+    q_ref[...] = mixed[0]
+    g_ref[...] = (mixed[1] * mixed[2]).astype(g_ref.dtype)
     for ring in order:
         for copy in copies[ring]:
             copy.wait_send()
 
 
-def ring_reduce_scatter(partial, n_ring=6):
-    n, rows, width = partial.shape
+def project_and_gate(tok_ext, w_flat, taps, n_ring=6):
+    n, ext_len, _ = tok_ext.shape
+    width = w_flat.shape[1]
+    rows, third = ext_len - 2, width // 3
+    vmem = pl.BlockSpec(memory_space=pltpu.VMEM)
     return pl.pallas_call(
         rs_kernel,
-        out_shape=jax.ShapeDtypeStruct((rows, width), jnp.bfloat16),
-        in_specs=[pl.BlockSpec(memory_space=pltpu.VMEM)],
-        out_specs=pl.BlockSpec(memory_space=pltpu.VMEM),
+        out_shape=(
+            jax.ShapeDtypeStruct((rows, third), jnp.float32),
+            jax.ShapeDtypeStruct((rows, third), jnp.bfloat16),
+        ),
+        in_specs=[vmem, vmem, vmem],
+        out_specs=(vmem, vmem),
         scratch_shapes=[
-            pltpu.VMEM((n_ring, n - 1, rows, width // n_ring), jnp.bfloat16),
-            pltpu.VMEM((n_ring, n - 1, rows, width // n_ring), jnp.bfloat16),
+            pltpu.VMEM((n_ring, n - 1, ext_len, width // n_ring), jnp.bfloat16),
+            pltpu.VMEM((n_ring, n - 1, ext_len, width // n_ring), jnp.bfloat16),
+            pltpu.VMEM((ext_len, width), jnp.float32),
             pltpu.SemaphoreType.DMA((n_ring, n - 1)),
             pltpu.SemaphoreType.DMA((n_ring, n - 1)),
         ],
         compiler_params=pltpu.CompilerParams(
             collective_id=0, has_side_effects=True, vmem_limit_bytes=48 * 1024 * 1024
         ),
-    )(partial)
+    )(tok_ext, w_flat, taps)
 
 
 def tok_kernel(src_ref, out_ref, send_sem, recv_sem):
@@ -247,22 +275,7 @@
     shifted_tail = jnp.concatenate([jnp.zeros_like(partner_tail[:1]), partner_tail[:-1]], axis=0)
     prior = jnp.where(core == 1, partner_tail, shifted_tail)
     tok_ext = jnp.concatenate([prior, tok_t], axis=1)
-    n_blk, ext_len = tok_ext.shape[0], tok_ext.shape[1]
-    partial = jnp.dot(
-        tok_ext.reshape(n_blk * ext_len, -1), flat_w, preferred_element_type=jnp.float32
-    ).reshape(n_blk, ext_len, -1)
-    proj = ring_reduce_scatter(partial).astype(jnp.float32)
-    first = jnp.logical_and(chip == 0, core == 0)
-    row_id = lax.broadcasted_iota(jnp.int32, proj.shape, 0)
-    proj = jnp.where(jnp.logical_and(first, row_id < 2), 0.0, proj)
-    proj = proj.astype(jnp.bfloat16).astype(jnp.float32).reshape(ext_len, 3, local_width)
-    mixed = (
-        short_filter[0] * proj[2:]
-        + short_filter[1] * proj[1:-1]
-        + short_filter[2] * proj[:-2]
-    )
-    query = mixed[:, 0]
-    gated = (mixed[:, 1] * mixed[:, 2]).astype(jnp.bfloat16)
+    query, gated = project_and_gate(tok_ext, flat_w, short_filter)
     x = gated.reshape(block_len, group_count, GROUP)
 
     pole_weight = residue * jnp.sqrt(2.0 * decay_rate)
@@ -284,7 +297,7 @@
     gap = (me - 1 - jnp.arange(n_ctx)).astype(jnp.float32)
     fac = jnp.exp(-decay_rate[None] * (block_len * jnp.maximum(gap, 0.0))[:, None, None])
     fac = jnp.where(gap[:, None, None] >= 0.0, fac, 0.0)
-    s_in = jnp.sum(fac[..., None] * s_all, axis=0)
+    s_in = jnp.einsum("kgr,kgrc->grc", fac, s_all, precision=HIGH)
     f_mat = pole_weight[:, None, :] * jnp.exp(-lam * (pos + 1.0)[None, :, None])
     far = jnp.einsum("gtr,grc->tgc", f_mat, s_in, precision=HIGH)
     long_out = (near + far).reshape(block_len, local_width)

time: 153 us -> 131 us (0.86)
  matrix products: 17.5 us -> 6.04 us
  local copies, waits for them, and re-layouts: 18.8 us -> 7.9 us
  other arithmetic: 5.98 us -> 8.48 us
  Pallas kernels: 109 us -> 107 us
    dot_general x1 -> x0, matrix products: 10 us -> none  [local(): jnp.dot(tok_ext.reshape(n_blk * ext_len, -1), flat_w, preferred_element_t...]
    slice x4 -> x0, local copies, waits for them, and re-layouts: 7.15 us -> none  [the longest x2 3.7 us: local(): proj[2:]]
    mul x3 -> x0, local copies, waits for them, and re-layouts: 3.65 us -> none  [the longest x2 3.65 us: local(): s_in = jnp.sum(fac[..., None] * s_all, axis=0)]
    select_n x1, other arithmetic: 0.1 us -> 3.48 us  [local(): jnp.where(core == 0, jnp.concatenate([w_flat, w_other], axis=0), jnp.conc...]
    unnamed x22 -> x14, local copies, waits for them, and re-layouts: 1.67 us -> 3.93 us
    concatenate x0 -> x1, other arithmetic: none -> 2.23 us  [local(): tok_ext = jnp.concatenate([prior, tok_t], axis=1)]
    add x1 -> x0, other arithmetic: 2.05 us -> none  [local(): short_filter[0] * proj[2:] + short_filter[1] * proj[1:-1]]
    unnamed x0 -> x2, other arithmetic: none -> 1.94 us
where the time goes in v7:
time: 131 us
  Pallas kernels  107 us (82%)
  other arithmetic  8.48 us (6%)
  local copies, waits for them, and re-layouts  7.9 us (6%)
  matrix products  6.04 us (5%)
    pallas_call x1, Pallas kernels, project_and_gate(): pl.pallas_call(rs_kernel, out_shape=(jax.ShapeDtypeStruct((rows, third),...  59.1 us
    pallas_call x1, Pallas kernels, spread_tokens(): pl.pallas_call(tok_kernel, out_shape=jax.ShapeDtypeStruct((n, rows, width...  35.1 us
    pallas_call x1, Pallas kernels, gather_earlier(): pl.pallas_call(state_kernel, out_shape=jax.ShapeDtypeStruct((n,) + state....  12.7 us
    unnamed x14, local copies, waits for them, and re-layouts  3.93 us
    dot_general x1, matrix products, local(): toep = jnp.einsum('gtr,gsr->gts', a_mat, b_mat, precision=HIGH)  3.65 us
    select_n x1, other arithmetic, local(): jnp.where(core == 0, jnp.concatenate([w_flat, w_other], axis=0), jnp.conc...  3.48 us
  transfers between devices with their start and end apart: 2, of which 0 were waited for; matrix products, arithmetic and copies ran while one was open for 7% of the time, Pallas kernels for 0%

profile of v7, /device:TPU:1, one launch (start us, length us, event | category | flops | bytes accessed | tf_op | source)
XLA Modules:
  0.0 130.5 jit_solution(2002774784917492774)
XLA Ops:
  0.0 0.0 copy-start.1
  0.0 35.1 %shard_map.64 = bf16[8,128,1024]{2,1,0:T(8,128)(2,1)} custom-call(bf16[128,1024]{1,0:T(8,128)(2,1)} %src_ref.1), custom_call_target="tpu_custom_call" | custom-call | tf_op jit(solution)/shard_map/pallas_call | solution.py:189
  35.1 0.9 slice.6
  36.0 1.0 collective-permute-start
  37.0 0.0 copy-done.1
  37.0 0.7 copy.17
  37.7 0.0 copy-start.2
  37.7 0.0 copy-start.3
  37.8 1.6 %copy.19 = bf16[512,1536]{1,0:T(8,128)(2,1)} copy(bf16[512,1536]{0,1:T(8,128)(2,1)S(1)} %bitcast.18) | data formatting | bytes 3145728 | tf_op jit(solution)/shard_map/reshape | solution.py:265
  39.3 0.0 collective-permute-start.1
  39.4 0.0 copy-done.2
  39.4 0.0 copy-done.3
  39.4 0.1 copy.24
  39.5 0.1 copy.23
  39.5 0.1 copy.22
  39.7 0.1 select_bitcast_fusion
  39.8 3.7 %fusion.11 = f32[32,128,128]{2,1,0:T(8,128)S(1)} fusion(f32[32,16]{1,0:T(8,128)S(1)} %copy.24, f32[32,16]{1,0:T(8,128)S(1)} %copy.23, f32[32,16]{1,0:T(8,128)S(1)} %copy.22), kind=kOutput, calls=%fused_computation.22 | convolution fusion | flops 100859904 | bytes 2103296 | tf_op jit(solution)/shard_map/gtr,gsr->gts/dot_general | solution.py:286
  43.5 0.1 copy.39
  43.6 0.0 collective-permute-done
  43.6 0.1 broadcast_select_fusion
  43.7 2.2 %pad_maximum_fusion.tok_ref = bf16[8,130,1024]{2,1,0:T(8,128)(2,1)S(1)} fusion(bf16[8,128,1024]{2,1,0:T(8,128)(2,1)} %shard_map.64, bf16[8,2,1024]{2,1,0:T(2,128)(2,1)S(1)} %broadcast_select_fusion), kind=kLoop, calls=%fused_computation.1 | loop fusion | flops 4259840 | bytes 4259840 | tf_op jit(solution)/shard_map/concatenate | solution.py:277
  45.9 0.0 copy-start
  45.9 0.0 collective-permute-done.1
  45.9 3.5 %maximum_select_fusion.w_ref = bf16[1024,1536]{1,0:T(8,128)(2,1)S(1)} fusion(bf16[512,1536]{1,0:T(8,128)(2,1)} %collective-permute-done.1, bf16[512,1536]{1,0:T(8,128)(2,1)} %copy.19, pred[]{:T(512)S(6)} %eq.7), kind=kLoop, calls=%fused_computation | loop fusion | flops 14155776 | bytes 6291457 | tf_op jit(solution)/shard_map/jit(_where)/select_n | solution.py:267
  49.4 0.0 copy-done
  49.4 59.1 %shard_map.65 = (f32[128,512]{1,0:T(8,128)S(1)}, bf16[128,512]{1,0:T(8,128)(2,1)S(1)}) custom-call(bf16[8,130,1024]{2,1,0:T(8,128)(2,1)S(1)} %pad_maximum_fusion.tok_ref, bf16[1024,1536]{1,0:T(8,128)(2,1)S(1)} %maximum_select_fusion.w_ref, f32[3,3,512]{2,1,0:T(4,128)S(1)} %copy-done), custom_call_target="tpu_custom_call" | custom-call | tf_op jit(solution)/shard_map/pallas_call | solution.py:112
  108.6 0.1 copy.21
  108.7 0.3 fusion.19
  109.0 0.3 convolution_add_fusion.1
  109.2 0.2 copy.26
  109.4 0.7 copy.27.src_ref
  110.1 12.7 %shard_map.66 = f32[16,32,256]{2,1,0:T(8,128)} custom-call(f32[32,256]{1,0:T(8,128)} %copy.27.src_ref), custom_call_target="tpu_custom_call" | custom-call | tf_op jit(solution)/shard_map/pallas_call | solution.py:244
  122.8 3.0 %copy.38 = f32[16,32,256]{1,2,0:T(8,128)} copy(f32[16,32,256]{2,1,0:T(8,128)} %shard_map.66) | data formatting | bytes 1048576
  125.8 1.8 %multiply_reduce_fusion = f32[32,16,16]{0,2,1:T(8,128)S(1)} fusion(f32[32,16,16,16]{0,3,1,2:T(8,128)} %bitcast.17, f32[32,16,16]{0,1,2:T(8,128)S(1)} %copy.39), kind=kLoop, calls=%fused_computation.2 | loop fusion | flops 253952 | bytes 589824
  127.6 0.2 copy.37
  127.8 0.6 fusion.2
  128.5 0.0 copy-start.4
  128.5 0.7 fusion.1
  129.1 0.5 convolution_add_fusion
  129.6 0.1 copy.29
  129.8 0.0 copy-done.4
  129.8 0.7 multiply_convert_fusion
  (7 shorter events, 0.1 us)
Async XLA Ops:
  0.0 37.0 %copy-start.1 = (bf16[512,3,512]{2,0,1:T(8,128)(2,1)S(1)}, bf16[512,3,512]{2,0,1:T(8,128)(2,1)}, u32[]{:S(2)}) copy-start(bf16[512,3,512]{2,0,1:T(8,128)(2,1)} %param.7) | copy-start | bytes 4718596
  36.0 7.5 %collective-permute-start = (bf16[8,2,1024]{2,1,0:T(2,128)(2,1)S(1)}, bf16[8,2,1024]{2,1,0:T(2,128)(2,1)S(1)}, u32[]{:S(2)}, u32[]{:S(2)}) collective-permute-start(bf16[8,2,1024]{2,1,0:T(2,128)(2,1)S(1)} %slice.6), channel_id=1, source_target_pairs={{0,8},{8,0},{1,9},{9,1},{2,10},{10,2},{3,11},{11,3},{4,12},{12,4},... | collective-permute-start | bytes 98312 | tf_op jit(solution)/shard_map/ppermute | solution.py:274
  37.7 1.6 %copy-start.2 = (f32[32,16]{0,1:T(8,128)S(1)}, f32[32,16]{0,1:T(8,128)}, u32[]{:S(2)}) copy-start(f32[32,16]{0,1:T(8,128)} %param.9) | copy-start | bytes 6148
  37.7 1.6 %copy-start.3 = (f32[32,16]{0,1:T(8,128)S(1)}, f32[32,16]{0,1:T(8,128)}, u32[]{:S(2)}) copy-start(f32[32,16]{0,1:T(8,128)} %param.10) | copy-start | bytes 6148
  39.3 6.6 %collective-permute-start.1 = (bf16[512,1536]{1,0:T(8,128)(2,1)}, bf16[512,1536]{1,0:T(8,128)(2,1)}, u32[]{:S(2)}, u32[]{:S(2)}) collective-permute-start(bf16[512,1536]{1,0:T(8,128)(2,1)} %copy.19), channel_id=1, source_target_pairs={{0,8},{8,0},{1,9},{9,1},{2,10},{10,2},{3,11},{11,3},{4,12},{12,4},... | collective-permute-start | bytes 4718600 | tf_op jit(solution)/shard_map/ppermute | solution.py:266
  45.9 3.5 %copy-start = (f32[3,3,512]{2,1,0:T(4,128)S(1)}, f32[3,3,512]{2,1,0:T(4,128)}, u32[]{:S(2)}) copy-start(f32[3,3,512]{2,1,0:T(4,128)} %taps_ref.1) | copy-start | bytes 55300
  128.5 1.3 %copy-start.4 = (f32[512]{0:T(512)S(1)}, f32[512]{0:T(512)}, u32[]{:S(2)}) copy-start(f32[512]{0:T(512)} %param.11) | copy-start | bytes 6148

commit v8 on v7

--- a/solution.py
+++ b/solution.py
@@ -21,6 +21,25 @@
     return jnp.einsum(spec, hi, data, preferred_element_type=jnp.float32) + jnp.einsum(
         spec, lo, data, preferred_element_type=jnp.float32
     )
+
+
+CYCLES = (
+    (0, 1, 3, 2, 4, 5, 7, 6),
+    (0, 1, 3, 5, 7, 6, 4, 2),
+    (0, 1, 7, 5, 3, 2, 4, 6),
+    (0, 1, 7, 6, 4, 5, 3, 2),
+    (0, 2, 3, 1, 7, 5, 4, 6),
+    (0, 2, 4, 5, 3, 1, 7, 6),
+)
+
+
+def lookup(table, v):
+    n = len(table)
+    total = 0
+    for k, t in enumerate(table):
+        if t:
+            total = total + t * (1 - ((v - k + n) % n + n - 1) // n)
+    return total
 
 
 def ring_chip(r, n):
@@ -41,25 +60,31 @@
     chip = lax.axis_index("p")
     core = lax.axis_index("c")
     col = lax.axis_index("ch")
-    r = ring_pos(chip, n)
-    nxt = ring_chip((r + 1) % n, n)
-    prv = ring_chip((r - 1 + n) % n, n)
     mesh_id = pl.DeviceIdType.MESH
+    rings = []
+    for cyc in CYCLES:
+        inv = [cyc.index(p) for p in range(n)]
+        r = lookup(inv, chip)
+        for d in (1, -1):
+            rings.append((cyc, d, r, lookup(cyc, (r + d + n) % n)))
+    z, y = chip // 2, chip % 2
+    n_z = n // 2
+    neighbours = (2 * ((z + 1) % n_z) + y, 2 * ((z + n_z - 1) % n_z) + y, 2 * z + 1 - y)
     barrier = pltpu.get_barrier_semaphore()
-    for nb in (nxt, prv):
+    for nb in neighbours:
         pl.semaphore_signal(barrier, 1, device_id=(nb, core, col), device_id_type=mesh_id)
-    pl.semaphore_wait(barrier, 2)
+    pl.semaphore_wait(barrier, len(neighbours))
 
     def part(blk, cols):
         return jnp.dot(tok_ref[blk], w_ref[:, cols], preferred_element_type=jnp.float32)
 
     copies = [[] for _ in range(n_ring)]
-    order = [h * (n_ring // 2) + k for k in range(n_ring // 2) for h in range(2)]
+    order = list(range(n_ring))
     for s in range(n - 1):
         for ring in order:
-            d, dest = (1, nxt) if ring < n_ring // 2 else (-1, prv)
+            cyc, d, r, dest = rings[ring]
             cols = pl.ds(ring * chunk, chunk)
-            q = ring_chip((r - d * (1 + s) + 2 * n) % n, n)
+            q = lookup(cyc, (r - d * (1 + s) + 2 * n) % n)
             if s == 0:
                 sbuf[ring, 0] = part(q, cols).astype(sbuf.dtype)
             else:
@@ -104,7 +129,7 @@
             copy.wait_send()
 
 
-def project_and_gate(tok_ext, w_flat, taps, n_ring=6):
+def project_and_gate(tok_ext, w_flat, taps, n_ring=2 * len(CYCLES)):
     n, ext_len, _ = tok_ext.shape
     width = w_flat.shape[1]
     rows, third = ext_len - 2, width // 3

time: 131 us -> 128 us (0.977)
  Pallas kernels: 107 us -> 104 us
    pallas_call x1, Pallas kernels: 59.1 us -> 55.4 us  [project_and_gate(): pl.pallas_call(rs_kernel, out_shape=(jax.ShapeDtypeStruct((rows, third),...]
where the time goes in v8:
time: 128 us
  Pallas kernels  104 us (81%)
  other arithmetic  8.48 us (7%)
  local copies, waits for them, and re-layouts  7.9 us (6%)
  matrix products  6.05 us (5%)
    pallas_call x1, Pallas kernels, project_and_gate(): pl.pallas_call(rs_kernel, out_shape=(jax.ShapeDtypeStruct((rows, third),...  55.4 us
    pallas_call x1, Pallas kernels, spread_tokens(): pl.pallas_call(tok_kernel, out_shape=jax.ShapeDtypeStruct((n, rows, width...  35.1 us
    pallas_call x1, Pallas kernels, gather_earlier(): pl.pallas_call(state_kernel, out_shape=jax.ShapeDtypeStruct((n,) + state....  13.8 us
    unnamed x14, local copies, waits for them, and re-layouts  3.93 us
    dot_general x1, matrix products, local(): toep = jnp.einsum('gtr,gsr->gts', a_mat, b_mat, precision=HIGH)  3.65 us
    select_n x1, other arithmetic, local(): jnp.where(core == 0, jnp.concatenate([w_flat, w_other], axis=0), jnp.conc...  3.48 us
  transfers between devices with their start and end apart: 2, of which 0 were waited for; matrix products, arithmetic and copies ran while one was open for 7% of the time, Pallas kernels for 0%

profile of v8, /device:TPU:1, one launch (start us, length us, event | category | flops | bytes accessed | tf_op | source)
XLA Modules:
  0.0 128.0 jit_solution(8873909098178040456)
XLA Ops:
  0.0 0.0 copy-start.1
  0.0 35.1 %shard_map.64 = bf16[8,128,1024]{2,1,0:T(8,128)(2,1)} custom-call(bf16[128,1024]{1,0:T(8,128)(2,1)} %src_ref.1), custom_call_target="tpu_custom_call" | custom-call | tf_op jit(solution)/shard_map/pallas_call | solution.py:214
  35.1 0.9 slice.6
  36.0 1.0 collective-permute-start
  37.0 0.0 copy-done.1
  37.0 0.7 copy.17
  37.7 0.0 copy-start.2
  37.7 0.0 copy-start.3
  37.8 1.6 %copy.19 = bf16[512,1536]{1,0:T(8,128)(2,1)} copy(bf16[512,1536]{0,1:T(8,128)(2,1)S(1)} %bitcast.18) | data formatting | bytes 3145728 | tf_op jit(solution)/shard_map/reshape | solution.py:290
  39.3 0.0 collective-permute-start.1
  39.4 0.0 copy-done.2
  39.4 0.0 copy-done.3
  39.4 0.1 copy.24
  39.5 0.1 copy.23
  39.5 0.1 copy.22
  39.7 0.1 select_bitcast_fusion
  39.8 3.7 %fusion.11 = f32[32,128,128]{2,1,0:T(8,128)S(1)} fusion(f32[32,16]{1,0:T(8,128)S(1)} %copy.24, f32[32,16]{1,0:T(8,128)S(1)} %copy.23, f32[32,16]{1,0:T(8,128)S(1)} %copy.22), kind=kOutput, calls=%fused_computation.22 | convolution fusion | flops 100859904 | bytes 2103296 | tf_op jit(solution)/shard_map/gtr,gsr->gts/dot_general | solution.py:311
  43.5 0.1 copy.39
  43.6 0.0 collective-permute-done
  43.6 0.1 broadcast_select_fusion
  43.7 2.2 %pad_maximum_fusion.tok_ref = bf16[8,130,1024]{2,1,0:T(8,128)(2,1)S(1)} fusion(bf16[8,128,1024]{2,1,0:T(8,128)(2,1)} %shard_map.64, bf16[8,2,1024]{2,1,0:T(2,128)(2,1)S(1)} %broadcast_select_fusion), kind=kLoop, calls=%fused_computation.1 | loop fusion | flops 4259840 | bytes 4259840 | tf_op jit(solution)/shard_map/concatenate | solution.py:302
  45.9 0.0 copy-start
  45.9 0.0 collective-permute-done.1
  45.9 3.5 %maximum_select_fusion.w_ref = bf16[1024,1536]{1,0:T(8,128)(2,1)S(1)} fusion(bf16[512,1536]{1,0:T(8,128)(2,1)} %collective-permute-done.1, bf16[512,1536]{1,0:T(8,128)(2,1)} %copy.19, pred[]{:T(512)S(6)} %eq.7), kind=kLoop, calls=%fused_computation | loop fusion | flops 14155776 | bytes 6291457 | tf_op jit(solution)/shard_map/jit(_where)/select_n | solution.py:292
  49.4 0.0 copy-done
  49.4 55.4 %shard_map.65 = (f32[128,512]{1,0:T(8,128)S(1)}, bf16[128,512]{1,0:T(8,128)(2,1)S(1)}) custom-call(bf16[8,130,1024]{2,1,0:T(8,128)(2,1)S(1)} %pad_maximum_fusion.tok_ref, bf16[1024,1536]{1,0:T(8,128)(2,1)S(1)} %maximum_select_fusion.w_ref, f32[3,3,512]{2,1,0:T(4,128)S(1)} %copy-done), custom_call_target="tpu_custom_call" | custom-call | tf_op jit(solution)/shard_map/pallas_call | solution.py:137
  104.9 0.1 copy.21
  105.0 0.3 fusion.19
  105.3 0.3 convolution_add_fusion.1
  105.6 0.2 copy.26
  105.7 0.7 copy.27.src_ref
  106.4 13.8 %shard_map.66 = f32[16,32,256]{2,1,0:T(8,128)} custom-call(f32[32,256]{1,0:T(8,128)} %copy.27.src_ref), custom_call_target="tpu_custom_call" | custom-call | tf_op jit(solution)/shard_map/pallas_call | solution.py:269
  120.2 3.0 %copy.38 = f32[16,32,256]{1,2,0:T(8,128)} copy(f32[16,32,256]{2,1,0:T(8,128)} %shard_map.66) | data formatting | bytes 1048576
  123.2 1.8 %multiply_reduce_fusion = f32[32,16,16]{0,2,1:T(8,128)S(1)} fusion(f32[32,16,16,16]{0,3,1,2:T(8,128)} %bitcast.17, f32[32,16,16]{0,1,2:T(8,128)S(1)} %copy.39), kind=kLoop, calls=%fused_computation.2 | loop fusion | flops 253952 | bytes 589824
  125.1 0.2 copy.37
  125.3 0.6 fusion.2
  125.9 0.0 copy-start.4
  125.9 0.7 fusion.1
  126.6 0.5 convolution_add_fusion
  127.1 0.1 copy.29
  127.2 0.0 copy-done.4
  127.2 0.7 multiply_convert_fusion
  (7 shorter events, 0.1 us)
Async XLA Ops:
  0.0 37.0 %copy-start.1 = (bf16[512,3,512]{2,0,1:T(8,128)(2,1)S(1)}, bf16[512,3,512]{2,0,1:T(8,128)(2,1)}, u32[]{:S(2)}) copy-start(bf16[512,3,512]{2,0,1:T(8,128)(2,1)} %param.7) | copy-start | bytes 4718596
  36.0 7.5 %collective-permute-start = (bf16[8,2,1024]{2,1,0:T(2,128)(2,1)S(1)}, bf16[8,2,1024]{2,1,0:T(2,128)(2,1)S(1)}, u32[]{:S(2)}, u32[]{:S(2)}) collective-permute-start(bf16[8,2,1024]{2,1,0:T(2,128)(2,1)S(1)} %slice.6), channel_id=1, source_target_pairs={{0,8},{8,0},{1,9},{9,1},{2,10},{10,2},{3,11},{11,3},{4,12},{12,4},... | collective-permute-start | bytes 98312 | tf_op jit(solution)/shard_map/ppermute | solution.py:299
  37.7 1.6 %copy-start.2 = (f32[32,16]{0,1:T(8,128)S(1)}, f32[32,16]{0,1:T(8,128)}, u32[]{:S(2)}) copy-start(f32[32,16]{0,1:T(8,128)} %param.9) | copy-start | bytes 6148
  37.7 1.6 %copy-start.3 = (f32[32,16]{0,1:T(8,128)S(1)}, f32[32,16]{0,1:T(8,128)}, u32[]{:S(2)}) copy-start(f32[32,16]{0,1:T(8,128)} %param.10) | copy-start | bytes 6148
  39.3 6.6 %collective-permute-start.1 = (bf16[512,1536]{1,0:T(8,128)(2,1)}, bf16[512,1536]{1,0:T(8,128)(2,1)}, u32[]{:S(2)}, u32[]{:S(2)}) collective-permute-start(bf16[512,1536]{1,0:T(8,128)(2,1)} %copy.19), channel_id=1, source_target_pairs={{0,8},{8,0},{1,9},{9,1},{2,10},{10,2},{3,11},{11,3},{4,12},{12,4},... | collective-permute-start | bytes 4718600 | tf_op jit(solution)/shard_map/ppermute | solution.py:291
  45.9 3.5 %copy-start = (f32[3,3,512]{2,1,0:T(4,128)S(1)}, f32[3,3,512]{2,1,0:T(4,128)}, u32[]{:S(2)}) copy-start(f32[3,3,512]{2,1,0:T(4,128)} %taps_ref.1) | copy-start | bytes 55300
  125.9 1.3 %copy-start.4 = (f32[512]{0:T(512)S(1)}, f32[512]{0:T(512)}, u32[]{:S(2)}) copy-start(f32[512]{0:T(512)} %param.11) | copy-start | bytes 6148

commit v9 on v8

--- a/solution.py
+++ b/solution.py
@@ -52,9 +52,13 @@
     return z + y * (n - 1 - 2 * z)
 
 
-def rs_kernel(tok_ref, w_ref, taps_ref, q_ref, g_ref, sbuf, rbuf, proj, send_sem, recv_sem):
-    n, ext_len, _ = tok_ref.shape
-    width = w_ref.shape[1]
+def rs_kernel(
+    tok_ref, prior_ref, w_own, w_other, taps_ref, q_ref, g_ref, sbuf, rbuf, proj, send_sem, recv_sem
+):
+    n, rows, _ = tok_ref.shape
+    tail = prior_ref.shape[1]
+    ext_len = rows + tail
+    half, width = w_own.shape
     n_ring = sbuf.shape[0]
     chunk = width // n_ring
     chip = lax.axis_index("p")
@@ -75,8 +79,16 @@
         pl.semaphore_signal(barrier, 1, device_id=(nb, core, col), device_id_type=mesh_id)
     pl.semaphore_wait(barrier, len(neighbours))
 
+    own_cols = pl.ds(pl.multiple_of(core * half, half), half)
+    other_cols = pl.ds(pl.multiple_of((1 - core) * half, half), half)
+
     def part(blk, cols):
-        return jnp.dot(tok_ref[blk], w_ref[:, cols], preferred_element_type=jnp.float32)
+        def proj_rows(ref):
+            return jnp.dot(
+                ref[blk, :, own_cols], w_own[:, cols], preferred_element_type=jnp.float32
+            ) + jnp.dot(ref[blk, :, other_cols], w_other[:, cols], preferred_element_type=jnp.float32)
+
+        return jnp.concatenate([proj_rows(tok_ref), proj_rows(prior_ref)], axis=0)
 
     copies = [[] for _ in range(n_ring)]
     order = list(range(n_ring))
@@ -105,14 +117,15 @@
         cols = pl.ds(ring * chunk, chunk)
         mine = part(chip, cols)
         copies[ring][-1].wait_recv()
-        total = rbuf[ring, n - 2].astype(jnp.float32) + mine
-        proj[:, cols] = total.astype(jnp.bfloat16).astype(jnp.float32)
+        total = (rbuf[ring, n - 2].astype(jnp.float32) + mine).astype(jnp.bfloat16)
+        total = total.astype(jnp.float32)
+        proj[pl.ds(tail, rows), cols] = total[:rows]
+        proj[pl.ds(0, tail), cols] = total[rows:]
 
     @pl.when(jnp.logical_and(chip == 0, core == 0))
     def _():
         proj[0:2, :] = jnp.zeros((2, width), jnp.float32)
 
-    rows = ext_len - 2
     third = width // 3
     mixed = []
     for j in range(3):
@@ -129,10 +142,11 @@
             copy.wait_send()
 
 
-def project_and_gate(tok_ext, w_flat, taps, n_ring=2 * len(CYCLES)):
-    n, ext_len, _ = tok_ext.shape
-    width = w_flat.shape[1]
-    rows, third = ext_len - 2, width // 3
+def project_and_gate(tok, prior, w_own, w_other, taps, n_ring=2 * len(CYCLES)):
+    n, rows, _ = tok.shape
+    ext_len = rows + prior.shape[1]
+    width = w_own.shape[1]
+    third = width // 3
     vmem = pl.BlockSpec(memory_space=pltpu.VMEM)
     return pl.pallas_call(
         rs_kernel,
@@ -140,7 +154,7 @@
             jax.ShapeDtypeStruct((rows, third), jnp.float32),
             jax.ShapeDtypeStruct((rows, third), jnp.bfloat16),
         ),
-        in_specs=[vmem, vmem, vmem],
+        in_specs=[vmem] * 5,
         out_specs=(vmem, vmem),
         scratch_shapes=[
             pltpu.VMEM((n_ring, n - 1, ext_len, width // n_ring), jnp.bfloat16),
@@ -152,14 +166,16 @@
         compiler_params=pltpu.CompilerParams(
             collective_id=0, has_side_effects=True, vmem_limit_bytes=48 * 1024 * 1024
         ),
-    )(tok_ext, w_flat, taps)
-
-
-def tok_kernel(src_ref, out_ref, send_sem, recv_sem):
-    n = out_ref.shape[0]
+    )(tok, prior, w_own, w_other, taps)
+
+
+def tok_kernel(src_ref, out_ref, prior_ref, send_sem, recv_sem, psend_sem, precv_sem):
+    n, rows, _ = out_ref.shape
+    tail = prior_ref.shape[1]
     chip = lax.axis_index("p")
     core = lax.axis_index("c")
     col = lax.axis_index("ch")
+    other = 1 - core
     mesh_id = pl.DeviceIdType.MESH
     diag = chip == col
     barrier = pltpu.get_barrier_semaphore()
@@ -174,7 +190,14 @@
         else:
             pl.semaphore_signal(barrier, 1, device_id=dest, device_id_type=mesh_id)
             pl.semaphore_signal(barrier, 1, device_id=srce, device_id_type=mesh_id)
-    pl.semaphore_wait(barrier, 2 * n - 2 * diag.astype(jnp.int32))
+        pl.semaphore_signal(
+            barrier, 1, device_id=(col, other, (chip + k) % n), device_id_type=mesh_id
+        )
+        pl.semaphore_signal(
+            barrier, 1, device_id=((chip + k) % n, other, chip), device_id_type=mesh_id
+        )
+    pl.semaphore_wait(barrier, 4 * n - 2 * diag.astype(jnp.int32))
+    slot = (chip + core) % n
     copies = []
     for k in range(n):
         copy = pltpu.make_async_remote_copy(
@@ -198,8 +221,23 @@
         else:
             copy.start()
         copies.append(copy)
+    pcopies = []
+    for k in range(n):
+        pcopy = pltpu.make_async_remote_copy(
+            src_ref=src_ref.at[pl.ds(rows - tail, tail)],
+            dst_ref=prior_ref.at[slot],
+            send_sem=psend_sem.at[k],
+            recv_sem=precv_sem.at[slot],
+            device_id=(col, other, (chip + k) % n),
+            device_id_type=mesh_id,
+        )
+        pcopy.start()
+        pcopies.append(pcopy)
     for j in range(n):
         pltpu.make_async_copy(src_ref, out_ref.at[j], recv_sem.at[j]).wait()
+        pltpu.make_async_copy(
+            src_ref.at[pl.ds(rows - tail, tail)], prior_ref.at[j], precv_sem.at[j]
+        ).wait()
     for k in range(n):
         if k == 0:
             @pl.when(jnp.logical_not(diag))
@@ -207,16 +245,21 @@
                 copies[0].wait_send()
         else:
             copies[k].wait_send()
-
-
-def spread_tokens(tokens, n):
+        pcopies[k].wait_send()
+
+
+def spread_tokens(tokens, n, tail=2):
     rows, width = tokens.shape
+    vmem = pl.BlockSpec(memory_space=pltpu.VMEM)
     return pl.pallas_call(
         tok_kernel,
-        out_shape=jax.ShapeDtypeStruct((n, rows, width), tokens.dtype),
-        in_specs=[pl.BlockSpec(memory_space=pltpu.VMEM)],
-        out_specs=pl.BlockSpec(memory_space=pltpu.VMEM),
-        scratch_shapes=[pltpu.SemaphoreType.DMA((n,)), pltpu.SemaphoreType.DMA((n,))],
+        out_shape=(
+            jax.ShapeDtypeStruct((n, rows, width), tokens.dtype),
+            jax.ShapeDtypeStruct((n, tail, width), tokens.dtype),
+        ),
+        in_specs=[vmem],
+        out_specs=(vmem, vmem),
+        scratch_shapes=[pltpu.SemaphoreType.DMA((n,))] * 4,
         compiler_params=pltpu.CompilerParams(collective_id=1, has_side_effects=True),
     )(tokens)
 
@@ -286,21 +329,10 @@
     col = lax.axis_index("ch")
 
     n_col = lax.axis_size("ch")
-    tok_t = spread_tokens(tokens, n_col)
-    w_flat = w_in.reshape(w_in.shape[0], -1)
-    w_other = lax.ppermute(w_flat, "c", [(0, 1), (1, 0)])
-    flat_w = jnp.where(
-        core == 0,
-        jnp.concatenate([w_flat, w_other], axis=0),
-        jnp.concatenate([w_other, w_flat], axis=0),
-    )
-
-    tail = tok_t[:, block_len - 2 :]
-    partner_tail = lax.ppermute(tail, "c", [(0, 1), (1, 0)])
-    shifted_tail = jnp.concatenate([jnp.zeros_like(partner_tail[:1]), partner_tail[:-1]], axis=0)
-    prior = jnp.where(core == 1, partner_tail, shifted_tail)
-    tok_ext = jnp.concatenate([prior, tok_t], axis=1)
-    query, gated = project_and_gate(tok_ext, flat_w, short_filter)
+    tok_t, prior = spread_tokens(tokens, n_col)
+    w_own = w_in.reshape(w_in.shape[0], -1)
+    w_other = lax.ppermute(w_own, "c", [(0, 1), (1, 0)])
+    query, gated = project_and_gate(tok_t, prior, w_own, w_other, short_filter)
     x = gated.reshape(block_len, group_count, GROUP)
 
     pole_weight = residue * jnp.sqrt(2.0 * decay_rate)

time: 128 us -> 130 us (1.016)
  other arithmetic: 8.48 us -> 4.5 us
  Pallas kernels: 104 us -> 107 us
  matrix products: 6.05 us -> 8.59 us
    select_n x2 -> x0, other arithmetic: 3.53 us -> none  [the longest x1 3.48 us: local(): jnp.where(core == 0, jnp.concatenate([w_flat, w_other], axis=0), jnp.conc...]
    unnamed x14 -> x28, local copies, waits for them, and re-layouts: 3.93 us -> 6.32 us
    pallas_call x1, Pallas kernels: 55.4 us -> 57.8 us  [project_and_gate(): pl.pallas_call(rs_kernel, out_shape=(jax.ShapeDtypeStruct((rows, third),...]
    concatenate x1 -> x0, other arithmetic: 2.23 us -> none  [local(): tok_ext = jnp.concatenate([prior, tok_t], axis=1)]
    dot_general x1, matrix products: 3.65 us -> 4.98 us  [local(): toep = jnp.einsum('gtr,gsr->gts', a_mat, b_mat, precision=HIGH)]
  transfers between devices with their start and end apart: 2 -> 1, of which waited for: 0 -> 0; matrix products, arithmetic and copies ran while one was open for 7% -> 6% of each run, Pallas kernels for 0% -> 27%
where the time goes in v9:
time: 130 us
  Pallas kernels  107 us (82%)
  matrix products  8.59 us (7%)
  local copies, waits for them, and re-layouts  8.47 us (7%)
  other arithmetic  4.5 us (3%)
  starting transfers between devices  1.5 us (1%)
    pallas_call x1, Pallas kernels, project_and_gate(): pl.pallas_call(rs_kernel, out_shape=(jax.ShapeDtypeStruct((rows, third),...  57.8 us
    pallas_call x1, Pallas kernels, spread_tokens(): pl.pallas_call(tok_kernel, out_shape=(jax.ShapeDtypeStruct((n, rows, widt...  35.4 us
    pallas_call x1, Pallas kernels, gather_earlier(): pl.pallas_call(state_kernel, out_shape=jax.ShapeDtypeStruct((n,) + state....  13.5 us
    unnamed x28, local copies, waits for them, and re-layouts  6.32 us
    dot_general x1, matrix products, local(): toep = jnp.einsum('gtr,gsr->gts', a_mat, b_mat, precision=HIGH)  4.98 us
  transfers between devices with their start and end apart: 1, of which 0 were waited for; matrix products, arithmetic and copies ran while one was open for 6% of the time, Pallas kernels for 27%

profile of v9, /device:TPU:1, one launch (start us, length us, event | category | flops | bytes accessed | tf_op | source)
XLA Modules:
  0.0 130.0 jit_solution(3300423388247943153)
XLA Ops:
  0.0 1.7 %copy.17 = bf16[512,3,512]{0,2,1:T(8,128)(2,1)S(1)} copy(bf16[512,3,512]{2,0,1:T(8,128)(2,1)} %param.7) | data formatting | bytes 3145728 | tf_op args[1]
  1.7 0.0 copy-start.8
  1.7 0.0 copy-start.9
  1.7 0.7 copy.19.w_own
  2.5 1.5 %collective-permute-start = (bf16[512,1536]{1,0:T(8,128)(2,1)S(1)}, bf16[512,1536]{1,0:T(8,128)(2,1)S(1)}, u32[]{:S(2)}, u32[]{:S(2)}) collective-permute-start(bf16[512,1536]{1,0:T(8,128)(2,1)S(1)} %copy.19.w_own), channel_id=1, source_target_pairs={{0,8},{8,0},{1,9},{9,1},{2,10},{10,2},{3,11},{11,3},{4,12},{12,4},... | collective-permute-start | bytes 4718600 | tf_op jit(solution)/shard_map/ppermute | solution.py:334
  4.0 35.4 %shard_map.64 = (bf16[8,128,1024]{2,1,0:T(8,128)(2,1)}, bf16[8,2,1024]{2,1,0:T(2,128)(2,1)}) custom-call(bf16[128,1024]{1,0:T(8,128)(2,1)} %src_ref.1), custom_call_target="tpu_custom_call" | custom-call | tf_op jit(solution)/shard_map/pallas_call | solution.py:254
  39.3 0.0 copy-done.8
  39.4 0.1 copy.23
  39.4 0.0 copy-done.9
  39.5 0.1 copy.22
  39.5 0.1 select_bitcast_fusion
  39.7 0.8 copy.38
  40.5 0.1 copy.21
  40.5 0.0 copy-start.6
  40.5 0.0 copy-start
  40.5 0.0 copy-start.1
  40.5 0.5 iota_subtract_fusion
  41.1 0.5 iota_add_fusion
  41.6 0.6 iota_compare_fusion
  42.2 5.0 %fusion.13 = f32[32,128,128]{2,1,0:T(8,128)} fusion(f32[32,16]{1,0:T(8,128)S(1)} %copy.23, f32[32,16]{1,0:T(8,128)S(1)} %copy.22, f32[32,16]{1,0:T(8,128)S(1)} %copy.21), kind=kOutput, calls=%fused_computation.21 | convolution fusion | flops 100859904 | bytes 2103296 | tf_op jit(solution)/shard_map/gtr,gsr->gts/dot_general | solution.py:343
  47.2 0.0 collective-permute-done.w_other
  47.2 0.0 copy-done.6
  47.2 0.0 copy-done
  47.2 0.0 copy-done.1
  47.2 0.0 copy-start.2
  47.2 0.7 copy-done.2
  48.0 57.8 %shard_map.65 = (f32[128,512]{1,0:T(8,128)S(1)}, bf16[128,512]{1,0:T(8,128)(2,1)S(1)}) custom-call(bf16[8,128,1024]{2,1,0:T(8,128)(2,1)S(1)} %copy-done, bf16[8,2,1024]{2,1,0:T(2,128)(2,1)S(1)} %copy-done.1, bf16[512,1536]{1,0:T(8,128)(2,1)S(1)} %copy.19.w_own, bf16[512,1536]{1,0:T(8,128)(2,1)S(1)} %collective-permute-done.w_other, f32[3,3,512]{2,1,0:T(4,128)S(1)} %copy-done.2), custom_call_target="tpu_custom_call" | custom-call | tf_op jit(solution)/shard_map/pallas_call | solution.py:151
  105.7 0.1 copy.20
  105.8 0.9 fusion.22
  106.7 0.0 copy-start.4
  106.7 0.9 convolution_add_fusion
  107.7 0.2 copy.25
  107.8 0.7 copy.26.src_ref
  108.5 13.5 %shard_map.66 = f32[16,32,256]{2,1,0:T(8,128)} custom-call(f32[32,256]{1,0:T(8,128)} %copy.26.src_ref), custom_call_target="tpu_custom_call" | custom-call | tf_op jit(solution)/shard_map/pallas_call | solution.py:312
  122.1 0.0 copy-start.7
  122.1 0.0 copy-start.11
  122.1 3.0 %copy.37 = f32[16,32,256]{1,2,0:T(8,128)} copy(f32[16,32,256]{2,1,0:T(8,128)} %shard_map.66) | data formatting | bytes 1048576
  125.0 0.0 copy-start.3
  125.0 0.0 copy-start.5
  125.1 0.0 copy-done.4
  125.1 2.0 %multiply_reduce_fusion = f32[32,16,16]{0,2,1:T(8,128)S(1)} fusion(f32[32,16,16,16]{0,3,1,2:T(8,128)} %bitcast.17, f32[32,16,16]{0,1,2:T(8,128)S(1)} %copy-done.4), kind=kLoop, calls=%fused_computation | loop fusion | flops 253952 | bytes 589824
  127.0 0.2 copy.36
  127.2 0.0 copy-done.7
  127.2 0.0 copy-done.11
  127.2 0.5 fusion.8
  127.7 0.0 copy-done.3
  127.8 0.0 copy-done.5
  127.8 0.6 fusion.3
  128.4 0.0 copy-start.10
  128.4 0.7 fusion.2
  129.1 0.2 copy.28
  129.2 0.0 copy-done.10
  129.2 0.7 multiply_convert_fusion
  (3 shorter events, 0.0 us)
Async XLA Ops:
  1.7 37.6 %copy-start.8 = (f32[32,16]{0,1:T(8,128)S(1)}, f32[32,16]{0,1:T(8,128)}, u32[]{:S(2)}) copy-start(f32[32,16]{0,1:T(8,128)} %param.9) | copy-start | bytes 6148
  1.7 37.7 %copy-start.9 = (f32[32,16]{0,1:T(8,128)S(1)}, f32[32,16]{0,1:T(8,128)}, u32[]{:S(2)}) copy-start(f32[32,16]{0,1:T(8,128)} %param.10) | copy-start | bytes 6148
  2.5 44.7 %collective-permute-start = (bf16[512,1536]{1,0:T(8,128)(2,1)S(1)}, bf16[512,1536]{1,0:T(8,128)(2,1)S(1)}, u32[]{:S(2)}, u32[]{:S(2)}) collective-permute-start(bf16[512,1536]{1,0:T(8,128)(2,1)S(1)} %copy.19.w_own), channel_id=1, source_target_pairs={{0,8},{8,0},{1,9},{9,1},{2,10},{10,2},{3,11},{11,3},{4,12},{12,4},... | collective-permute-start | bytes 4718600 | tf_op jit(solution)/shard_map/ppermute | solution.py:334
  40.5 6.7 %copy-start.6 = (f32[32,16]{1,0:T(8,128)}, f32[32,16]{1,0:T(8,128)S(1)}, u32[]{:S(2)}) copy-start(f32[32,16]{1,0:T(8,128)S(1)} %copy.21) | copy-start | bytes 6148
  40.5 6.7 %copy-start = (bf16[8,128,1024]{2,1,0:T(8,128)(2,1)S(1)}, bf16[8,128,1024]{2,1,0:T(8,128)(2,1)}, u32[]{:S(2)}) copy-start(bf16[8,128,1024]{2,1,0:T(8,128)(2,1)} %get-tuple-element.9.tok_ref) | copy-start | bytes 6291460
  40.5 6.7 %copy-start.1 = (bf16[8,2,1024]{2,1,0:T(2,128)(2,1)S(1)}, bf16[8,2,1024]{2,1,0:T(2,128)(2,1)}, u32[]{:S(2)}) copy-start(bf16[8,2,1024]{2,1,0:T(2,128)(2,1)} %get-tuple-element.10.prior_ref) | copy-start | bytes 98308
  47.2 0.7 copy-start.2
  106.7 18.3 %copy-start.4 = (f32[32,16,16]{0,1,2:T(8,128)S(1)}, f32[32,16,16]{0,1,2:T(8,128)}, u32[]{:S(2)}) copy-start(f32[32,16,16]{0,1,2:T(8,128)} %copy.38) | copy-start | bytes 98308
  122.1 5.1 %copy-start.7 = (f32[32,16]{1,0:T(8,128)S(1)}, f32[32,16]{1,0:T(8,128)}, u32[]{:S(2)}) copy-start(f32[32,16]{1,0:T(8,128)} %copy-done.6) | copy-start | bytes 6148
  122.1 5.1 %copy-start.11 = (f32[128]{0:T(128)S(1)}, f32[128]{0:T(128)}, u32[]{:S(2)}) copy-start(f32[128]{0:T(128)} %iota_add_fusion) | copy-start | bytes 1540
  125.0 2.7 %copy-start.3 = (f32[32,128,128]{2,1,0:T(8,128)S(1)}, f32[32,128,128]{2,1,0:T(8,128)}, u32[]{:S(2)}) copy-start(f32[32,128,128]{2,1,0:T(8,128)} %fusion.13) | copy-start | bytes 6291460
  125.0 2.7 %copy-start.5 = (pred[128,128]{1,0:T(8,128)(4,1)S(1)}, pred[128,128]{1,0:T(8,128)(4,1)}, u32[]{:S(2)}) copy-start(pred[128,128]{1,0:T(8,128)(4,1)} %iota_compare_fusion) | copy-start | bytes 49156
  128.4 0.8 copy-start.10

commit v10 on v9

--- a/solution.py
+++ b/solution.py
@@ -53,10 +53,12 @@
 
 
 def rs_kernel(
-    tok_ref, prior_ref, w_own, w_other, taps_ref, q_ref, g_ref, sbuf, rbuf, proj, send_sem, recv_sem
+    src_ref, w_own, w_other, taps_ref, q_ref, g_ref,
+    tok_buf, prior_buf, sbuf, rbuf, proj,
+    tsend, trecv, psend, precv, send_sem, recv_sem,
 ):
-    n, rows, _ = tok_ref.shape
-    tail = prior_ref.shape[1]
+    n, rows, _ = tok_buf.shape
+    tail = prior_buf.shape[1]
     ext_len = rows + tail
     half, width = w_own.shape
     n_ring = sbuf.shape[0]
@@ -64,20 +66,76 @@
     chip = lax.axis_index("p")
     core = lax.axis_index("c")
     col = lax.axis_index("ch")
+    other = 1 - core
     mesh_id = pl.DeviceIdType.MESH
-    rings = []
-    for cyc in CYCLES:
-        inv = [cyc.index(p) for p in range(n)]
-        r = lookup(inv, chip)
-        for d in (1, -1):
-            rings.append((cyc, d, r, lookup(cyc, (r + d + n) % n)))
-    z, y = chip // 2, chip % 2
-    n_z = n // 2
-    neighbours = (2 * ((z + 1) % n_z) + y, 2 * ((z + n_z - 1) % n_z) + y, 2 * z + 1 - y)
+    diag = chip == col
+    cyc = CYCLES[0]
+    r = lookup([cyc.index(p) for p in range(n)], chip)
+    nxt = lookup(cyc, (r + 1) % n)
+    prv = lookup(cyc, (r + n - 1) % n)
+
     barrier = pltpu.get_barrier_semaphore()
-    for nb in neighbours:
+    for k in range(n):
+        dest = (col, core, (chip + k) % n)
+        srce = ((chip + k) % n, core, chip)
+        if k == 0:
+            @pl.when(jnp.logical_not(diag))
+            def _():
+                pl.semaphore_signal(barrier, 1, device_id=dest, device_id_type=mesh_id)
+                pl.semaphore_signal(barrier, 1, device_id=srce, device_id_type=mesh_id)
+        else:
+            pl.semaphore_signal(barrier, 1, device_id=dest, device_id_type=mesh_id)
+            pl.semaphore_signal(barrier, 1, device_id=srce, device_id_type=mesh_id)
+        pl.semaphore_signal(
+            barrier, 1, device_id=(col, other, (chip + k) % n), device_id_type=mesh_id
+        )
+        pl.semaphore_signal(
+            barrier, 1, device_id=((chip + k) % n, other, chip), device_id_type=mesh_id
+        )
+    for nb in (nxt, prv):
         pl.semaphore_signal(barrier, 1, device_id=(nb, core, col), device_id_type=mesh_id)
-    pl.semaphore_wait(barrier, len(neighbours))
+    pl.semaphore_wait(barrier, 4 * n + 2 - 2 * diag.astype(jnp.int32))
+
+    slot = (chip + core) % n
+    tail_rows = src_ref.at[pl.ds(rows - tail, tail)]
+    tcopies, pcopies = [], []
+    for k in range(n):
+        dev = (col, core, (chip + k) % n)
+        copy = pltpu.make_async_remote_copy(
+            src_ref=src_ref, dst_ref=tok_buf.at[chip], send_sem=tsend.at[k],
+            recv_sem=trecv.at[chip], device_id=dev, device_id_type=mesh_id,
+        )
+        if k == 0:
+            own = pltpu.make_async_copy(src_ref, tok_buf.at[chip], trecv.at[chip])
+
+            @pl.when(diag)
+            def _():
+                own.start()
+
+            @pl.when(jnp.logical_not(diag))
+            def _():
+                copy.start()
+        else:
+            copy.start()
+        tcopies.append(copy)
+    for k in range(n):
+        pcopy = pltpu.make_async_remote_copy(
+            src_ref=tail_rows, dst_ref=prior_buf.at[slot], send_sem=psend.at[k],
+            recv_sem=precv.at[slot], device_id=(col, other, (chip + k) % n),
+            device_id_type=mesh_id,
+        )
+        pcopy.start()
+        pcopies.append(pcopy)
+
+    waited = set()
+
+    def arrive(offset):
+        if offset in waited:
+            return
+        waited.add(offset)
+        blk = lookup(cyc, (r + offset) % n)
+        pltpu.make_async_copy(src_ref, tok_buf.at[blk], trecv.at[blk]).wait()
+        pltpu.make_async_copy(tail_rows, prior_buf.at[blk], precv.at[blk]).wait()
 
     own_cols = pl.ds(pl.multiple_of(core * half, half), half)
     other_cols = pl.ds(pl.multiple_of((1 - core) * half, half), half)
@@ -88,13 +146,15 @@
                 ref[blk, :, own_cols], w_own[:, cols], preferred_element_type=jnp.float32
             ) + jnp.dot(ref[blk, :, other_cols], w_other[:, cols], preferred_element_type=jnp.float32)
 
-        return jnp.concatenate([proj_rows(tok_ref), proj_rows(prior_ref)], axis=0)
+        return jnp.concatenate([proj_rows(tok_buf), proj_rows(prior_buf)], axis=0)
 
     copies = [[] for _ in range(n_ring)]
-    order = list(range(n_ring))
     for s in range(n - 1):
-        for ring in order:
-            cyc, d, r, dest = rings[ring]
+        arrive((n - 1 - s) % n)
+        arrive((1 + s) % n)
+        for ring in range(n_ring):
+            fwd = ring < n_ring // 2
+            d, dest = (1, nxt) if fwd else (-1, prv)
             cols = pl.ds(ring * chunk, chunk)
             q = lookup(cyc, (r - d * (1 + s) + 2 * n) % n)
             if s == 0:
@@ -113,7 +173,8 @@
             )
             copy.start()
             copies[ring].append(copy)
-    for ring in order:
+    arrive(0)
+    for ring in range(n_ring):
         cols = pl.ds(ring * chunk, chunk)
         mine = part(chip, cols)
         copies[ring][-1].wait_recv()
@@ -124,7 +185,7 @@
 
     @pl.when(jnp.logical_and(chip == 0, core == 0))
     def _():
-        proj[0:2, :] = jnp.zeros((2, width), jnp.float32)
+        proj[0:tail, :] = jnp.zeros((tail, width), jnp.float32)
 
     third = width // 3
     mixed = []
@@ -137,14 +198,23 @@
         )
     q_ref[...] = mixed[0]
     g_ref[...] = (mixed[1] * mixed[2]).astype(g_ref.dtype)
-    for ring in order:
+    for ring in range(n_ring):
         for copy in copies[ring]:
             copy.wait_send()
-
-
-def project_and_gate(tok, prior, w_own, w_other, taps, n_ring=2 * len(CYCLES)):
-    n, rows, _ = tok.shape
-    ext_len = rows + prior.shape[1]
+    for k in range(n):
+        if k == 0:
+            @pl.when(jnp.logical_not(diag))
+            def _():
+                tcopies[0].wait_send()
+        else:
+            tcopies[k].wait_send()
+        pcopies[k].wait_send()
+
+
+def project_and_gate(tokens, w_own, w_other, taps, n_ring=12, tail=2):
+    rows, tok_width = tokens.shape
+    n = lax.axis_size("p")
+    ext_len = rows + tail
     width = w_own.shape[1]
     third = width // 3
     vmem = pl.BlockSpec(memory_space=pltpu.VMEM)
@@ -154,19 +224,21 @@
             jax.ShapeDtypeStruct((rows, third), jnp.float32),
             jax.ShapeDtypeStruct((rows, third), jnp.bfloat16),
         ),
-        in_specs=[vmem] * 5,
+        in_specs=[vmem] * 4,
         out_specs=(vmem, vmem),
         scratch_shapes=[
+            pltpu.VMEM((n, rows, tok_width), tokens.dtype),
+            pltpu.VMEM((n, tail, tok_width), tokens.dtype),
             pltpu.VMEM((n_ring, n - 1, ext_len, width // n_ring), jnp.bfloat16),
             pltpu.VMEM((n_ring, n - 1, ext_len, width // n_ring), jnp.bfloat16),
             pltpu.VMEM((ext_len, width), jnp.float32),
-            pltpu.SemaphoreType.DMA((n_ring, n - 1)),
-            pltpu.SemaphoreType.DMA((n_ring, n - 1)),
-        ],
+        ]
+        + [pltpu.SemaphoreType.DMA((n,))] * 4
+        + [pltpu.SemaphoreType.DMA((n_ring, n - 1))] * 2,
         compiler_params=pltpu.CompilerParams(
             collective_id=0, has_side_effects=True, vmem_limit_bytes=48 * 1024 * 1024
         ),
-    )(tok, prior, w_own, w_other, taps)
+    )(tokens, w_own, w_other, taps)
 
 
 def tok_kernel(src_ref, out_ref, prior_ref, send_sem, recv_sem, psend_sem, precv_sem):
@@ -329,10 +401,9 @@
     col = lax.axis_index("ch")
 
     n_col = lax.axis_size("ch")
-    tok_t, prior = spread_tokens(tokens, n_col)
     w_own = w_in.reshape(w_in.shape[0], -1)
     w_other = lax.ppermute(w_own, "c", [(0, 1), (1, 0)])
-    query, gated = project_and_gate(tok_t, prior, w_own, w_other, short_filter)
+    query, gated = project_and_gate(tokens, w_own, w_other, short_filter)
     x = gated.reshape(block_len, group_count, GROUP)
 
     pole_weight = residue * jnp.sqrt(2.0 * decay_rate)

time: 130 us -> 128 us (0.985)
  Pallas kernels: 107 us -> 103 us
    pallas_call x1, Pallas kernels: 57.8 us -> 93.8 us  [project_and_gate(): pl.pallas_call(rs_kernel, out_shape=(jax.ShapeDtypeStruct((rows, third),...]
    pallas_call x1 -> x0, Pallas kernels: 35.4 us -> none  [spread_tokens(): pl.pallas_call(tok_kernel, out_shape=(jax.ShapeDtypeStruct((n, rows, widt...]
    pallas_call x1, Pallas kernels: 13.5 us -> 9.5 us  [gather_earlier(): pl.pallas_call(state_kernel, out_shape=jax.ShapeDtypeStruct((n,) + state....]
    unnamed x28 -> x26, local copies, waits for them, and re-layouts: 6.32 us -> 7.27 us
  transfers between devices with their start and end apart: 1 -> 1, of which waited for: 0 -> 0; matrix products, arithmetic and copies ran while one was open for 6% -> 6% of each run, Pallas kernels for 27% -> 0%
where the time goes in v10:
time: 128 us
  Pallas kernels  103 us (80%)
  local copies, waits for them, and re-layouts  9.42 us (7%)
  matrix products  8.71 us (7%)
  other arithmetic  4.57 us (4%)
  starting transfers between devices  1.5 us (1%)
    pallas_call x1, Pallas kernels, project_and_gate(): pl.pallas_call(rs_kernel, out_shape=(jax.ShapeDtypeStruct((rows, third),...  93.8 us
    pallas_call x1, Pallas kernels, gather_earlier(): pl.pallas_call(state_kernel, out_shape=jax.ShapeDtypeStruct((n,) + state....  9.5 us
    unnamed x26, local copies, waits for them, and re-layouts  7.27 us
    dot_general x1, matrix products, local(): toep = jnp.einsum('gtr,gsr->gts', a_mat, b_mat, precision=HIGH)  4.98 us
  transfers between devices with their start and end apart: 1, of which 0 were waited for; matrix products, arithmetic and copies ran while one was open for 6% of the time, Pallas kernels for 0%

profile of v10, /device:TPU:1, one launch (start us, length us, event | category | flops | bytes accessed | tf_op | source)
XLA Modules:
  0.0 127.6 jit_solution(16595227187465021190)
XLA Ops:
  0.0 1.7 %copy.17 = bf16[512,3,512]{0,2,1:T(8,128)(2,1)S(1)} copy(bf16[512,3,512]{2,0,1:T(8,128)(2,1)} %param.7) | data formatting | bytes 3145728 | tf_op args[1]
  1.7 0.0 copy-start.7
  1.7 0.0 copy-start.8
  1.7 0.7 copy.19.w_own
  2.5 1.5 %collective-permute-start = (bf16[512,1536]{1,0:T(8,128)(2,1)S(1)}, bf16[512,1536]{1,0:T(8,128)(2,1)S(1)}, u32[]{:S(2)}, u32[]{:S(2)}) collective-permute-start(bf16[512,1536]{1,0:T(8,128)(2,1)S(1)} %copy.19.w_own), channel_id=1, source_target_pairs={{0,8},{8,0},{1,9},{9,1},{2,10},{10,2},{3,11},{11,3},{4,12},{12,4},... | collective-permute-start | bytes 4718600 | tf_op jit(solution)/shard_map/ppermute | solution.py:405
  4.0 0.0 copy-done.7
  4.0 0.1 copy.23
  4.0 0.0 copy-done.8
  4.1 0.1 copy.22
  4.2 0.1 select_bitcast_fusion
  4.3 0.8 copy.38
  5.1 0.1 copy.21
  5.1 0.0 copy-start.5
  5.1 0.6 iota_subtract_fusion
  5.7 0.5 iota_add_fusion
  6.3 0.6 iota_compare_fusion
  6.9 5.0 %fusion.13 = f32[32,128,128]{2,1,0:T(8,128)} fusion(f32[32,16]{1,0:T(8,128)S(1)} %copy.23, f32[32,16]{1,0:T(8,128)S(1)} %copy.22, f32[32,16]{1,0:T(8,128)S(1)} %copy.21), kind=kOutput, calls=%fused_computation.21 | convolution fusion | flops 100859904 | bytes 2103296 | tf_op jit(solution)/shard_map/gtr,gsr->gts/dot_general | solution.py:414
  11.9 0.0 copy-done.5
  11.9 0.0 collective-permute-done.w_other
  11.9 0.0 copy-start
  11.9 0.9 copy-done
  12.8 0.0 copy-start.1
  12.8 0.7 copy-done.1
  13.6 93.8 %shard_map.64 = (f32[128,512]{1,0:T(8,128)S(1)}, bf16[128,512]{1,0:T(8,128)(2,1)S(1)}) custom-call(bf16[128,1024]{1,0:T(8,128)(2,1)S(1)} %copy-done, bf16[512,1536]{1,0:T(8,128)(2,1)S(1)} %copy.19.w_own, bf16[512,1536]{1,0:T(8,128)(2,1)S(1)} %collective-permute-done.w_other, f32[3,3,512]{2,1,0:T(4,128)S(1)} %copy-done.1), custom_call_target="tpu_custom_call" | custom-call | tf_op jit(solution)/shard_map/pallas_call | solution.py:221
  107.3 0.1 copy.20
  107.4 0.9 fusion.22
  108.4 0.0 copy-start.3
  108.4 1.0 convolution_add_fusion
  109.4 0.2 copy.25
  109.5 0.7 copy.26.src_ref
  110.2 9.5 %shard_map.65 = f32[16,32,256]{2,1,0:T(8,128)} custom-call(f32[32,256]{1,0:T(8,128)} %copy.26.src_ref), custom_call_target="tpu_custom_call" | custom-call | tf_op jit(solution)/shard_map/pallas_call | solution.py:384
  119.7 0.0 copy-start.6
  119.7 0.0 copy-start.10
  119.8 3.0 %copy.37 = f32[16,32,256]{1,2,0:T(8,128)} copy(f32[16,32,256]{2,1,0:T(8,128)} %shard_map.65) | data formatting | bytes 1048576
  122.7 0.0 copy-start.2
  122.7 0.0 copy-start.4
  122.7 0.0 copy-done.3
  122.7 2.0 %multiply_reduce_fusion = f32[32,16,16]{0,2,1:T(8,128)S(1)} fusion(f32[32,16,16,16]{0,3,1,2:T(8,128)} %bitcast.17, f32[32,16,16]{0,1,2:T(8,128)S(1)} %copy-done.3), kind=kLoop, calls=%fused_computation | loop fusion | flops 253952 | bytes 589824
  124.7 0.2 copy.36
  124.9 0.0 copy-done.6
  124.9 0.0 copy-done.10
  124.9 0.5 fusion.8
  125.4 0.0 copy-done.2
  125.4 0.0 copy-done.4
  125.4 0.6 fusion.3
  126.1 0.0 copy-start.9
  126.1 0.7 fusion.2
  126.7 0.2 copy.28
  126.9 0.0 copy-done.9
  126.9 0.7 multiply_convert_fusion
  (3 shorter events, 0.0 us)
Async XLA Ops:
  1.7 2.2 %copy-start.7 = (f32[32,16]{0,1:T(8,128)S(1)}, f32[32,16]{0,1:T(8,128)}, u32[]{:S(2)}) copy-start(f32[32,16]{0,1:T(8,128)} %param.9) | copy-start | bytes 6148
  1.7 2.3 %copy-start.8 = (f32[32,16]{0,1:T(8,128)S(1)}, f32[32,16]{0,1:T(8,128)}, u32[]{:S(2)}) copy-start(f32[32,16]{0,1:T(8,128)} %param.10) | copy-start | bytes 6148
  2.5 9.4 %collective-permute-start = (bf16[512,1536]{1,0:T(8,128)(2,1)S(1)}, bf16[512,1536]{1,0:T(8,128)(2,1)S(1)}, u32[]{:S(2)}, u32[]{:S(2)}) collective-permute-start(bf16[512,1536]{1,0:T(8,128)(2,1)S(1)} %copy.19.w_own), channel_id=1, source_target_pairs={{0,8},{8,0},{1,9},{9,1},{2,10},{10,2},{3,11},{11,3},{4,12},{12,4},... | collective-permute-start | bytes 4718600 | tf_op jit(solution)/shard_map/ppermute | solution.py:405
  5.1 6.7 %copy-start.5 = (f32[32,16]{1,0:T(8,128)}, f32[32,16]{1,0:T(8,128)S(1)}, u32[]{:S(2)}) copy-start(f32[32,16]{1,0:T(8,128)S(1)} %copy.21) | copy-start | bytes 6148
  11.9 1.0 copy-start
  12.8 0.7 copy-start.1
  108.4 14.3 %copy-start.3 = (f32[32,16,16]{0,1,2:T(8,128)S(1)}, f32[32,16,16]{0,1,2:T(8,128)}, u32[]{:S(2)}) copy-start(f32[32,16,16]{0,1,2:T(8,128)} %copy.38) | copy-start | bytes 98308
  119.7 5.2 %copy-start.6 = (f32[32,16]{1,0:T(8,128)S(1)}, f32[32,16]{1,0:T(8,128)}, u32[]{:S(2)}) copy-start(f32[32,16]{1,0:T(8,128)} %copy-done.5) | copy-start | bytes 6148
  119.7 5.2 %copy-start.10 = (f32[128]{0:T(128)S(1)}, f32[128]{0:T(128)}, u32[]{:S(2)}) copy-start(f32[128]{0:T(128)} %iota_add_fusion) | copy-start | bytes 1540
  122.7 2.7 %copy-start.2 = (f32[32,128,128]{2,1,0:T(8,128)S(1)}, f32[32,128,128]{2,1,0:T(8,128)}, u32[]{:S(2)}) copy-start(f32[32,128,128]{2,1,0:T(8,128)} %fusion.13) | copy-start | bytes 6291460
  122.7 2.7 %copy-start.4 = (pred[128,128]{1,0:T(8,128)(4,1)S(1)}, pred[128,128]{1,0:T(8,128)(4,1)}, u32[]{:S(2)}) copy-start(pred[128,128]{1,0:T(8,128)(4,1)} %iota_compare_fusion) | copy-start | bytes 49156
  126.1 0.8 copy-start.9

commit v11 on v10

--- a/solution.py
+++ b/solution.py
@@ -336,8 +336,8 @@
     )(tokens)
 
 
-def state_kernel(src_ref, out_ref, send_sem, recv_sem):
-    n = out_ref.shape[0]
+def state_kernel(src_ref, fac_ref, out_ref, got, send_sem, recv_sem):
+    n = got.shape[0]
     n_core = lax.axis_size("c")
     me = lax.axis_index("p") * n_core + lax.axis_index("c")
     col = lax.axis_index("ch")
@@ -351,14 +351,14 @@
     for j in range(n):
         @pl.when(j >= me)
         def _():
-            out_ref[j] = jnp.zeros(out_ref.shape[1:], out_ref.dtype)
+            got[j] = jnp.zeros(got.shape[1:], got.dtype)
     pl.semaphore_wait(barrier, n - 1)
     copies = []
     for k in range(1, n):
         other = me + k
         copy = pltpu.make_async_remote_copy(
             src_ref=src_ref,
-            dst_ref=out_ref.at[me],
+            dst_ref=got.at[me],
             send_sem=send_sem.at[k],
             recv_sem=recv_sem.at[me],
             device_id=(other // n_core, other % n_core, col),
@@ -373,22 +373,31 @@
     for j in range(n):
         @pl.when(j < me)
         def _():
-            pltpu.make_async_copy(src_ref, out_ref.at[j], recv_sem.at[j]).wait()
+            pltpu.make_async_copy(src_ref, got.at[j], recv_sem.at[j]).wait()
+    acc = jnp.zeros(out_ref.shape, jnp.float32)
+    for j in range(n):
+        acc = acc + fac_ref[j] * got[j]
+    out_ref[...] = acc
     for other, copy in copies:
         @pl.when(other < n)
         def _():
             copy.wait_send()
 
 
-def gather_earlier(state, n):
+def gather_earlier(state, fac, n):
+    vmem = pl.BlockSpec(memory_space=pltpu.VMEM)
     return pl.pallas_call(
         state_kernel,
-        out_shape=jax.ShapeDtypeStruct((n,) + state.shape, state.dtype),
-        in_specs=[pl.BlockSpec(memory_space=pltpu.VMEM)],
-        out_specs=pl.BlockSpec(memory_space=pltpu.VMEM),
-        scratch_shapes=[pltpu.SemaphoreType.DMA((n,)), pltpu.SemaphoreType.DMA((n,))],
+        out_shape=jax.ShapeDtypeStruct(state.shape, state.dtype),
+        in_specs=[vmem, vmem],
+        out_specs=vmem,
+        scratch_shapes=[
+            pltpu.VMEM((n,) + state.shape, state.dtype),
+            pltpu.SemaphoreType.DMA((n,)),
+            pltpu.SemaphoreType.DMA((n,)),
+        ],
         compiler_params=pltpu.CompilerParams(collective_id=2, has_side_effects=True),
-    )(state)
+    )(state, fac)
 
 
 def local(tokens, w_in, short_filter, decay_rate, residue, skip):
@@ -411,7 +420,7 @@
     lam = decay_rate[:, None, :]
     a_mat = pole_weight[:, None, :] * jnp.exp(-lam * pos[None, :, None])
     b_mat = jnp.exp(lam * pos[None, :, None])
-    toep = jnp.einsum("gtr,gsr->gts", a_mat, b_mat, precision=HIGH)
+    toep = jnp.einsum("gtr,gsr->gts", a_mat, b_mat, precision=lax.Precision.HIGH)
     causal = pos[:, None] >= pos[None, :]
     toep = jnp.where(causal[None], toep, 0.0)
     near = dot_split("gts,sgc->tgc", toep, x)
@@ -421,11 +430,11 @@
     n_ctx = n_chip * lax.axis_size("c")
     me = chip * lax.axis_size("c") + core
     s_flat = s_loc.reshape(group_count, -1)
-    s_all = gather_earlier(s_flat, n_ctx).reshape((n_ctx,) + s_loc.shape)
     gap = (me - 1 - jnp.arange(n_ctx)).astype(jnp.float32)
     fac = jnp.exp(-decay_rate[None] * (block_len * jnp.maximum(gap, 0.0))[:, None, None])
     fac = jnp.where(gap[:, None, None] >= 0.0, fac, 0.0)
-    s_in = jnp.einsum("kgr,kgrc->grc", fac, s_all, precision=HIGH)
+    fac = jnp.broadcast_to(fac[..., None], fac.shape + (GROUP,)).reshape(n_ctx, group_count, -1)
+    s_in = gather_earlier(s_flat, fac, n_ctx).reshape(s_loc.shape)
     f_mat = pole_weight[:, None, :] * jnp.exp(-lam * (pos + 1.0)[None, :, None])
     far = jnp.einsum("gtr,grc->tgc", f_mat, s_in, precision=HIGH)
     long_out = (near + far).reshape(block_len, local_width)

time: 128 us -> 126 us (0.984)
  other arithmetic: 4.57 us -> 2.49 us
  local copies, waits for them, and re-layouts: 9.42 us -> 11 us
  matrix products: 8.71 us -> 7.16 us
    unnamed x26 -> x22, local copies, waits for them, and re-layouts: 7.27 us -> 3.51 us
    reshape x0 -> x2, local copies, waits for them, and re-layouts: none -> 3.16 us  [the longest x1 2.98 us: local(): jnp.broadcast_to(fac[..., None], fac.shape + (GROUP,))]
    unnamed x2 -> x0, other arithmetic: 2.08 us -> none
    dot_general x1, matrix products: 4.98 us -> 3.37 us  [local(): jnp.einsum('gtr,gsr->gts', a_mat, b_mat, precision=lax.Precision.HIGH)]
    broadcast_in_dim x0 -> x1, local copies, waits for them, and re-layouts: none -> 1.49 us  [local(): jnp.broadcast_to(fac[..., None], fac.shape + (GROUP,))]
  transfers between devices with their start and end apart: 1 -> 1, of which waited for: 0 -> 0; matrix products, arithmetic and copies ran while one was open for 6% -> 8% of each run, Pallas kernels for 0% -> 0%
where the time goes in v11:
time: 126 us
  Pallas kernels  103 us (82%)
  local copies, waits for them, and re-layouts  11 us (9%)
  matrix products  7.16 us (6%)
  other arithmetic  2.49 us (2%)
  starting transfers between devices  1.5 us (1%)
    pallas_call x1, Pallas kernels, project_and_gate(): pl.pallas_call(rs_kernel, out_shape=(jax.ShapeDtypeStruct((rows, third),...  93.7 us
    pallas_call x1, Pallas kernels, gather_earlier(): pl.pallas_call(state_kernel, out_shape=jax.ShapeDtypeStruct(state.shape,...  9.64 us
    unnamed x22, local copies, waits for them, and re-layouts  3.51 us
    dot_general x1, matrix products, local(): jnp.einsum('gtr,gsr->gts', a_mat, b_mat, precision=lax.Precision.HIGH)  3.37 us
    reshape x1, local copies, waits for them, and re-layouts, local(): jnp.broadcast_to(fac[..., None], fac.shape + (GROUP,))  2.98 us
  transfers between devices with their start and end apart: 1, of which 0 were waited for; matrix products, arithmetic and copies ran while one was open for 8% of the time, Pallas kernels for 0%

profile of v11, /device:TPU:1, one launch (start us, length us, event | category | flops | bytes accessed | tf_op | source)
XLA Modules:
  0.0 125.7 jit_solution(13729617148905542452)
XLA Ops:
  0.0 1.7 %copy.18 = bf16[512,3,512]{0,2,1:T(8,128)(2,1)S(1)} copy(bf16[512,3,512]{2,0,1:T(8,128)(2,1)} %param.7) | data formatting | bytes 3145728 | tf_op args[1]
  1.7 0.0 copy-start.6
  1.7 0.0 copy-start.7
  1.7 0.7 copy.20.w_own
  2.5 1.5 %collective-permute-start = (bf16[512,1536]{1,0:T(8,128)(2,1)S(1)}, bf16[512,1536]{1,0:T(8,128)(2,1)S(1)}, u32[]{:S(2)}, u32[]{:S(2)}) collective-permute-start(bf16[512,1536]{1,0:T(8,128)(2,1)S(1)} %copy.20.w_own), channel_id=1, source_target_pairs={{0,8},{8,0},{1,9},{9,1},{2,10},{10,2},{3,11},{11,3},{4,12},{12,4},... | collective-permute-start | bytes 4718600 | tf_op jit(solution)/shard_map/ppermute | solution.py:414
  4.0 0.0 copy-done.6
  4.0 0.1 copy.24
  4.0 0.0 copy-done.7
  4.1 0.1 copy.23
  4.2 0.1 exponential_select_fusion
  4.3 1.5 %broadcast_in_dim.30 = f32[16,32,16,16]{1,3,2,0:T(8,128)} broadcast(f32[16,32,16]{1,2,0:T(8,128)S(1)} %exponential_select_fusion), dimensions={0,1,2} | broadcast | bytes 557056 | tf_op jit(solution)/shard_map/broadcast_in_dim | solution.py:436
  5.8 3.0 %copy.27.fac_ref = f32[16,32,256]{2,1,0:T(8,128)} copy(f32[16,32,256]{1,2,0:T(8,128)} %bitcast.13) | data formatting | bytes 1048576 | tf_op jit(solution)/shard_map/reshape | solution.py:436
  8.7 0.1 copy.22
  8.8 0.0 copy-start.4
  8.8 0.5 iota_subtract_fusion.1
  9.3 0.5 iota_add_fusion
  9.8 0.6 iota_compare_fusion
  10.5 3.4 %fusion.13 = f32[32,128,128]{2,1,0:T(8,128)} fusion(f32[32,16]{1,0:T(8,128)S(1)} %copy.24, f32[32,16]{1,0:T(8,128)S(1)} %copy.23, f32[32,16]{1,0:T(8,128)S(1)} %copy.22), kind=kOutput, calls=%fused_computation.19 | convolution fusion | flops 50528256 | bytes 2103296 | tf_op jit(solution)/shard_map/gtr,gsr->gts/dot_general | solution.py:423
  13.8 0.0 copy-done.4
  13.8 0.0 collective-permute-done.w_other
  13.8 0.0 copy-start
  13.8 0.9 copy-done
  14.8 0.0 copy-start.1
  14.8 0.7 copy-done.1
  15.5 93.7 %shard_map.64 = (f32[128,512]{1,0:T(8,128)S(1)}, bf16[128,512]{1,0:T(8,128)(2,1)S(1)}) custom-call(bf16[128,1024]{1,0:T(8,128)(2,1)S(1)} %copy-done, bf16[512,1536]{1,0:T(8,128)(2,1)S(1)} %copy.20.w_own, bf16[512,1536]{1,0:T(8,128)(2,1)S(1)} %collective-permute-done.w_other, f32[3,3,512]{2,1,0:T(4,128)S(1)} %copy-done.1), custom_call_target="tpu_custom_call" | custom-call | tf_op jit(solution)/shard_map/pallas_call | solution.py:221
  109.3 0.0 copy-start.5
  109.3 0.0 copy-start.9
  109.3 0.0 copy-start.2
  109.3 0.0 copy-start.3
  109.3 0.1 copy.21
  109.4 1.1 fusion.22
  110.5 0.9 convolution_add_fusion
  111.4 0.2 copy.25
  111.6 0.7 copy.26.src_ref
  112.3 9.6 %shard_map.65 = f32[32,256]{1,0:T(8,128)} custom-call(f32[32,256]{1,0:T(8,128)} %copy.26.src_ref, f32[16,32,256]{2,1,0:T(8,128)} %copy.27.fac_ref), custom_call_target="tpu_custom_call" | custom-call | tf_op jit(solution)/shard_map/pallas_call | solution.py:389
  121.9 0.9 copy.28
  122.8 0.2 copy.29
  123.0 0.0 copy-done.5
  123.0 0.0 copy-done.9
  123.0 0.5 fusion.8
  123.5 0.0 copy-done.2
  123.5 0.0 copy-done.3
  123.5 0.6 fusion.3
  124.2 0.0 copy-start.8
  124.2 0.7 fusion.2
  124.8 0.2 copy.30
  125.0 0.0 copy-done.8
  125.0 0.7 multiply_convert_fusion
  (3 shorter events, 0.0 us)
Async XLA Ops:
  1.7 2.2 %copy-start.6 = (f32[32,16]{0,1:T(8,128)S(1)}, f32[32,16]{0,1:T(8,128)}, u32[]{:S(2)}) copy-start(f32[32,16]{0,1:T(8,128)} %param.9) | copy-start | bytes 6148
  1.7 2.3 %copy-start.7 = (f32[32,16]{0,1:T(8,128)S(1)}, f32[32,16]{0,1:T(8,128)}, u32[]{:S(2)}) copy-start(f32[32,16]{0,1:T(8,128)} %param.10) | copy-start | bytes 6148
  2.5 11.4 %collective-permute-start = (bf16[512,1536]{1,0:T(8,128)(2,1)S(1)}, bf16[512,1536]{1,0:T(8,128)(2,1)S(1)}, u32[]{:S(2)}, u32[]{:S(2)}) collective-permute-start(bf16[512,1536]{1,0:T(8,128)(2,1)S(1)} %copy.20.w_own), channel_id=1, source_target_pairs={{0,8},{8,0},{1,9},{9,1},{2,10},{10,2},{3,11},{11,3},{4,12},{12,4},... | collective-permute-start | bytes 4718600 | tf_op jit(solution)/shard_map/ppermute | solution.py:414
  8.8 5.0 %copy-start.4 = (f32[32,16]{1,0:T(8,128)}, f32[32,16]{1,0:T(8,128)S(1)}, u32[]{:S(2)}) copy-start(f32[32,16]{1,0:T(8,128)S(1)} %copy.22) | copy-start | bytes 6148
  13.8 1.0 copy-start
  14.8 0.7 copy-start.1
  109.3 13.7 %copy-start.5 = (f32[32,16]{1,0:T(8,128)S(1)}, f32[32,16]{1,0:T(8,128)}, u32[]{:S(2)}) copy-start(f32[32,16]{1,0:T(8,128)} %copy-done.4) | copy-start | bytes 6148
  109.3 13.7 %copy-start.9 = (f32[128]{0:T(128)S(1)}, f32[128]{0:T(128)}, u32[]{:S(2)}) copy-start(f32[128]{0:T(128)} %iota_add_fusion) | copy-start | bytes 1540
  109.3 14.2 %copy-start.2 = (f32[32,128,128]{2,1,0:T(8,128)S(1)}, f32[32,128,128]{2,1,0:T(8,128)}, u32[]{:S(2)}) copy-start(f32[32,128,128]{2,1,0:T(8,128)} %fusion.13) | copy-start | bytes 6291460
  109.3 14.2 %copy-start.3 = (pred[128,128]{1,0:T(8,128)(4,1)S(1)}, pred[128,128]{1,0:T(8,128)(4,1)}, u32[]{:S(2)}) copy-start(pred[128,128]{1,0:T(8,128)(4,1)} %iota_compare_fusion) | copy-start | bytes 49156
  124.2 0.8 copy-start.8

commit v12 on v11

--- a/solution.py
+++ b/solution.py
@@ -1,3 +1,5 @@
+import functools
+
 import jax
 import jax.numpy as jnp
 from jax import lax
@@ -336,7 +338,7 @@
     )(tokens)
 
 
-def state_kernel(src_ref, fac_ref, out_ref, got, send_sem, recv_sem):
+def state_kernel(src_ref, lam_ref, out_ref, got, fac, send_sem, recv_sem, block_len):
     n = got.shape[0]
     n_core = lax.axis_size("c")
     me = lax.axis_index("p") * n_core + lax.axis_index("c")
@@ -352,6 +354,9 @@
         @pl.when(j >= me)
         def _():
             got[j] = jnp.zeros(got.shape[1:], got.dtype)
+
+        gap = jnp.maximum(me - 1 - j, 0).astype(jnp.float32)
+        fac[j] = jnp.exp(-lam_ref[...] * (block_len * gap))
     pl.semaphore_wait(barrier, n - 1)
     copies = []
     for k in range(1, n):
@@ -376,7 +381,7 @@
             pltpu.make_async_copy(src_ref, got.at[j], recv_sem.at[j]).wait()
     acc = jnp.zeros(out_ref.shape, jnp.float32)
     for j in range(n):
-        acc = acc + fac_ref[j] * got[j]
+        acc = acc + fac[j] * got[j]
     out_ref[...] = acc
     for other, copy in copies:
         @pl.when(other < n)
@@ -384,20 +389,21 @@
             copy.wait_send()
 
 
-def gather_earlier(state, fac, n):
+def gather_earlier(state, lam, n, block_len):
     vmem = pl.BlockSpec(memory_space=pltpu.VMEM)
     return pl.pallas_call(
-        state_kernel,
+        functools.partial(state_kernel, block_len=float(block_len)),
         out_shape=jax.ShapeDtypeStruct(state.shape, state.dtype),
         in_specs=[vmem, vmem],
         out_specs=vmem,
         scratch_shapes=[
             pltpu.VMEM((n,) + state.shape, state.dtype),
+            pltpu.VMEM((n,) + state.shape, jnp.float32),
             pltpu.SemaphoreType.DMA((n,)),
             pltpu.SemaphoreType.DMA((n,)),
         ],
         compiler_params=pltpu.CompilerParams(collective_id=2, has_side_effects=True),
-    )(state, fac)
+    )(state, lam)
 
 
 def local(tokens, w_in, short_filter, decay_rate, residue, skip):
@@ -430,11 +436,9 @@
     n_ctx = n_chip * lax.axis_size("c")
     me = chip * lax.axis_size("c") + core
     s_flat = s_loc.reshape(group_count, -1)
-    gap = (me - 1 - jnp.arange(n_ctx)).astype(jnp.float32)
-    fac = jnp.exp(-decay_rate[None] * (block_len * jnp.maximum(gap, 0.0))[:, None, None])
-    fac = jnp.where(gap[:, None, None] >= 0.0, fac, 0.0)
-    fac = jnp.broadcast_to(fac[..., None], fac.shape + (GROUP,)).reshape(n_ctx, group_count, -1)
-    s_in = gather_earlier(s_flat, fac, n_ctx).reshape(s_loc.shape)
+    lam_b = jnp.broadcast_to(decay_rate[..., None], decay_rate.shape + (GROUP,))
+    s_in = gather_earlier(s_flat, lam_b.reshape(group_count, -1), n_ctx, block_len)
+    s_in = s_in.reshape(s_loc.shape)
     f_mat = pole_weight[:, None, :] * jnp.exp(-lam * (pos + 1.0)[None, :, None])
     far = jnp.einsum("gtr,grc->tgc", f_mat, s_in, precision=HIGH)
     long_out = (near + far).reshape(block_len, local_width)

time: 126 us -> 122 us (0.968)
  local copies, waits for them, and re-layouts: 11 us -> 7.22 us
    reshape x2, local copies, waits for them, and re-layouts: 3.16 us -> 0.86 us  [the longest x1 0.69 us: local(): lam_b.reshape(group_count, -1)]
    broadcast_in_dim x1, local copies, waits for them, and re-layouts: 1.49 us -> 0.01 us  [local(): lam_b = jnp.broadcast_to(decay_rate[..., None], decay_rate.shape + (GROUP,))]
  transfers between devices with their start and end apart: 1 -> 1, of which waited for: 0 -> 0; matrix products, arithmetic and copies ran while one was open for 8% -> 5% of each run, Pallas kernels for 0% -> 0%
where the time goes in v12:
time: 122 us
  Pallas kernels  103 us (84%)
  local copies, waits for them, and re-layouts  7.22 us (6%)
  matrix products  7.17 us (6%)
  other arithmetic  2.38 us (2%)
  starting transfers between devices  1.5 us (1%)
    pallas_call x1, Pallas kernels, project_and_gate(): pl.pallas_call(rs_kernel, out_shape=(jax.ShapeDtypeStruct((rows, third),...  93.8 us
    pallas_call x1, Pallas kernels, gather_earlier(): pl.pallas_call(functools.partial(state_kernel, block_len=float(block_len)...  9.33 us
    unnamed x22, local copies, waits for them, and re-layouts  3.51 us
    dot_general x1, matrix products, local(): jnp.einsum('gtr,gsr->gts', a_mat, b_mat, precision=lax.Precision.HIGH)  3.37 us
  transfers between devices with their start and end apart: 1, of which 0 were waited for; matrix products, arithmetic and copies ran while one was open for 5% of the time, Pallas kernels for 0%

profile of v12, /device:TPU:1, one launch (start us, length us, event | category | flops | bytes accessed | tf_op | source)
XLA Modules:
  0.0 121.5 jit_solution(12247328146525503827)
XLA Ops:
  0.0 1.7 %copy.18 = bf16[512,3,512]{0,2,1:T(8,128)(2,1)S(1)} copy(bf16[512,3,512]{2,0,1:T(8,128)(2,1)} %param.7) | data formatting | bytes 3145728 | tf_op args[1]
  1.7 0.0 copy-start.6
  1.7 0.0 copy-start.7
  1.7 0.7 copy.20.w_own
  2.5 1.5 %collective-permute-start = (bf16[512,1536]{1,0:T(8,128)(2,1)S(1)}, bf16[512,1536]{1,0:T(8,128)(2,1)S(1)}, u32[]{:S(2)}, u32[]{:S(2)}) collective-permute-start(bf16[512,1536]{1,0:T(8,128)(2,1)S(1)} %copy.20.w_own), channel_id=1, source_target_pairs={{0,8},{8,0},{1,9},{9,1},{2,10},{10,2},{3,11},{11,3},{4,12},{12,4},... | collective-permute-start | bytes 4718600 | tf_op jit(solution)/shard_map/ppermute | solution.py:420
  4.0 0.0 copy-done.6
  4.0 0.1 copy.24
  4.0 0.0 copy-done.7
  4.1 0.1 copy.23
  4.1 0.7 copy.27.lam_ref
  4.8 0.1 copy.22
  4.9 0.0 copy-start.4
  4.9 0.5 iota_subtract_fusion
  5.4 0.5 iota_add_fusion
  5.9 0.6 iota_compare_fusion
  6.6 3.4 %fusion.13 = f32[32,128,128]{2,1,0:T(8,128)} fusion(f32[32,16]{1,0:T(8,128)S(1)} %copy.24, f32[32,16]{1,0:T(8,128)S(1)} %copy.23, f32[32,16]{1,0:T(8,128)S(1)} %copy.22), kind=kOutput, calls=%fused_computation.19 | convolution fusion | flops 50528256 | bytes 2103296 | tf_op jit(solution)/shard_map/gtr,gsr->gts/dot_general | solution.py:429
  9.9 0.0 copy-done.4
  9.9 0.0 collective-permute-done.w_other
  9.9 0.0 copy-start
  9.9 0.9 copy-done
  10.9 0.0 copy-start.1
  10.9 0.7 copy-done.1
  11.6 93.8 %shard_map.64 = (f32[128,512]{1,0:T(8,128)S(1)}, bf16[128,512]{1,0:T(8,128)(2,1)S(1)}) custom-call(bf16[128,1024]{1,0:T(8,128)(2,1)S(1)} %copy-done, bf16[512,1536]{1,0:T(8,128)(2,1)S(1)} %copy.20.w_own, bf16[512,1536]{1,0:T(8,128)(2,1)S(1)} %collective-permute-done.w_other, f32[3,3,512]{2,1,0:T(4,128)S(1)} %copy-done.1), custom_call_target="tpu_custom_call" | custom-call | tf_op jit(solution)/shard_map/pallas_call | solution.py:223
  105.4 0.0 copy-start.5
  105.4 0.0 copy-start.9
  105.4 0.0 copy-start.2
  105.4 0.0 copy-start.3
  105.4 0.1 copy.21
  105.6 1.1 fusion.22
  106.6 0.9 convolution_add_fusion
  107.6 0.2 copy.25
  107.7 0.7 copy.26.src_ref
  108.4 9.3 %shard_map.65 = f32[32,256]{1,0:T(8,128)} custom-call(f32[32,256]{1,0:T(8,128)} %copy.26.src_ref, f32[32,256]{1,0:T(8,128)} %copy.27.lam_ref), custom_call_target="tpu_custom_call" | custom-call | tf_op jit(solution)/shard_map/pallas_call | solution.py:394
  117.8 0.9 copy.28
  118.6 0.2 copy.29
  118.8 0.0 copy-done.5
  118.8 0.0 copy-done.9
  118.8 0.5 fusion.8
  119.3 0.0 copy-done.2
  119.3 0.0 copy-done.3
  119.4 0.6 fusion.3
  120.0 0.0 copy-start.8
  120.0 0.7 fusion.2
  120.7 0.2 copy.30
  120.8 0.0 copy-done.8
  120.8 0.7 multiply_convert_fusion
  (2 shorter events, 0.0 us)
Async XLA Ops:
  1.7 2.2 %copy-start.6 = (f32[32,16]{0,1:T(8,128)S(1)}, f32[32,16]{0,1:T(8,128)}, u32[]{:S(2)}) copy-start(f32[32,16]{0,1:T(8,128)} %param.9) | copy-start | bytes 6148
  1.7 2.3 %copy-start.7 = (f32[32,16]{0,1:T(8,128)S(1)}, f32[32,16]{0,1:T(8,128)}, u32[]{:S(2)}) copy-start(f32[32,16]{0,1:T(8,128)} %param.10) | copy-start | bytes 6148
  2.5 7.5 %collective-permute-start = (bf16[512,1536]{1,0:T(8,128)(2,1)S(1)}, bf16[512,1536]{1,0:T(8,128)(2,1)S(1)}, u32[]{:S(2)}, u32[]{:S(2)}) collective-permute-start(bf16[512,1536]{1,0:T(8,128)(2,1)S(1)} %copy.20.w_own), channel_id=1, source_target_pairs={{0,8},{8,0},{1,9},{9,1},{2,10},{10,2},{3,11},{11,3},{4,12},{12,4},... | collective-permute-start | bytes 4718600 | tf_op jit(solution)/shard_map/ppermute | solution.py:420
  4.9 5.0 %copy-start.4 = (f32[32,16]{1,0:T(8,128)}, f32[32,16]{1,0:T(8,128)S(1)}, u32[]{:S(2)}) copy-start(f32[32,16]{1,0:T(8,128)S(1)} %copy.22) | copy-start | bytes 6148
  9.9 1.0 copy-start
  10.9 0.7 copy-start.1
  105.4 13.4 %copy-start.5 = (f32[32,16]{1,0:T(8,128)S(1)}, f32[32,16]{1,0:T(8,128)}, u32[]{:S(2)}) copy-start(f32[32,16]{1,0:T(8,128)} %copy-done.4) | copy-start | bytes 6148
  105.4 13.4 %copy-start.9 = (f32[128]{0:T(128)S(1)}, f32[128]{0:T(128)}, u32[]{:S(2)}) copy-start(f32[128]{0:T(128)} %iota_add_fusion) | copy-start | bytes 1540
  105.4 13.9 %copy-start.2 = (f32[32,128,128]{2,1,0:T(8,128)S(1)}, f32[32,128,128]{2,1,0:T(8,128)}, u32[]{:S(2)}) copy-start(f32[32,128,128]{2,1,0:T(8,128)} %fusion.13) | copy-start | bytes 6291460
  105.4 13.9 %copy-start.3 = (pred[128,128]{1,0:T(8,128)(4,1)S(1)}, pred[128,128]{1,0:T(8,128)(4,1)}, u32[]{:S(2)}) copy-start(pred[128,128]{1,0:T(8,128)(4,1)} %iota_compare_fusion) | copy-start | bytes 49156
  120.0 0.8 copy-start.8

commit v13 on v12

--- a/solution.py
+++ b/solution.py
@@ -55,9 +55,9 @@
 
 
 def rs_kernel(
-    src_ref, w_own, w_other, taps_ref, q_ref, g_ref,
-    tok_buf, prior_buf, sbuf, rbuf, proj,
-    tsend, trecv, psend, precv, send_sem, recv_sem,
+    src_ref, w_hbm, taps_ref, q_ref, g_ref,
+    tok_buf, prior_buf, w_own, w_other, sbuf, rbuf, proj,
+    tsend, trecv, psend, precv, send_sem, recv_sem, wsem,
 ):
     n, rows, _ = tok_buf.shape
     tail = prior_buf.shape[1]
@@ -96,7 +96,15 @@
         )
     for nb in (nxt, prv):
         pl.semaphore_signal(barrier, 1, device_id=(nb, core, col), device_id_type=mesh_id)
-    pl.semaphore_wait(barrier, 4 * n + 2 - 2 * diag.astype(jnp.int32))
+    pl.semaphore_signal(barrier, 1, device_id=(chip, other, col), device_id_type=mesh_id)
+    w_load = pltpu.make_async_copy(w_hbm, w_own, wsem.at[0])
+    w_load.start()
+    pl.semaphore_wait(barrier, 4 * n + 3 - 2 * diag.astype(jnp.int32))
+    w_swap = pltpu.make_async_remote_copy(
+        src_ref=w_hbm, dst_ref=w_other, send_sem=wsem.at[1], recv_sem=wsem.at[2],
+        device_id=(chip, other, col), device_id_type=mesh_id,
+    )
+    w_swap.start()
 
     slot = (chip + core) % n
     tail_rows = src_ref.at[pl.ds(rows - tail, tail)]
@@ -139,6 +147,8 @@
         pltpu.make_async_copy(src_ref, tok_buf.at[blk], trecv.at[blk]).wait()
         pltpu.make_async_copy(tail_rows, prior_buf.at[blk], precv.at[blk]).wait()
 
+    w_load.wait()
+    w_swap.wait_recv()
     own_cols = pl.ds(pl.multiple_of(core * half, half), half)
     other_cols = pl.ds(pl.multiple_of((1 - core) * half, half), half)
 
@@ -211,9 +221,10 @@
         else:
             tcopies[k].wait_send()
         pcopies[k].wait_send()
-
-
-def project_and_gate(tokens, w_own, w_other, taps, n_ring=12, tail=2):
+    w_swap.wait_send()
+
+
+def project_and_gate(tokens, w_own, taps, n_ring=12, tail=2):
     rows, tok_width = tokens.shape
     n = lax.axis_size("p")
     ext_len = rows + tail
@@ -226,21 +237,24 @@
             jax.ShapeDtypeStruct((rows, third), jnp.float32),
             jax.ShapeDtypeStruct((rows, third), jnp.bfloat16),
         ),
-        in_specs=[vmem] * 4,
+        in_specs=[vmem, pl.BlockSpec(memory_space=pl.ANY), vmem],
         out_specs=(vmem, vmem),
         scratch_shapes=[
             pltpu.VMEM((n, rows, tok_width), tokens.dtype),
             pltpu.VMEM((n, tail, tok_width), tokens.dtype),
+            pltpu.VMEM(w_own.shape, w_own.dtype),
+            pltpu.VMEM(w_own.shape, w_own.dtype),
             pltpu.VMEM((n_ring, n - 1, ext_len, width // n_ring), jnp.bfloat16),
             pltpu.VMEM((n_ring, n - 1, ext_len, width // n_ring), jnp.bfloat16),
             pltpu.VMEM((ext_len, width), jnp.float32),
         ]
         + [pltpu.SemaphoreType.DMA((n,))] * 4
-        + [pltpu.SemaphoreType.DMA((n_ring, n - 1))] * 2,
+        + [pltpu.SemaphoreType.DMA((n_ring, n - 1))] * 2
+        + [pltpu.SemaphoreType.DMA((3,))],
         compiler_params=pltpu.CompilerParams(
             collective_id=0, has_side_effects=True, vmem_limit_bytes=48 * 1024 * 1024
         ),
-    )(tokens, w_own, w_other, taps)
+    )(tokens, w_own, taps)
 
 
 def tok_kernel(src_ref, out_ref, prior_ref, send_sem, recv_sem, psend_sem, precv_sem):
@@ -417,8 +431,7 @@
 
     n_col = lax.axis_size("ch")
     w_own = w_in.reshape(w_in.shape[0], -1)
-    w_other = lax.ppermute(w_own, "c", [(0, 1), (1, 0)])
-    query, gated = project_and_gate(tokens, w_own, w_other, short_filter)
+    query, gated = project_and_gate(tokens, w_own, short_filter)
     x = gated.reshape(block_len, group_count, GROUP)
 
     pole_weight = residue * jnp.sqrt(2.0 * decay_rate)

time: 122 us -> 119 us (0.975)
  Pallas kernels: 103 us -> 106 us
  matrix products: 7.17 us -> 4.41 us
  other arithmetic: 2.38 us -> 0.77 us
  starting transfers between devices: 1.5 us -> 0 us
    pallas_call x1, Pallas kernels: 93.8 us -> 97.3 us  [project_and_gate(): pl.pallas_call(rs_kernel, out_shape=(jax.ShapeDtypeStruct((rows, third),...]
    ppermute x1 -> x0, starting transfers between devices: 1.5 us -> none  [local(): w_other = lax.ppermute(w_own, 'c', [(0, 1), (1, 0)])]
    dot_general x1, matrix products: 3.37 us -> 2.04 us  [local(): jnp.einsum('gtr,gsr->gts', a_mat, b_mat, precision=lax.Precision.HIGH)]
    unnamed x22 -> x12, local copies, waits for them, and re-layouts: 3.51 us -> 2.68 us
  transfers between devices with their start and end apart: 1 -> 0, of which waited for: 0 -> 0; matrix products, arithmetic and copies ran while one was open for 5% -> 0% of each run, Pallas kernels for 0% -> 0%
where the time goes in v13:
time: 119 us
  Pallas kernels  106 us (89%)
  local copies, waits for them, and re-layouts  7.41 us (6%)
  matrix products  4.41 us (4%)
    pallas_call x1, Pallas kernels, project_and_gate(): pl.pallas_call(rs_kernel, out_shape=(jax.ShapeDtypeStruct((rows, third),...  97.3 us
    pallas_call x1, Pallas kernels, gather_earlier(): pl.pallas_call(functools.partial(state_kernel, block_len=float(block_len)...  9.05 us
    unnamed x12, local copies, waits for them, and re-layouts  2.68 us

profile of v13, /device:TPU:1, one launch (start us, length us, event | category | flops | bytes accessed | tf_op | source)
XLA Modules:
  0.0 119.1 jit_solution(17038171253901399538)
XLA Ops:
  0.0 2.6 %copy.18 = bf16[512,3,512]{0,2,1:T(8,128)(2,1)} copy(bf16[512,3,512]{2,0,1:T(8,128)(2,1)} %param.7) | data formatting | bytes 3145728 | tf_op args[1]
  2.6 0.0 copy-start
  2.6 0.0 copy-start.1
  2.6 0.0 copy-start.2
  2.6 0.0 copy-start.3
  2.6 1.8 %copy.19.w_hbm = bf16[512,1536]{1,0:T(8,128)(2,1)S(1)} copy(bf16[512,1536]{0,1:T(8,128)(2,1)} %bitcast.13) | data formatting | bytes 3145728 | tf_op jit(solution)/shard_map/reshape | solution.py:433
  4.4 0.0 copy-done
  4.4 0.0 copy-done.1
  4.4 97.3 %shard_map.64 = (f32[128,512]{1,0:T(8,128)S(1)}, bf16[128,512]{1,0:T(8,128)(2,1)S(1)}) custom-call(bf16[128,1024]{1,0:T(8,128)(2,1)S(1)} %copy-done, bf16[512,1536]{1,0:T(8,128)(2,1)S(1)} %copy.19.w_hbm, f32[3,3,512]{2,1,0:T(4,128)S(1)} %copy-done.1), custom_call_target="tpu_custom_call" | custom-call | tf_op jit(solution)/shard_map/pallas_call | solution.py:234
  101.7 0.1 copy.20
  101.8 0.0 copy-done.2
  101.8 0.1 copy.23
  101.9 0.0 copy-done.3
  101.9 0.1 copy.22
  102.0 0.1 copy.21
  102.0 2.0 %fusion.11 = f32[32,128,128]{2,1,0:T(8,128)S(1)} fusion(f32[32,16]{1,0:T(8,128)S(1)} %copy.23, f32[32,16]{1,0:T(8,128)S(1)} %copy.22, f32[32,16]{1,0:T(8,128)S(1)} %copy.21), kind=kOutput, calls=%fused_computation.18 | convolution fusion | flops 50528256 | bytes 2103296 | tf_op jit(solution)/shard_map/gtr,gsr->gts/dot_general | solution.py:442
  104.1 0.6 fusion.2
  104.8 0.7 fusion.1
  105.4 0.0 copy-start.4
  105.5 0.3 fusion.19
  105.7 0.3 convolution_add_fusion.1
  106.0 0.2 copy.24
  106.2 0.7 copy.25.src_ref
  106.9 0.7 copy.26.lam_ref
  107.6 9.1 %shard_map.65 = f32[32,256]{1,0:T(8,128)} custom-call(f32[32,256]{1,0:T(8,128)} %copy.25.src_ref, f32[32,256]{1,0:T(8,128)} %copy.26.lam_ref), custom_call_target="tpu_custom_call" | custom-call | tf_op jit(solution)/shard_map/pallas_call | solution.py:408
  116.6 0.9 copy.27
  117.5 0.2 copy.28
  117.7 0.5 convolution_add_fusion
  118.2 0.1 copy.29
  118.4 0.0 copy-done.4
  118.4 0.7 multiply_convert_fusion
  (5 shorter events, 0.1 us)
Async XLA Ops:
  2.6 1.8 %copy-start = (bf16[128,1024]{1,0:T(8,128)(2,1)S(1)}, bf16[128,1024]{1,0:T(8,128)(2,1)}, u32[]{:S(2)}) copy-start(bf16[128,1024]{1,0:T(8,128)(2,1)} %src_ref.1) | copy-start | bytes 786436
  2.6 1.8 %copy-start.1 = (f32[3,3,512]{2,1,0:T(4,128)S(1)}, f32[3,3,512]{2,1,0:T(4,128)}, u32[]{:S(2)}) copy-start(f32[3,3,512]{2,1,0:T(4,128)} %taps_ref.1) | copy-start | bytes 55300
  2.6 99.2 %copy-start.2 = (f32[32,16]{0,1:T(8,128)S(1)}, f32[32,16]{0,1:T(8,128)}, u32[]{:S(2)}) copy-start(f32[32,16]{0,1:T(8,128)} %param.9) | copy-start | bytes 6148
  2.6 99.3 %copy-start.3 = (f32[32,16]{0,1:T(8,128)S(1)}, f32[32,16]{0,1:T(8,128)}, u32[]{:S(2)}) copy-start(f32[32,16]{0,1:T(8,128)} %param.10) | copy-start | bytes 6148
  105.4 12.9 %copy-start.4 = (f32[512]{0:T(512)S(1)}, f32[512]{0:T(512)}, u32[]{:S(2)}) copy-start(f32[512]{0:T(512)} %param.11) | copy-start | bytes 6148

commit v14 on v13

--- a/solution.py
+++ b/solution.py
@@ -97,14 +97,22 @@
     for nb in (nxt, prv):
         pl.semaphore_signal(barrier, 1, device_id=(nb, core, col), device_id_type=mesh_id)
     pl.semaphore_signal(barrier, 1, device_id=(chip, other, col), device_id_type=mesh_id)
-    w_load = pltpu.make_async_copy(w_hbm, w_own, wsem.at[0])
-    w_load.start()
+    n_part, part_width = w_hbm.shape[0], w_hbm.shape[2]
+    w_loads, w_swaps = [], []
+    for j in range(n_part):
+        w_cols = pl.ds(j * part_width, part_width)
+        w_loads.append(pltpu.make_async_copy(w_hbm.at[j], w_own.at[:, w_cols], wsem.at[0, j]))
+        w_loads[-1].start()
     pl.semaphore_wait(barrier, 4 * n + 3 - 2 * diag.astype(jnp.int32))
-    w_swap = pltpu.make_async_remote_copy(
-        src_ref=w_hbm, dst_ref=w_other, send_sem=wsem.at[1], recv_sem=wsem.at[2],
-        device_id=(chip, other, col), device_id_type=mesh_id,
-    )
-    w_swap.start()
+    for j in range(n_part):
+        w_cols = pl.ds(j * part_width, part_width)
+        w_swaps.append(
+            pltpu.make_async_remote_copy(
+                src_ref=w_hbm.at[j], dst_ref=w_other.at[:, w_cols], send_sem=wsem.at[1, j],
+                recv_sem=wsem.at[2, j], device_id=(chip, other, col), device_id_type=mesh_id,
+            )
+        )
+        w_swaps[-1].start()
 
     slot = (chip + core) % n
     tail_rows = src_ref.at[pl.ds(rows - tail, tail)]
@@ -147,8 +155,9 @@
         pltpu.make_async_copy(src_ref, tok_buf.at[blk], trecv.at[blk]).wait()
         pltpu.make_async_copy(tail_rows, prior_buf.at[blk], precv.at[blk]).wait()
 
-    w_load.wait()
-    w_swap.wait_recv()
+    for j in range(n_part):
+        w_loads[j].wait()
+        w_swaps[j].wait_recv()
     own_cols = pl.ds(pl.multiple_of(core * half, half), half)
     other_cols = pl.ds(pl.multiple_of((1 - core) * half, half), half)
 
@@ -221,14 +230,16 @@
         else:
             tcopies[k].wait_send()
         pcopies[k].wait_send()
-    w_swap.wait_send()
+    for j in range(n_part):
+        w_swaps[j].wait_send()
 
 
 def project_and_gate(tokens, w_own, taps, n_ring=12, tail=2):
     rows, tok_width = tokens.shape
     n = lax.axis_size("p")
     ext_len = rows + tail
-    width = w_own.shape[1]
+    n_part, half, part_width = w_own.shape
+    width = n_part * part_width
     third = width // 3
     vmem = pl.BlockSpec(memory_space=pltpu.VMEM)
     return pl.pallas_call(
@@ -242,15 +253,15 @@
         scratch_shapes=[
             pltpu.VMEM((n, rows, tok_width), tokens.dtype),
             pltpu.VMEM((n, tail, tok_width), tokens.dtype),
-            pltpu.VMEM(w_own.shape, w_own.dtype),
-            pltpu.VMEM(w_own.shape, w_own.dtype),
+            pltpu.VMEM((half, width), w_own.dtype),
+            pltpu.VMEM((half, width), w_own.dtype),
             pltpu.VMEM((n_ring, n - 1, ext_len, width // n_ring), jnp.bfloat16),
             pltpu.VMEM((n_ring, n - 1, ext_len, width // n_ring), jnp.bfloat16),
             pltpu.VMEM((ext_len, width), jnp.float32),
         ]
         + [pltpu.SemaphoreType.DMA((n,))] * 4
         + [pltpu.SemaphoreType.DMA((n_ring, n - 1))] * 2
-        + [pltpu.SemaphoreType.DMA((3,))],
+        + [pltpu.SemaphoreType.DMA((3, n_part))],
         compiler_params=pltpu.CompilerParams(
             collective_id=0, has_side_effects=True, vmem_limit_bytes=48 * 1024 * 1024
         ),
@@ -430,8 +441,8 @@
     col = lax.axis_index("ch")
 
     n_col = lax.axis_size("ch")
-    w_own = w_in.reshape(w_in.shape[0], -1)
-    query, gated = project_and_gate(tokens, w_own, short_filter)
+    w_parts = jnp.transpose(w_in, (1, 0, 2))
+    query, gated = project_and_gate(tokens, w_parts, short_filter)
     x = gated.reshape(block_len, group_count, GROUP)
 
     pole_weight = residue * jnp.sqrt(2.0 * decay_rate)

time: 119 us -> 118 us (level)
  local copies, waits for them, and re-layouts: 7.41 us -> 6.15 us
    reshape x1 -> x0, local copies, waits for them, and re-layouts: 1.76 us -> none  [local(): w_own = w_in.reshape(w_in.shape[0], -1)]
    unnamed x12 -> x13, local copies, waits for them, and re-layouts: 2.68 us -> 3.18 us
where the time goes in v14:
time: 118 us
  Pallas kernels  106 us (90%)
  local copies, waits for them, and re-layouts  6.15 us (5%)
  matrix products  4.41 us (4%)
    pallas_call x1, Pallas kernels, project_and_gate(): pl.pallas_call(rs_kernel, out_shape=(jax.ShapeDtypeStruct((rows, third),...  97 us
    pallas_call x1, Pallas kernels, gather_earlier(): pl.pallas_call(functools.partial(state_kernel, block_len=float(block_len)...  9.04 us
    unnamed x13, local copies, waits for them, and re-layouts  3.18 us

profile of v14, /device:TPU:1, one launch (start us, length us, event | category | flops | bytes accessed | tf_op | source)
XLA Modules:
  0.0 117.5 jit_solution(298246494614409388)
XLA Ops:
  0.0 0.0 copy-start
  0.0 1.4 %copy-done = bf16[512,3,512]{2,0,1:T(8,128)(2,1)S(1)} copy-done((bf16[512,3,512]{2,0,1:T(8,128)(2,1)S(1)}, bf16[512,3,512]{2,0,1:T(8,128)(2,1)}, u32[]{:S(2)}) %copy-start) | copy-done | bytes 1572888
  1.4 0.0 copy-start.1
  1.4 0.9 copy-done.1
  2.4 0.0 copy-start.2
  2.4 0.7 copy-done.2
  3.1 0.0 copy-start.3
  3.1 0.0 copy-start.4
  3.1 97.0 %shard_map.64 = (f32[128,512]{1,0:T(8,128)S(1)}, bf16[128,512]{1,0:T(8,128)(2,1)S(1)}) custom-call(bf16[128,1024]{1,0:T(8,128)(2,1)S(1)} %copy-done.1, bf16[3,512,512]{2,1,0:T(8,128)(2,1)S(1)} %bitcast.13, f32[3,3,512]{2,1,0:T(4,128)S(1)} %copy-done.2), custom_call_target="tpu_custom_call" | custom-call | tf_op jit(solution)/shard_map/pallas_call | solution.py:245
  100.2 0.1 copy.17
  100.3 0.0 copy-done.3
  100.3 0.1 copy.20
  100.4 0.0 copy-done.4
  100.4 0.1 copy.19
  100.5 0.1 copy.18
  100.5 2.0 %fusion.11 = f32[32,128,128]{2,1,0:T(8,128)S(1)} fusion(f32[32,16]{1,0:T(8,128)S(1)} %copy.20, f32[32,16]{1,0:T(8,128)S(1)} %copy.19, f32[32,16]{1,0:T(8,128)S(1)} %copy.18), kind=kOutput, calls=%fused_computation.18 | convolution fusion | flops 50528256 | bytes 2103296 | tf_op jit(solution)/shard_map/gtr,gsr->gts/dot_general | solution.py:453
  102.6 0.6 fusion.2
  103.3 0.7 fusion.1
  103.9 0.0 copy-start.5
  103.9 0.3 fusion.19
  104.2 0.3 convolution_add_fusion.1
  104.5 0.2 copy.21
  104.7 0.7 copy.22.src_ref
  105.4 0.7 copy.23.lam_ref
  106.1 9.0 %shard_map.65 = f32[32,256]{1,0:T(8,128)} custom-call(f32[32,256]{1,0:T(8,128)} %copy.22.src_ref, f32[32,256]{1,0:T(8,128)} %copy.23.lam_ref), custom_call_target="tpu_custom_call" | custom-call | tf_op jit(solution)/shard_map/pallas_call | solution.py:419
  115.1 0.9 copy.24
  116.0 0.2 copy.25
  116.2 0.5 convolution_add_fusion
  116.7 0.1 copy.26
  116.8 0.0 copy-done.5
  116.8 0.7 multiply_convert_fusion
  (5 shorter events, 0.1 us)
Async XLA Ops:
  0.0 1.4 %copy-start = (bf16[512,3,512]{2,0,1:T(8,128)(2,1)S(1)}, bf16[512,3,512]{2,0,1:T(8,128)(2,1)}, u32[]{:S(2)}) copy-start(bf16[512,3,512]{2,0,1:T(8,128)(2,1)} %param.7) | copy-start | bytes 4718596
  1.4 0.9 copy-start.1
  2.4 0.7 copy-start.2
  3.1 97.2 %copy-start.3 = (f32[32,16]{0,1:T(8,128)S(1)}, f32[32,16]{0,1:T(8,128)}, u32[]{:S(2)}) copy-start(f32[32,16]{0,1:T(8,128)} %param.9) | copy-start | bytes 6148
  3.1 97.3 %copy-start.4 = (f32[32,16]{0,1:T(8,128)S(1)}, f32[32,16]{0,1:T(8,128)}, u32[]{:S(2)}) copy-start(f32[32,16]{0,1:T(8,128)} %param.10) | copy-start | bytes 6148
  103.9 12.9 %copy-start.5 = (f32[512]{0:T(512)S(1)}, f32[512]{0:T(512)}, u32[]{:S(2)}) copy-start(f32[512]{0:T(512)} %param.11) | copy-start | bytes 6148

commit v15 on v14

--- a/solution.py
+++ b/solution.py
@@ -234,7 +234,7 @@
         w_swaps[j].wait_send()
 
 
-def project_and_gate(tokens, w_own, taps, n_ring=12, tail=2):
+def project_and_gate(tokens, w_own, taps, n_ring=6, tail=2):
     rows, tok_width = tokens.shape
     n = lax.axis_size("p")
     ext_len = rows + tail

time: 118 us -> 117 us (level)
    pallas_call x1, Pallas kernels: 97 us -> 95.4 us  [project_and_gate(): pl.pallas_call(rs_kernel, out_shape=(jax.ShapeDtypeStruct((rows, third),...]
    pallas_call x1, Pallas kernels: 9.04 us -> 10.3 us  [gather_earlier(): pl.pallas_call(functools.partial(state_kernel, block_len=float(block_len)...]
where the time goes in v15:
time: 117 us
  Pallas kernels  106 us (91%)
  local copies, waits for them, and re-layouts  6.15 us (5%)
  matrix products  4.41 us (4%)
    pallas_call x1, Pallas kernels, project_and_gate(): pl.pallas_call(rs_kernel, out_shape=(jax.ShapeDtypeStruct((rows, third),...  95.4 us
    pallas_call x1, Pallas kernels, gather_earlier(): pl.pallas_call(functools.partial(state_kernel, block_len=float(block_len)...  10.3 us
    unnamed x13, local copies, waits for them, and re-layouts  3.18 us

profile of v15, /device:TPU:1, one launch (start us, length us, event | category | flops | bytes accessed | tf_op | source)
XLA Modules:
  0.0 117.1 jit_solution(5501139054667269883)
XLA Ops:
  0.0 0.0 copy-start
  0.0 1.4 %copy-done = bf16[512,3,512]{2,0,1:T(8,128)(2,1)S(1)} copy-done((bf16[512,3,512]{2,0,1:T(8,128)(2,1)S(1)}, bf16[512,3,512]{2,0,1:T(8,128)(2,1)}, u32[]{:S(2)}) %copy-start) | copy-done | bytes 1572888
  1.4 0.0 copy-start.1
  1.4 0.9 copy-done.1
  2.4 0.0 copy-start.2
  2.4 0.7 copy-done.2
  3.1 0.0 copy-start.3
  3.1 0.0 copy-start.4
  3.1 95.4 %shard_map.64 = (f32[128,512]{1,0:T(8,128)S(1)}, bf16[128,512]{1,0:T(8,128)(2,1)S(1)}) custom-call(bf16[128,1024]{1,0:T(8,128)(2,1)S(1)} %copy-done.1, bf16[3,512,512]{2,1,0:T(8,128)(2,1)S(1)} %bitcast.13, f32[3,3,512]{2,1,0:T(4,128)S(1)} %copy-done.2), custom_call_target="tpu_custom_call" | custom-call | tf_op jit(solution)/shard_map/pallas_call | solution.py:245
  98.5 0.1 copy.17
  98.6 0.0 copy-done.3
  98.6 0.1 copy.20
  98.7 0.0 copy-done.4
  98.7 0.1 copy.19
  98.8 0.1 copy.18
  98.9 2.0 %fusion.11 = f32[32,128,128]{2,1,0:T(8,128)S(1)} fusion(f32[32,16]{1,0:T(8,128)S(1)} %copy.20, f32[32,16]{1,0:T(8,128)S(1)} %copy.19, f32[32,16]{1,0:T(8,128)S(1)} %copy.18), kind=kOutput, calls=%fused_computation.18 | convolution fusion | flops 50528256 | bytes 2103296 | tf_op jit(solution)/shard_map/gtr,gsr->gts/dot_general | solution.py:453
  100.9 0.6 fusion.2
  101.6 0.7 fusion.1
  102.2 0.0 copy-start.5
  102.3 0.3 fusion.19
  102.6 0.3 convolution_add_fusion.1
  102.8 0.2 copy.21
  103.0 0.7 copy.22.src_ref
  103.7 0.7 copy.23.lam_ref
  104.4 10.3 %shard_map.65 = f32[32,256]{1,0:T(8,128)} custom-call(f32[32,256]{1,0:T(8,128)} %copy.22.src_ref, f32[32,256]{1,0:T(8,128)} %copy.23.lam_ref), custom_call_target="tpu_custom_call" | custom-call | tf_op jit(solution)/shard_map/pallas_call | solution.py:419
  114.7 0.9 copy.24
  115.5 0.2 copy.25
  115.7 0.5 convolution_add_fusion
  116.2 0.1 copy.26
  116.4 0.0 copy-done.5
  116.4 0.7 multiply_convert_fusion
  (5 shorter events, 0.1 us)
Async XLA Ops:
  0.0 1.4 %copy-start = (bf16[512,3,512]{2,0,1:T(8,128)(2,1)S(1)}, bf16[512,3,512]{2,0,1:T(8,128)(2,1)}, u32[]{:S(2)}) copy-start(bf16[512,3,512]{2,0,1:T(8,128)(2,1)} %param.7) | copy-start | bytes 4718596
  1.4 0.9 copy-start.1
  2.4 0.7 copy-start.2
  3.1 95.5 %copy-start.3 = (f32[32,16]{0,1:T(8,128)S(1)}, f32[32,16]{0,1:T(8,128)}, u32[]{:S(2)}) copy-start(f32[32,16]{0,1:T(8,128)} %param.9) | copy-start | bytes 6148
  3.1 95.6 %copy-start.4 = (f32[32,16]{0,1:T(8,128)S(1)}, f32[32,16]{0,1:T(8,128)}, u32[]{:S(2)}) copy-start(f32[32,16]{0,1:T(8,128)} %param.10) | copy-start | bytes 6148
  102.2 14.1 %copy-start.5 = (f32[512]{0:T(512)S(1)}, f32[512]{0:T(512)}, u32[]{:S(2)}) copy-start(f32[512]{0:T(512)} %param.11) | copy-start | bytes 6148

commit v16 on v15

--- a/solution.py
+++ b/solution.py
@@ -234,7 +234,7 @@
         w_swaps[j].wait_send()
 
 
-def project_and_gate(tokens, w_own, taps, n_ring=6, tail=2):
+def project_and_gate(tokens, w_own, taps, n_ring=4, tail=2):
     rows, tok_width = tokens.shape
     n = lax.axis_size("p")
     ext_len = rows + tail

time: 117 us -> 118 us (level)
  no operation moved by 1% of the time
where the time goes in v16:
time: 118 us
  Pallas kernels  106 us (90%)
  local copies, waits for them, and re-layouts  6.15 us (5%)
  matrix products  4.41 us (4%)
    pallas_call x1, Pallas kernels, project_and_gate(): pl.pallas_call(rs_kernel, out_shape=(jax.ShapeDtypeStruct((rows, third),...  96.1 us
    pallas_call x1, Pallas kernels, gather_earlier(): pl.pallas_call(functools.partial(state_kernel, block_len=float(block_len)...  10.1 us
    unnamed x13, local copies, waits for them, and re-layouts  3.18 us

profile of v16, /device:TPU:1, one launch (start us, length us, event | category | flops | bytes accessed | tf_op | source)
XLA Modules:
  0.0 117.6 jit_solution(951158792752318194)
XLA Ops:
  0.0 0.0 copy-start
  0.0 1.4 %copy-done = bf16[512,3,512]{2,0,1:T(8,128)(2,1)S(1)} copy-done((bf16[512,3,512]{2,0,1:T(8,128)(2,1)S(1)}, bf16[512,3,512]{2,0,1:T(8,128)(2,1)}, u32[]{:S(2)}) %copy-start) | copy-done | bytes 1572888
  1.4 0.0 copy-start.1
  1.4 0.9 copy-done.1
  2.4 0.0 copy-start.2
  2.4 0.7 copy-done.2
  3.1 0.0 copy-start.3
  3.1 0.0 copy-start.4
  3.1 96.1 %shard_map.64 = (f32[128,512]{1,0:T(8,128)S(1)}, bf16[128,512]{1,0:T(8,128)(2,1)S(1)}) custom-call(bf16[128,1024]{1,0:T(8,128)(2,1)S(1)} %copy-done.1, bf16[3,512,512]{2,1,0:T(8,128)(2,1)S(1)} %bitcast.13, f32[3,3,512]{2,1,0:T(4,128)S(1)} %copy-done.2), custom_call_target="tpu_custom_call" | custom-call | tf_op jit(solution)/shard_map/pallas_call | solution.py:245
  99.2 0.1 copy.17
  99.3 0.0 copy-done.3
  99.3 0.1 copy.20
  99.4 0.0 copy-done.4
  99.4 0.1 copy.19
  99.5 0.1 copy.18
  99.6 2.0 %fusion.11 = f32[32,128,128]{2,1,0:T(8,128)S(1)} fusion(f32[32,16]{1,0:T(8,128)S(1)} %copy.20, f32[32,16]{1,0:T(8,128)S(1)} %copy.19, f32[32,16]{1,0:T(8,128)S(1)} %copy.18), kind=kOutput, calls=%fused_computation.18 | convolution fusion | flops 50528256 | bytes 2103296 | tf_op jit(solution)/shard_map/gtr,gsr->gts/dot_general | solution.py:453
  101.6 0.6 fusion.2
  102.3 0.7 fusion.1
  102.9 0.0 copy-start.5
  103.0 0.3 fusion.19
  103.3 0.3 convolution_add_fusion.1
  103.5 0.2 copy.21
  103.7 0.7 copy.22.src_ref
  104.4 0.7 copy.23.lam_ref
  105.1 10.1 %shard_map.65 = f32[32,256]{1,0:T(8,128)} custom-call(f32[32,256]{1,0:T(8,128)} %copy.22.src_ref, f32[32,256]{1,0:T(8,128)} %copy.23.lam_ref), custom_call_target="tpu_custom_call" | custom-call | tf_op jit(solution)/shard_map/pallas_call | solution.py:419
  115.2 0.9 copy.24
  116.0 0.2 copy.25
  116.2 0.5 convolution_add_fusion
  116.7 0.1 copy.26
  116.9 0.0 copy-done.5
  116.9 0.7 multiply_convert_fusion
  (5 shorter events, 0.1 us)
Async XLA Ops:
  0.0 1.4 %copy-start = (bf16[512,3,512]{2,0,1:T(8,128)(2,1)S(1)}, bf16[512,3,512]{2,0,1:T(8,128)(2,1)}, u32[]{:S(2)}) copy-start(bf16[512,3,512]{2,0,1:T(8,128)(2,1)} %param.7) | copy-start | bytes 4718596
  1.4 0.9 copy-start.1
  2.4 0.7 copy-start.2
  3.1 96.2 %copy-start.3 = (f32[32,16]{0,1:T(8,128)S(1)}, f32[32,16]{0,1:T(8,128)}, u32[]{:S(2)}) copy-start(f32[32,16]{0,1:T(8,128)} %param.9) | copy-start | bytes 6148
  3.1 96.3 %copy-start.4 = (f32[32,16]{0,1:T(8,128)S(1)}, f32[32,16]{0,1:T(8,128)}, u32[]{:S(2)}) copy-start(f32[32,16]{0,1:T(8,128)} %param.10) | copy-start | bytes 6148
  102.9 13.9 %copy-start.5 = (f32[512]{0:T(512)S(1)}, f32[512]{0:T(512)}, u32[]{:S(2)}) copy-start(f32[512]{0:T(512)} %param.11) | copy-start | bytes 6148

commit v17 on v15

--- a/solution.py
+++ b/solution.py
@@ -117,12 +117,19 @@
     slot = (chip + core) % n
     tail_rows = src_ref.at[pl.ds(rows - tail, tail)]
     tcopies, pcopies = [], []
+    half_rows = rows // 2
     for k in range(n):
         dev = (col, core, (chip + k) % n)
-        copy = pltpu.make_async_remote_copy(
-            src_ref=src_ref, dst_ref=tok_buf.at[chip], send_sem=tsend.at[k],
-            recv_sem=trecv.at[chip], device_id=dev, device_id_type=mesh_id,
-        )
+        pair = []
+        for h in range(2):
+            piece = pl.ds(h * half_rows, half_rows)
+            pair.append(
+                pltpu.make_async_remote_copy(
+                    src_ref=src_ref.at[piece], dst_ref=tok_buf.at[chip, piece],
+                    send_sem=tsend.at[k, h], recv_sem=trecv.at[chip], device_id=dev,
+                    device_id_type=mesh_id,
+                )
+            )
         if k == 0:
             own = pltpu.make_async_copy(src_ref, tok_buf.at[chip], trecv.at[chip])
 
@@ -132,10 +139,12 @@
 
             @pl.when(jnp.logical_not(diag))
             def _():
+                for copy in pair:
+                    copy.start()
+        else:
+            for copy in pair:
                 copy.start()
-        else:
-            copy.start()
-        tcopies.append(copy)
+        tcopies.append(pair)
     for k in range(n):
         pcopy = pltpu.make_async_remote_copy(
             src_ref=tail_rows, dst_ref=prior_buf.at[slot], send_sem=psend.at[k],
@@ -226,9 +235,11 @@
         if k == 0:
             @pl.when(jnp.logical_not(diag))
             def _():
-                tcopies[0].wait_send()
+                for copy in tcopies[0]:
+                    copy.wait_send()
         else:
-            tcopies[k].wait_send()
+            for copy in tcopies[k]:
+                copy.wait_send()
         pcopies[k].wait_send()
     for j in range(n_part):
         w_swaps[j].wait_send()
@@ -259,7 +270,8 @@
             pltpu.VMEM((n_ring, n - 1, ext_len, width // n_ring), jnp.bfloat16),
             pltpu.VMEM((ext_len, width), jnp.float32),
         ]
-        + [pltpu.SemaphoreType.DMA((n,))] * 4
+        + [pltpu.SemaphoreType.DMA((n, 2)), pltpu.SemaphoreType.DMA((n,))]
+        + [pltpu.SemaphoreType.DMA((n,))] * 2
         + [pltpu.SemaphoreType.DMA((n_ring, n - 1))] * 2
         + [pltpu.SemaphoreType.DMA((3, n_part))],
         compiler_params=pltpu.CompilerParams(

time: 117 us -> 117 us (level)
  no operation moved by 1% of the time
where the time goes in v17:
time: 117 us
  Pallas kernels  106 us (91%)
  local copies, waits for them, and re-layouts  6.15 us (5%)
  matrix products  4.41 us (4%)
    pallas_call x1, Pallas kernels, project_and_gate(): pl.pallas_call(rs_kernel, out_shape=(jax.ShapeDtypeStruct((rows, third),...  95.4 us
    pallas_call x1, Pallas kernels, gather_earlier(): pl.pallas_call(functools.partial(state_kernel, block_len=float(block_len)...  10.2 us
    unnamed x13, local copies, waits for them, and re-layouts  3.18 us

profile of v17, /device:TPU:1, one launch (start us, length us, event | category | flops | bytes accessed | tf_op | source)
XLA Modules:
  0.0 117.1 jit_solution(14909735885775577715)
XLA Ops:
  0.0 0.0 copy-start
  0.0 1.4 %copy-done = bf16[512,3,512]{2,0,1:T(8,128)(2,1)S(1)} copy-done((bf16[512,3,512]{2,0,1:T(8,128)(2,1)S(1)}, bf16[512,3,512]{2,0,1:T(8,128)(2,1)}, u32[]{:S(2)}) %copy-start) | copy-done | bytes 1572888
  1.4 0.0 copy-start.1
  1.4 0.9 copy-done.1
  2.4 0.0 copy-start.2
  2.4 0.7 copy-done.2
  3.1 0.0 copy-start.3
  3.1 0.0 copy-start.4
  3.1 95.4 %shard_map.64 = (f32[128,512]{1,0:T(8,128)S(1)}, bf16[128,512]{1,0:T(8,128)(2,1)S(1)}) custom-call(bf16[128,1024]{1,0:T(8,128)(2,1)S(1)} %copy-done.1, bf16[3,512,512]{2,1,0:T(8,128)(2,1)S(1)} %bitcast.13, f32[3,3,512]{2,1,0:T(4,128)S(1)} %copy-done.2), custom_call_target="tpu_custom_call" | custom-call | tf_op jit(solution)/shard_map/pallas_call | solution.py:256
  98.6 0.1 copy.17
  98.7 0.0 copy-done.3
  98.7 0.1 copy.20
  98.8 0.0 copy-done.4
  98.8 0.1 copy.19
  98.9 0.1 copy.18
  98.9 2.0 %fusion.11 = f32[32,128,128]{2,1,0:T(8,128)S(1)} fusion(f32[32,16]{1,0:T(8,128)S(1)} %copy.20, f32[32,16]{1,0:T(8,128)S(1)} %copy.19, f32[32,16]{1,0:T(8,128)S(1)} %copy.18), kind=kOutput, calls=%fused_computation.18 | convolution fusion | flops 50528256 | bytes 2103296 | tf_op jit(solution)/shard_map/gtr,gsr->gts/dot_general | solution.py:465
  101.0 0.6 fusion.2
  101.7 0.7 fusion.1
  102.3 0.0 copy-start.5
  102.3 0.3 fusion.19
  102.6 0.3 convolution_add_fusion.1
  102.9 0.2 copy.21
  103.1 0.7 copy.22.src_ref
  103.8 0.7 copy.23.lam_ref
  104.5 10.2 %shard_map.65 = f32[32,256]{1,0:T(8,128)} custom-call(f32[32,256]{1,0:T(8,128)} %copy.22.src_ref, f32[32,256]{1,0:T(8,128)} %copy.23.lam_ref), custom_call_target="tpu_custom_call" | custom-call | tf_op jit(solution)/shard_map/pallas_call | solution.py:431
  114.7 0.9 copy.24
  115.6 0.2 copy.25
  115.8 0.5 convolution_add_fusion
  116.3 0.1 copy.26
  116.4 0.0 copy-done.5
  116.4 0.7 multiply_convert_fusion
  (5 shorter events, 0.1 us)
Async XLA Ops:
  0.0 1.4 %copy-start = (bf16[512,3,512]{2,0,1:T(8,128)(2,1)S(1)}, bf16[512,3,512]{2,0,1:T(8,128)(2,1)}, u32[]{:S(2)}) copy-start(bf16[512,3,512]{2,0,1:T(8,128)(2,1)} %param.7) | copy-start | bytes 4718596
  1.4 0.9 copy-start.1
  2.4 0.7 copy-start.2
  3.1 95.6 %copy-start.3 = (f32[32,16]{0,1:T(8,128)S(1)}, f32[32,16]{0,1:T(8,128)}, u32[]{:S(2)}) copy-start(f32[32,16]{0,1:T(8,128)} %param.9) | copy-start | bytes 6148
  3.1 95.7 %copy-start.4 = (f32[32,16]{0,1:T(8,128)S(1)}, f32[32,16]{0,1:T(8,128)}, u32[]{:S(2)}) copy-start(f32[32,16]{0,1:T(8,128)} %param.10) | copy-start | bytes 6148
  102.3 14.1 %copy-start.5 = (f32[512]{0:T(512)S(1)}, f32[512]{0:T(512)}, u32[]{:S(2)}) copy-start(f32[512]{0:T(512)} %param.11) | copy-start | bytes 6148

commit v18 on v15

--- a/solution.py
+++ b/solution.py
@@ -55,9 +55,9 @@
 
 
 def rs_kernel(
-    src_ref, w_hbm, taps_ref, q_ref, g_ref,
-    tok_buf, prior_buf, w_own, w_other, sbuf, rbuf, proj,
-    tsend, trecv, psend, precv, send_sem, recv_sem, wsem,
+    src_hbm, w_hbm, taps_hbm, q_ref, g_ref,
+    src_ref, taps_ref, tok_buf, prior_buf, w_own, w_other, sbuf, rbuf, proj,
+    tsend, trecv, psend, precv, send_sem, recv_sem, wsem, lsem,
 ):
     n, rows, _ = tok_buf.shape
     tail = prior_buf.shape[1]
@@ -76,6 +76,10 @@
     nxt = lookup(cyc, (r + 1) % n)
     prv = lookup(cyc, (r + n - 1) % n)
 
+    src_load = pltpu.make_async_copy(src_hbm, src_ref, lsem.at[0])
+    src_load.start()
+    taps_load = pltpu.make_async_copy(taps_hbm, taps_ref, lsem.at[1])
+    taps_load.start()
     barrier = pltpu.get_barrier_semaphore()
     for k in range(n):
         dest = (col, core, (chip + k) % n)
@@ -104,6 +108,7 @@
         w_loads.append(pltpu.make_async_copy(w_hbm.at[j], w_own.at[:, w_cols], wsem.at[0, j]))
         w_loads[-1].start()
     pl.semaphore_wait(barrier, 4 * n + 3 - 2 * diag.astype(jnp.int32))
+    src_load.wait()
     for j in range(n_part):
         w_cols = pl.ds(j * part_width, part_width)
         w_swaps.append(
@@ -208,6 +213,8 @@
     def _():
         proj[0:tail, :] = jnp.zeros((tail, width), jnp.float32)
 
+    taps_load.wait()
+
     third = width // 3
     mixed = []
     for j in range(3):
@@ -248,9 +255,11 @@
             jax.ShapeDtypeStruct((rows, third), jnp.float32),
             jax.ShapeDtypeStruct((rows, third), jnp.bfloat16),
         ),
-        in_specs=[vmem, pl.BlockSpec(memory_space=pl.ANY), vmem],
+        in_specs=[pl.BlockSpec(memory_space=pl.ANY)] * 3,
         out_specs=(vmem, vmem),
         scratch_shapes=[
+            pltpu.VMEM(tokens.shape, tokens.dtype),
+            pltpu.VMEM(taps.shape, taps.dtype),
             pltpu.VMEM((n, rows, tok_width), tokens.dtype),
             pltpu.VMEM((n, tail, tok_width), tokens.dtype),
             pltpu.VMEM((half, width), w_own.dtype),
@@ -261,9 +270,9 @@
         ]
         + [pltpu.SemaphoreType.DMA((n,))] * 4
         + [pltpu.SemaphoreType.DMA((n_ring, n - 1))] * 2
-        + [pltpu.SemaphoreType.DMA((3, n_part))],
+        + [pltpu.SemaphoreType.DMA((3, n_part)), pltpu.SemaphoreType.DMA((2,))],
         compiler_params=pltpu.CompilerParams(
-            collective_id=0, has_side_effects=True, vmem_limit_bytes=48 * 1024 * 1024
+            collective_id=0, has_side_effects=True, vmem_limit_bytes=67043328
         ),
     )(tokens, w_own, taps)
 
@@ -277,6 +286,10 @@
     other = 1 - core
     mesh_id = pl.DeviceIdType.MESH
     diag = chip == col
+    src_load = pltpu.make_async_copy(src_hbm, src_ref, lsem.at[0])
+    src_load.start()
+    taps_load = pltpu.make_async_copy(taps_hbm, taps_ref, lsem.at[1])
+    taps_load.start()
     barrier = pltpu.get_barrier_semaphore()
     for k in range(n):
         dest = (col, core, (chip + k) % n)

time: 117 us -> 117 us (level)
  local copies, waits for them, and re-layouts: 6.15 us -> 4.66 us
    unnamed x13 -> x9, local copies, waits for them, and re-layouts: 3.18 us -> 0.79 us
where the time goes in v18:
time: 117 us
  Pallas kernels  106 us (91%)
  local copies, waits for them, and re-layouts  4.66 us (4%)
  matrix products  4.41 us (4%)
  other arithmetic  1.5 us (1%)
    pallas_call x1, Pallas kernels, project_and_gate(): pl.pallas_call(rs_kernel, out_shape=(jax.ShapeDtypeStruct((rows, third),...  96.1 us
    pallas_call x1, Pallas kernels, gather_earlier(): pl.pallas_call(functools.partial(state_kernel, block_len=float(block_len)...  10.2 us

profile of v18, /device:TPU:1, one launch (start us, length us, event | category | flops | bytes accessed | tf_op | source)
XLA Modules:
  0.0 117.0 jit_solution(12165658095111379115)
XLA Ops:
  0.0 96.1 %shard_map.64 = (f32[128,512]{1,0:T(8,128)}, bf16[128,512]{1,0:T(8,128)(2,1)}) custom-call(bf16[128,1024]{1,0:T(8,128)(2,1)} %src_hbm.1, bf16[3,512,512]{2,1,0:T(8,128)(2,1)} %bitcast.17, f32[3,3,512]{2,1,0:T(4,128)} %taps_hbm.1), custom_call_target="tpu_custom_call" | custom-call | tf_op jit(solution)/shard_map/pallas_call | solution.py:252
  96.1 1.0 copy.17
  97.1 0.8 copy.20
  97.9 0.7 sqrt_multiply_fusion
  98.6 0.1 copy.19
  98.7 0.1 copy.18
  98.8 2.0 %fusion.11 = f32[32,128,128]{2,1,0:T(8,128)S(1)} fusion(f32[32,16]{1,0:T(8,128)S(1)} %copy.20, f32[32,16]{1,0:T(8,128)S(1)} %copy.19, f32[32,16]{1,0:T(8,128)S(1)} %copy.18), kind=kOutput, calls=%fused_computation.18 | convolution fusion | flops 50528256 | bytes 2103296 | tf_op jit(solution)/shard_map/gtr,gsr->gts/dot_general | solution.py:466
  100.8 0.6 fusion.2
  101.5 0.0 copy-start.2
  101.5 0.7 fusion.1
  102.1 0.0 copy-start
  102.1 0.0 copy-start.1
  102.2 0.0 copy-start.3
  102.2 0.3 fusion.19
  102.5 0.3 convolution_add_fusion.1
  102.8 0.2 copy.21
  102.9 0.7 copy.22.src_ref
  103.6 0.0 copy-done.2
  103.6 0.7 copy.23.lam_ref
  104.3 10.2 %shard_map.65 = f32[32,256]{1,0:T(8,128)} custom-call(f32[32,256]{1,0:T(8,128)} %copy.22.src_ref, f32[32,256]{1,0:T(8,128)} %copy.23.lam_ref), custom_call_target="tpu_custom_call" | custom-call | tf_op jit(solution)/shard_map/pallas_call | solution.py:432
  114.5 0.9 copy.24
  115.4 0.2 copy.25
  115.6 0.5 convolution_add_fusion
  116.1 0.1 copy.26
  116.2 0.0 copy-done
  116.2 0.0 copy-done.1
  116.3 0.0 copy-done.3
  116.3 0.7 multiply_convert_fusion
  (4 shorter events, 0.1 us)
Async XLA Ops:
  101.5 2.1 %copy-start.2 = (f32[32,16]{0,1:T(8,128)S(1)}, f32[32,16]{0,1:T(8,128)}, u32[]{:S(2)}) copy-start(f32[32,16]{0,1:T(8,128)} %param.9) | copy-start | bytes 6148
  102.1 14.1 %copy-start = (bf16[128,512]{1,0:T(8,128)(2,1)S(1)}, bf16[128,512]{1,0:T(8,128)(2,1)}, u32[]{:S(2)}) copy-start(bf16[128,512]{1,0:T(8,128)(2,1)} %get-tuple-element.8) | copy-start | bytes 393220
  102.1 14.1 %copy-start.1 = (f32[128,512]{1,0:T(8,128)S(1)}, f32[128,512]{1,0:T(8,128)}, u32[]{:S(2)}) copy-start(f32[128,512]{1,0:T(8,128)} %get-tuple-element.7) | copy-start | bytes 786436
  102.2 14.1 %copy-start.3 = (f32[512]{0:T(512)S(1)}, f32[512]{0:T(512)}, u32[]{:S(2)}) copy-start(f32[512]{0:T(512)} %param.11) | copy-start | bytes 6148

commit v19 on v18

--- a/solution.py
+++ b/solution.py
@@ -123,6 +123,14 @@
     tail_rows = src_ref.at[pl.ds(rows - tail, tail)]
     tcopies, pcopies = [], []
     for k in range(n):
+        pcopy = pltpu.make_async_remote_copy(
+            src_ref=tail_rows, dst_ref=prior_buf.at[slot], send_sem=psend.at[k],
+            recv_sem=precv.at[slot], device_id=(col, other, (chip + k) % n),
+            device_id_type=mesh_id,
+        )
+        pcopy.start()
+        pcopies.append(pcopy)
+    for k in range(n):
         dev = (col, core, (chip + k) % n)
         copy = pltpu.make_async_remote_copy(
             src_ref=src_ref, dst_ref=tok_buf.at[chip], send_sem=tsend.at[k],
@@ -141,14 +149,6 @@
         else:
             copy.start()
         tcopies.append(copy)
-    for k in range(n):
-        pcopy = pltpu.make_async_remote_copy(
-            src_ref=tail_rows, dst_ref=prior_buf.at[slot], send_sem=psend.at[k],
-            recv_sem=precv.at[slot], device_id=(col, other, (chip + k) % n),
-            device_id_type=mesh_id,
-        )
-        pcopy.start()
-        pcopies.append(pcopy)
 
     waited = set()
 

time: 117 us -> 112 us (0.957)
  the two profiles are of different devices: /device:TPU:1 before, /device:TPU:22 now
where the time goes in v19:
time: 112 us
  Pallas kernels  101 us (90%)
  local copies, waits for them, and re-layouts  4.66 us (4%)
  matrix products  4.41 us (4%)
  other arithmetic  1.5 us (1%)
    pallas_call x1, Pallas kernels, project_and_gate(): pl.pallas_call(rs_kernel, out_shape=(jax.ShapeDtypeStruct((rows, third),...  89.7 us
    pallas_call x1, Pallas kernels, gather_earlier(): pl.pallas_call(functools.partial(state_kernel, block_len=float(block_len)...  11.5 us

profile of v19, /device:TPU:22, one launch (start us, length us, event | category | flops | bytes accessed | tf_op | source)
XLA Modules:
  0.0 111.8 jit_solution(18952650960624300)
XLA Ops:
  0.0 89.7 %shard_map.64 = (f32[128,512]{1,0:T(8,128)}, bf16[128,512]{1,0:T(8,128)(2,1)}) custom-call(bf16[128,1024]{1,0:T(8,128)(2,1)} %src_hbm.1, bf16[3,512,512]{2,1,0:T(8,128)(2,1)} %bitcast.17, f32[3,3,512]{2,1,0:T(4,128)} %taps_hbm.1), custom_call_target="tpu_custom_call" | custom-call | tf_op jit(solution)/shard_map/pallas_call | solution.py:252
  89.7 1.0 copy.17
  90.7 0.8 copy.20
  91.5 0.7 sqrt_multiply_fusion
  92.2 0.1 copy.19
  92.3 0.1 copy.18
  92.3 2.0 %fusion.11 = f32[32,128,128]{2,1,0:T(8,128)S(1)} fusion(f32[32,16]{1,0:T(8,128)S(1)} %copy.20, f32[32,16]{1,0:T(8,128)S(1)} %copy.19, f32[32,16]{1,0:T(8,128)S(1)} %copy.18), kind=kOutput, calls=%fused_computation.18 | convolution fusion | flops 50528256 | bytes 2103296 | tf_op jit(solution)/shard_map/gtr,gsr->gts/dot_general | solution.py:466
  94.4 0.6 fusion.2
  95.1 0.0 copy-start.2
  95.1 0.7 fusion.1
  95.7 0.0 copy-start
  95.7 0.0 copy-start.1
  95.7 0.0 copy-start.3
  95.8 0.3 fusion.19
  96.0 0.3 convolution_add_fusion.1
  96.3 0.2 copy.21
  96.5 0.7 copy.22.src_ref
  97.2 0.0 copy-done.2
  97.2 0.7 copy.23.lam_ref
  97.9 11.5 %shard_map.65 = f32[32,256]{1,0:T(8,128)} custom-call(f32[32,256]{1,0:T(8,128)} %copy.22.src_ref, f32[32,256]{1,0:T(8,128)} %copy.23.lam_ref), custom_call_target="tpu_custom_call" | custom-call | tf_op jit(solution)/shard_map/pallas_call | solution.py:432
  109.4 0.9 copy.24
  110.3 0.2 copy.25
  110.5 0.5 convolution_add_fusion
  111.0 0.1 copy.26
  111.1 0.0 copy-done
  111.1 0.0 copy-done.1
  111.1 0.0 copy-done.3
  111.1 0.7 multiply_convert_fusion
  (4 shorter events, 0.1 us)
Async XLA Ops:
  95.1 2.1 %copy-start.2 = (f32[32,16]{0,1:T(8,128)S(1)}, f32[32,16]{0,1:T(8,128)}, u32[]{:S(2)}) copy-start(f32[32,16]{0,1:T(8,128)} %param.9) | copy-start | bytes 6148
  95.7 15.4 %copy-start = (bf16[128,512]{1,0:T(8,128)(2,1)S(1)}, bf16[128,512]{1,0:T(8,128)(2,1)}, u32[]{:S(2)}) copy-start(bf16[128,512]{1,0:T(8,128)(2,1)} %get-tuple-element.8) | copy-start | bytes 393220
  95.7 15.4 %copy-start.1 = (f32[128,512]{1,0:T(8,128)S(1)}, f32[128,512]{1,0:T(8,128)}, u32[]{:S(2)}) copy-start(f32[128,512]{1,0:T(8,128)} %get-tuple-element.7) | copy-start | bytes 786436
  95.7 15.4 %copy-start.3 = (f32[512]{0:T(512)S(1)}, f32[512]{0:T(512)}, u32[]{:S(2)}) copy-start(f32[512]{0:T(512)} %param.11) | copy-start | bytes 6148

commit v20 on v19

--- a/solution.py
+++ b/solution.py
@@ -109,6 +109,37 @@
         w_loads[-1].start()
     pl.semaphore_wait(barrier, 4 * n + 3 - 2 * diag.astype(jnp.int32))
     src_load.wait()
+    slot = (chip + core) % n
+    tail_rows = src_ref.at[pl.ds(rows - tail, tail)]
+    tcopies, pcopies = [], []
+    for k in range(n):
+        pcopy = pltpu.make_async_remote_copy(
+            src_ref=tail_rows, dst_ref=prior_buf.at[slot], send_sem=psend.at[k],
+            recv_sem=precv.at[slot], device_id=(col, other, (chip + k) % n),
+            device_id_type=mesh_id,
+        )
+        pcopy.start()
+        pcopies.append(pcopy)
+    for k in range(n):
+        dev = (col, core, (chip + k) % n)
+        copy = pltpu.make_async_remote_copy(
+            src_ref=src_ref, dst_ref=tok_buf.at[chip], send_sem=tsend.at[k],
+            recv_sem=trecv.at[chip], device_id=dev, device_id_type=mesh_id,
+        )
+        if k == 0:
+            own = pltpu.make_async_copy(src_ref, tok_buf.at[chip], trecv.at[chip])
+
+            @pl.when(diag)
+            def _():
+                own.start()
+
+            @pl.when(jnp.logical_not(diag))
+            def _():
+                copy.start()
+        else:
+            copy.start()
+        tcopies.append(copy)
+
     for j in range(n_part):
         w_cols = pl.ds(j * part_width, part_width)
         w_swaps.append(
@@ -118,37 +149,6 @@
             )
         )
         w_swaps[-1].start()
-
-    slot = (chip + core) % n
-    tail_rows = src_ref.at[pl.ds(rows - tail, tail)]
-    tcopies, pcopies = [], []
-    for k in range(n):
-        pcopy = pltpu.make_async_remote_copy(
-            src_ref=tail_rows, dst_ref=prior_buf.at[slot], send_sem=psend.at[k],
-            recv_sem=precv.at[slot], device_id=(col, other, (chip + k) % n),
-            device_id_type=mesh_id,
-        )
-        pcopy.start()
-        pcopies.append(pcopy)
-    for k in range(n):
-        dev = (col, core, (chip + k) % n)
-        copy = pltpu.make_async_remote_copy(
-            src_ref=src_ref, dst_ref=tok_buf.at[chip], send_sem=tsend.at[k],
-            recv_sem=trecv.at[chip], device_id=dev, device_id_type=mesh_id,
-        )
-        if k == 0:
-            own = pltpu.make_async_copy(src_ref, tok_buf.at[chip], trecv.at[chip])
-
-            @pl.when(diag)
-            def _():
-                own.start()
-
-            @pl.when(jnp.logical_not(diag))
-            def _():
-                copy.start()
-        else:
-            copy.start()
-        tcopies.append(copy)
 
     waited = set()
 

time: 112 us -> 112 us (level)
  no operation moved by 1% of the time
where the time goes in v20:
time: 112 us
  Pallas kernels  101 us (90%)
  local copies, waits for them, and re-layouts  4.66 us (4%)
  matrix products  4.41 us (4%)
  other arithmetic  1.5 us (1%)
    pallas_call x1, Pallas kernels, project_and_gate(): pl.pallas_call(rs_kernel, out_shape=(jax.ShapeDtypeStruct((rows, third),...  89.7 us
    pallas_call x1, Pallas kernels, gather_earlier(): pl.pallas_call(functools.partial(state_kernel, block_len=float(block_len)...  11.5 us

profile of v20, /device:TPU:22, one launch (start us, length us, event | category | flops | bytes accessed | tf_op | source)
XLA Modules:
  0.0 111.8 jit_solution(2302748669104747181)
XLA Ops:
  0.0 89.7 %shard_map.64 = (f32[128,512]{1,0:T(8,128)}, bf16[128,512]{1,0:T(8,128)(2,1)}) custom-call(bf16[128,1024]{1,0:T(8,128)(2,1)} %src_hbm.1, bf16[3,512,512]{2,1,0:T(8,128)(2,1)} %bitcast.17, f32[3,3,512]{2,1,0:T(4,128)} %taps_hbm.1), custom_call_target="tpu_custom_call" | custom-call | tf_op jit(solution)/shard_map/pallas_call | solution.py:252
  89.7 1.0 copy.17
  90.7 0.8 copy.20
  91.5 0.7 sqrt_multiply_fusion
  92.2 0.1 copy.19
  92.3 0.1 copy.18
  92.3 2.0 %fusion.11 = f32[32,128,128]{2,1,0:T(8,128)S(1)} fusion(f32[32,16]{1,0:T(8,128)S(1)} %copy.20, f32[32,16]{1,0:T(8,128)S(1)} %copy.19, f32[32,16]{1,0:T(8,128)S(1)} %copy.18), kind=kOutput, calls=%fused_computation.18 | convolution fusion | flops 50528256 | bytes 2103296 | tf_op jit(solution)/shard_map/gtr,gsr->gts/dot_general | solution.py:466
  94.4 0.6 fusion.2
  95.1 0.0 copy-start.2
  95.1 0.7 fusion.1
  95.7 0.0 copy-start
  95.7 0.0 copy-start.1
  95.7 0.0 copy-start.3
  95.8 0.3 fusion.19
  96.0 0.3 convolution_add_fusion.1
  96.3 0.2 copy.21
  96.5 0.7 copy.22.src_ref
  97.2 0.0 copy-done.2
  97.2 0.7 copy.23.lam_ref
  97.9 11.5 %shard_map.65 = f32[32,256]{1,0:T(8,128)} custom-call(f32[32,256]{1,0:T(8,128)} %copy.22.src_ref, f32[32,256]{1,0:T(8,128)} %copy.23.lam_ref), custom_call_target="tpu_custom_call" | custom-call | tf_op jit(solution)/shard_map/pallas_call | solution.py:432
  109.4 0.9 copy.24
  110.3 0.2 copy.25
  110.5 0.5 convolution_add_fusion
  111.0 0.1 copy.26
  111.1 0.0 copy-done
  111.1 0.0 copy-done.1
  111.1 0.0 copy-done.3
  111.1 0.7 multiply_convert_fusion
  (4 shorter events, 0.1 us)
Async XLA Ops:
  95.1 2.1 %copy-start.2 = (f32[32,16]{0,1:T(8,128)S(1)}, f32[32,16]{0,1:T(8,128)}, u32[]{:S(2)}) copy-start(f32[32,16]{0,1:T(8,128)} %param.9) | copy-start | bytes 6148
  95.7 15.4 %copy-start = (bf16[128,512]{1,0:T(8,128)(2,1)S(1)}, bf16[128,512]{1,0:T(8,128)(2,1)}, u32[]{:S(2)}) copy-start(bf16[128,512]{1,0:T(8,128)(2,1)} %get-tuple-element.8) | copy-start | bytes 393220
  95.7 15.4 %copy-start.1 = (f32[128,512]{1,0:T(8,128)S(1)}, f32[128,512]{1,0:T(8,128)}, u32[]{:S(2)}) copy-start(f32[128,512]{1,0:T(8,128)} %get-tuple-element.7) | copy-start | bytes 786436
  95.7 15.4 %copy-start.3 = (f32[512]{0:T(512)S(1)}, f32[512]{0:T(512)}, u32[]{:S(2)}) copy-start(f32[512]{0:T(512)} %param.11) | copy-start | bytes 6148

commit v21 on v20

--- a/solution.py
+++ b/solution.py
@@ -120,13 +120,15 @@
         )
         pcopy.start()
         pcopies.append(pcopy)
-    for k in range(n):
-        dev = (col, core, (chip + k) % n)
+    n_x = n // 2
+    far_first = [(dy, dx) for dy in (1, 0) for dx in (2, 1, 3, 0)]
+    for k, (dy, dx) in enumerate(far_first):
+        dev = (col, core, ((col // n_x + dy) % 2) * n_x + (col % n_x + dx) % n_x)
         copy = pltpu.make_async_remote_copy(
             src_ref=src_ref, dst_ref=tok_buf.at[chip], send_sem=tsend.at[k],
             recv_sem=trecv.at[chip], device_id=dev, device_id_type=mesh_id,
         )
-        if k == 0:
+        if k == n - 1:
             own = pltpu.make_async_copy(src_ref, tok_buf.at[chip], trecv.at[chip])
 
             @pl.when(diag)
@@ -230,10 +232,10 @@
         for copy in copies[ring]:
             copy.wait_send()
     for k in range(n):
-        if k == 0:
+        if k == n - 1:
             @pl.when(jnp.logical_not(diag))
             def _():
-                tcopies[0].wait_send()
+                tcopies[k].wait_send()
         else:
             tcopies[k].wait_send()
         pcopies[k].wait_send()

time: 112 us -> 125 us (1.12)
  the two profiles are of different devices: /device:TPU:22 before, /device:TPU:2 now
where the time goes in v21:
time: 125 us
  Pallas kernels  114 us (91%)
  local copies, waits for them, and re-layouts  4.66 us (4%)
  matrix products  4.41 us (4%)
  other arithmetic  1.5 us (1%)
    pallas_call x1, Pallas kernels, project_and_gate(): pl.pallas_call(rs_kernel, out_shape=(jax.ShapeDtypeStruct((rows, third),...  103 us
    pallas_call x1, Pallas kernels, gather_earlier(): pl.pallas_call(functools.partial(state_kernel, block_len=float(block_len)...  11.5 us

profile of v21, /device:TPU:2, one launch (start us, length us, event | category | flops | bytes accessed | tf_op | source)
XLA Modules:
  0.0 124.7 jit_solution(16384040950608395729)
XLA Ops:
  0.0 102.5 %shard_map.64 = (f32[128,512]{1,0:T(8,128)}, bf16[128,512]{1,0:T(8,128)(2,1)}) custom-call(bf16[128,1024]{1,0:T(8,128)(2,1)} %src_hbm.1, bf16[3,512,512]{2,1,0:T(8,128)(2,1)} %bitcast.17, f32[3,3,512]{2,1,0:T(4,128)} %taps_hbm.1), custom_call_target="tpu_custom_call" | custom-call | tf_op jit(solution)/shard_map/pallas_call | solution.py:254
  102.6 1.0 copy.17
  103.6 0.8 copy.20
  104.4 0.7 sqrt_multiply_fusion
  105.1 0.1 copy.19
  105.2 0.1 copy.18
  105.2 2.0 %fusion.11 = f32[32,128,128]{2,1,0:T(8,128)S(1)} fusion(f32[32,16]{1,0:T(8,128)S(1)} %copy.20, f32[32,16]{1,0:T(8,128)S(1)} %copy.19, f32[32,16]{1,0:T(8,128)S(1)} %copy.18), kind=kOutput, calls=%fused_computation.18 | convolution fusion | flops 50528256 | bytes 2103296 | tf_op jit(solution)/shard_map/gtr,gsr->gts/dot_general | solution.py:468
  107.3 0.6 fusion.2
  108.0 0.0 copy-start.2
  108.0 0.7 fusion.1
  108.6 0.0 copy-start
  108.6 0.0 copy-start.1
  108.6 0.0 copy-start.3
  108.7 0.3 fusion.19
  108.9 0.3 convolution_add_fusion.1
  109.2 0.2 copy.21
  109.4 0.7 copy.22.src_ref
  110.1 0.0 copy-done.2
  110.1 0.7 copy.23.lam_ref
  110.8 11.5 %shard_map.65 = f32[32,256]{1,0:T(8,128)} custom-call(f32[32,256]{1,0:T(8,128)} %copy.22.src_ref, f32[32,256]{1,0:T(8,128)} %copy.23.lam_ref), custom_call_target="tpu_custom_call" | custom-call | tf_op jit(solution)/shard_map/pallas_call | solution.py:434
  122.3 0.9 copy.24
  123.1 0.2 copy.25
  123.3 0.5 convolution_add_fusion
  123.8 0.1 copy.26
  124.0 0.0 copy-done
  124.0 0.0 copy-done.1
  124.0 0.0 copy-done.3
  124.0 0.7 multiply_convert_fusion
  (4 shorter events, 0.1 us)
Async XLA Ops:
  108.0 2.1 %copy-start.2 = (f32[32,16]{0,1:T(8,128)S(1)}, f32[32,16]{0,1:T(8,128)}, u32[]{:S(2)}) copy-start(f32[32,16]{0,1:T(8,128)} %param.9) | copy-start | bytes 6148
  108.6 15.4 %copy-start = (bf16[128,512]{1,0:T(8,128)(2,1)S(1)}, bf16[128,512]{1,0:T(8,128)(2,1)}, u32[]{:S(2)}) copy-start(bf16[128,512]{1,0:T(8,128)(2,1)} %get-tuple-element.8) | copy-start | bytes 393220
  108.6 15.4 %copy-start.1 = (f32[128,512]{1,0:T(8,128)S(1)}, f32[128,512]{1,0:T(8,128)}, u32[]{:S(2)}) copy-start(f32[128,512]{1,0:T(8,128)} %get-tuple-element.7) | copy-start | bytes 786436
  108.6 15.4 %copy-start.3 = (f32[512]{0:T(512)S(1)}, f32[512]{0:T(512)}, u32[]{:S(2)}) copy-start(f32[512]{0:T(512)} %param.11) | copy-start | bytes 6148

commit v22 on v21

--- a/solution.py
+++ b/solution.py
@@ -121,14 +121,14 @@
         pcopy.start()
         pcopies.append(pcopy)
     n_x = n // 2
-    far_first = [(dy, dx) for dy in (1, 0) for dx in (2, 1, 3, 0)]
-    for k, (dy, dx) in enumerate(far_first):
+    near_first = [(dy, dx) for dy in (0, 1) for dx in (0, 1, 3, 2)]
+    for k, (dy, dx) in enumerate(near_first):
         dev = (col, core, ((col // n_x + dy) % 2) * n_x + (col % n_x + dx) % n_x)
         copy = pltpu.make_async_remote_copy(
             src_ref=src_ref, dst_ref=tok_buf.at[chip], send_sem=tsend.at[k],
             recv_sem=trecv.at[chip], device_id=dev, device_id_type=mesh_id,
         )
-        if k == n - 1:
+        if k == 0:
             own = pltpu.make_async_copy(src_ref, tok_buf.at[chip], trecv.at[chip])
 
             @pl.when(diag)
@@ -232,7 +232,7 @@
         for copy in copies[ring]:
             copy.wait_send()
     for k in range(n):
-        if k == n - 1:
+        if k == 0:
             @pl.when(jnp.logical_not(diag))
             def _():
                 tcopies[k].wait_send()

time: 125 us -> 122 us (0.976)
  the two profiles are of different devices: /device:TPU:2 before, /device:TPU:1 now
where the time goes in v22:
time: 122 us
  Pallas kernels  111 us (91%)
  local copies, waits for them, and re-layouts  4.66 us (4%)
  matrix products  4.41 us (4%)
  other arithmetic  1.5 us (1%)
    pallas_call x1, Pallas kernels, project_and_gate(): pl.pallas_call(rs_kernel, out_shape=(jax.ShapeDtypeStruct((rows, third),...  96.8 us
    pallas_call x1, Pallas kernels, gather_earlier(): pl.pallas_call(functools.partial(state_kernel, block_len=float(block_len)...  14.6 us

profile of v22, /device:TPU:1, one launch (start us, length us, event | category | flops | bytes accessed | tf_op | source)
XLA Modules:
  0.0 122.1 jit_solution(7057138107326652093)
XLA Ops:
  0.0 96.8 %shard_map.64 = (f32[128,512]{1,0:T(8,128)}, bf16[128,512]{1,0:T(8,128)(2,1)}) custom-call(bf16[128,1024]{1,0:T(8,128)(2,1)} %src_hbm.1, bf16[3,512,512]{2,1,0:T(8,128)(2,1)} %bitcast.17, f32[3,3,512]{2,1,0:T(4,128)} %taps_hbm.1), custom_call_target="tpu_custom_call" | custom-call | tf_op jit(solution)/shard_map/pallas_call | solution.py:254
  96.8 1.0 copy.17
  97.8 0.8 copy.20
  98.6 0.7 sqrt_multiply_fusion
  99.3 0.1 copy.19
  99.4 0.1 copy.18
  99.5 2.0 %fusion.11 = f32[32,128,128]{2,1,0:T(8,128)S(1)} fusion(f32[32,16]{1,0:T(8,128)S(1)} %copy.20, f32[32,16]{1,0:T(8,128)S(1)} %copy.19, f32[32,16]{1,0:T(8,128)S(1)} %copy.18), kind=kOutput, calls=%fused_computation.18 | convolution fusion | flops 50528256 | bytes 2103296 | tf_op jit(solution)/shard_map/gtr,gsr->gts/dot_general | solution.py:468
  101.5 0.6 fusion.2
  102.2 0.0 copy-start.2
  102.2 0.7 fusion.1
  102.8 0.0 copy-start
  102.8 0.0 copy-start.1
  102.8 0.0 copy-start.3
  102.9 0.3 fusion.19
  103.2 0.3 convolution_add_fusion.1
  103.4 0.2 copy.21
  103.6 0.7 copy.22.src_ref
  104.3 0.0 copy-done.2
  104.3 0.7 copy.23.lam_ref
  105.0 14.6 %shard_map.65 = f32[32,256]{1,0:T(8,128)} custom-call(f32[32,256]{1,0:T(8,128)} %copy.22.src_ref, f32[32,256]{1,0:T(8,128)} %copy.23.lam_ref), custom_call_target="tpu_custom_call" | custom-call | tf_op jit(solution)/shard_map/pallas_call | solution.py:434
  119.6 0.9 copy.24
  120.5 0.2 copy.25
  120.7 0.5 convolution_add_fusion
  121.2 0.1 copy.26
  121.3 0.0 copy-done
  121.4 0.0 copy-done.1
  121.4 0.0 copy-done.3
  121.4 0.7 multiply_convert_fusion
  (4 shorter events, 0.1 us)
Async XLA Ops:
  102.2 2.1 %copy-start.2 = (f32[32,16]{0,1:T(8,128)S(1)}, f32[32,16]{0,1:T(8,128)}, u32[]{:S(2)}) copy-start(f32[32,16]{0,1:T(8,128)} %param.9) | copy-start | bytes 6148
  102.8 18.5 %copy-start = (bf16[128,512]{1,0:T(8,128)(2,1)S(1)}, bf16[128,512]{1,0:T(8,128)(2,1)}, u32[]{:S(2)}) copy-start(bf16[128,512]{1,0:T(8,128)(2,1)} %get-tuple-element.8) | copy-start | bytes 393220
  102.8 18.5 %copy-start.1 = (f32[128,512]{1,0:T(8,128)S(1)}, f32[128,512]{1,0:T(8,128)}, u32[]{:S(2)}) copy-start(f32[128,512]{1,0:T(8,128)} %get-tuple-element.7) | copy-start | bytes 786436
  102.8 18.5 %copy-start.3 = (f32[512]{0:T(512)S(1)}, f32[512]{0:T(512)}, u32[]{:S(2)}) copy-start(f32[512]{0:T(512)} %param.11) | copy-start | bytes 6148

commit v23 on v20

--- a/solution.py
+++ b/solution.py
@@ -175,10 +175,11 @@
         return jnp.concatenate([proj_rows(tok_buf), proj_rows(prior_buf)], axis=0)
 
     copies = [[] for _ in range(n_ring)]
+    order = [h * (n_ring // 2) + k for k in range(n_ring // 2) for h in range(2)]
     for s in range(n - 1):
         arrive((n - 1 - s) % n)
         arrive((1 + s) % n)
-        for ring in range(n_ring):
+        for ring in order:
             fwd = ring < n_ring // 2
             d, dest = (1, nxt) if fwd else (-1, prv)
             cols = pl.ds(ring * chunk, chunk)

time: 112 us -> 109 us (0.973)
  the two profiles are of different devices: /device:TPU:22 before, /device:TPU:1 now
where the time goes in v23:
time: 109 us; the launch traced here: 107 us
  Pallas kernels  96.7 us (89%)
  local copies, waits for them, and re-layouts  4.66 us (4%)
  matrix products  4.41 us (4%)
  other arithmetic  1.5 us (1%)
    pallas_call x1, Pallas kernels, project_and_gate(): pl.pallas_call(rs_kernel, out_shape=(jax.ShapeDtypeStruct((rows, third),...  86.3 us
    pallas_call x1, Pallas kernels, gather_earlier(): pl.pallas_call(functools.partial(state_kernel, block_len=float(block_len)...  10.4 us

profile of v23, /device:TPU:1, one launch (start us, length us, event | category | flops | bytes accessed | tf_op | source)
XLA Modules:
  0.0 107.4 jit_solution(9198782991549075489)
XLA Ops:
  0.0 86.3 %shard_map.64 = (f32[128,512]{1,0:T(8,128)}, bf16[128,512]{1,0:T(8,128)(2,1)}) custom-call(bf16[128,1024]{1,0:T(8,128)(2,1)} %src_hbm.1, bf16[3,512,512]{2,1,0:T(8,128)(2,1)} %bitcast.17, f32[3,3,512]{2,1,0:T(4,128)} %taps_hbm.1), custom_call_target="tpu_custom_call" | custom-call | tf_op jit(solution)/shard_map/pallas_call | solution.py:253
  86.3 1.0 copy.17
  87.3 0.8 copy.20
  88.1 0.7 sqrt_multiply_fusion
  88.8 0.1 copy.19
  88.9 0.1 copy.18
  89.0 2.0 %fusion.11 = f32[32,128,128]{2,1,0:T(8,128)S(1)} fusion(f32[32,16]{1,0:T(8,128)S(1)} %copy.20, f32[32,16]{1,0:T(8,128)S(1)} %copy.19, f32[32,16]{1,0:T(8,128)S(1)} %copy.18), kind=kOutput, calls=%fused_computation.18 | convolution fusion | flops 50528256 | bytes 2103296 | tf_op jit(solution)/shard_map/gtr,gsr->gts/dot_general | solution.py:467
  91.1 0.6 fusion.2
  91.7 0.0 copy-start.2
  91.7 0.7 fusion.1
  92.4 0.0 copy-start
  92.4 0.0 copy-start.1
  92.4 0.0 copy-start.3
  92.4 0.3 fusion.19
  92.7 0.3 convolution_add_fusion.1
  93.0 0.2 copy.21
  93.1 0.7 copy.22.src_ref
  93.8 0.0 copy-done.2
  93.9 0.7 copy.23.lam_ref
  94.5 10.4 %shard_map.65 = f32[32,256]{1,0:T(8,128)} custom-call(f32[32,256]{1,0:T(8,128)} %copy.22.src_ref, f32[32,256]{1,0:T(8,128)} %copy.23.lam_ref), custom_call_target="tpu_custom_call" | custom-call | tf_op jit(solution)/shard_map/pallas_call | solution.py:433
  104.9 0.9 copy.24
  105.8 0.2 copy.25
  106.0 0.5 convolution_add_fusion
  106.5 0.1 copy.26
  106.6 0.0 copy-done
  106.6 0.0 copy-done.1
  106.7 0.0 copy-done.3
  106.7 0.7 multiply_convert_fusion
  (4 shorter events, 0.1 us)
Async XLA Ops:
  91.7 2.1 %copy-start.2 = (f32[32,16]{0,1:T(8,128)S(1)}, f32[32,16]{0,1:T(8,128)}, u32[]{:S(2)}) copy-start(f32[32,16]{0,1:T(8,128)} %param.9) | copy-start | bytes 6148
  92.4 14.3 %copy-start = (bf16[128,512]{1,0:T(8,128)(2,1)S(1)}, bf16[128,512]{1,0:T(8,128)(2,1)}, u32[]{:S(2)}) copy-start(bf16[128,512]{1,0:T(8,128)(2,1)} %get-tuple-element.8) | copy-start | bytes 393220
  92.4 14.3 %copy-start.1 = (f32[128,512]{1,0:T(8,128)S(1)}, f32[128,512]{1,0:T(8,128)}, u32[]{:S(2)}) copy-start(f32[128,512]{1,0:T(8,128)} %get-tuple-element.7) | copy-start | bytes 786436
  92.4 14.3 %copy-start.3 = (f32[512]{0:T(512)S(1)}, f32[512]{0:T(512)}, u32[]{:S(2)}) copy-start(f32[512]{0:T(512)} %param.11) | copy-start | bytes 6148

commit v24 on v23

--- a/solution.py
+++ b/solution.py
@@ -177,10 +177,9 @@
     copies = [[] for _ in range(n_ring)]
     order = [h * (n_ring // 2) + k for k in range(n_ring // 2) for h in range(2)]
     for s in range(n - 1):
-        arrive((n - 1 - s) % n)
-        arrive((1 + s) % n)
         for ring in order:
             fwd = ring < n_ring // 2
+            arrive((n - 1 - s) % n if fwd else (1 + s) % n)
             d, dest = (1, nxt) if fwd else (-1, prv)
             cols = pl.ds(ring * chunk, chunk)
             q = lookup(cyc, (r - d * (1 + s) + 2 * n) % n)

time: 109 us -> 109 us (level)
  no operation moved by 1% of the time
where the time goes in v24:
time: 109 us; the launch traced here: 107 us
  Pallas kernels  96.7 us (89%)
  local copies, waits for them, and re-layouts  4.66 us (4%)
  matrix products  4.41 us (4%)
  other arithmetic  1.5 us (1%)
    pallas_call x1, Pallas kernels, project_and_gate(): pl.pallas_call(rs_kernel, out_shape=(jax.ShapeDtypeStruct((rows, third),...  86.3 us
    pallas_call x1, Pallas kernels, gather_earlier(): pl.pallas_call(functools.partial(state_kernel, block_len=float(block_len)...  10.4 us

profile of v24, /device:TPU:1, one launch (start us, length us, event | category | flops | bytes accessed | tf_op | source)
XLA Modules:
  0.0 107.4 jit_solution(2568400185632371667)
XLA Ops:
  0.0 86.3 %shard_map.64 = (f32[128,512]{1,0:T(8,128)}, bf16[128,512]{1,0:T(8,128)(2,1)}) custom-call(bf16[128,1024]{1,0:T(8,128)(2,1)} %src_hbm.1, bf16[3,512,512]{2,1,0:T(8,128)(2,1)} %bitcast.17, f32[3,3,512]{2,1,0:T(4,128)} %taps_hbm.1), custom_call_target="tpu_custom_call" | custom-call | tf_op jit(solution)/shard_map/pallas_call | solution.py:252
  86.3 1.0 copy.17
  87.3 0.8 copy.20
  88.1 0.7 sqrt_multiply_fusion
  88.8 0.1 copy.19
  88.9 0.1 copy.18
  89.0 2.0 %fusion.11 = f32[32,128,128]{2,1,0:T(8,128)S(1)} fusion(f32[32,16]{1,0:T(8,128)S(1)} %copy.20, f32[32,16]{1,0:T(8,128)S(1)} %copy.19, f32[32,16]{1,0:T(8,128)S(1)} %copy.18), kind=kOutput, calls=%fused_computation.18 | convolution fusion | flops 50528256 | bytes 2103296 | tf_op jit(solution)/shard_map/gtr,gsr->gts/dot_general | solution.py:466
  91.1 0.6 fusion.2
  91.7 0.0 copy-start.2
  91.7 0.7 fusion.1
  92.4 0.0 copy-start
  92.4 0.0 copy-start.1
  92.4 0.0 copy-start.3
  92.4 0.3 fusion.19
  92.7 0.3 convolution_add_fusion.1
  93.0 0.2 copy.21
  93.2 0.7 copy.22.src_ref
  93.8 0.0 copy-done.2
  93.9 0.7 copy.23.lam_ref
  94.5 10.4 %shard_map.65 = f32[32,256]{1,0:T(8,128)} custom-call(f32[32,256]{1,0:T(8,128)} %copy.22.src_ref, f32[32,256]{1,0:T(8,128)} %copy.23.lam_ref), custom_call_target="tpu_custom_call" | custom-call | tf_op jit(solution)/shard_map/pallas_call | solution.py:432
  104.9 0.9 copy.24
  105.8 0.2 copy.25
  106.0 0.5 convolution_add_fusion
  106.5 0.1 copy.26
  106.7 0.0 copy-done
  106.7 0.0 copy-done.1
  106.7 0.0 copy-done.3
  106.7 0.7 multiply_convert_fusion
  (4 shorter events, 0.1 us)
Async XLA Ops:
  91.7 2.1 %copy-start.2 = (f32[32,16]{0,1:T(8,128)S(1)}, f32[32,16]{0,1:T(8,128)}, u32[]{:S(2)}) copy-start(f32[32,16]{0,1:T(8,128)} %param.9) | copy-start | bytes 6148
  92.4 14.3 %copy-start = (bf16[128,512]{1,0:T(8,128)(2,1)S(1)}, bf16[128,512]{1,0:T(8,128)(2,1)}, u32[]{:S(2)}) copy-start(bf16[128,512]{1,0:T(8,128)(2,1)} %get-tuple-element.8) | copy-start | bytes 393220
  92.4 14.3 %copy-start.1 = (f32[128,512]{1,0:T(8,128)S(1)}, f32[128,512]{1,0:T(8,128)}, u32[]{:S(2)}) copy-start(f32[128,512]{1,0:T(8,128)} %get-tuple-element.7) | copy-start | bytes 786436
  92.4 14.3 %copy-start.3 = (f32[512]{0:T(512)S(1)}, f32[512]{0:T(512)}, u32[]{:S(2)}) copy-start(f32[512]{0:T(512)} %param.11) | copy-start | bytes 6148
